TPU v7x, 32 devices: a whole 2x2x4 slice. The times are simulated.
32 devices in a mesh: batch: 8 (over z, y), head: 4 (over x, core).
Axes of the slice: x: 2, y: 2, z: 4, core: 2. Of those that a mesh axis runs over, the one named last changes fastest.
Arguments:
- tokens: bfloat16 [20480, 768], P(('batch', 'head')), may hold values from -6 to 6
- pass_ids: int32 [20480], P(('batch', 'head')), may hold values from 0 to 4
- segment_ids: int32 [16, 1280], P('batch'), may hold values from 0 to 3, never falling along the last dimension, each value on 1 to 640 neighbouring positions
- pass_embed: bfloat16 [5, 768], replicated, may hold values from -3 to 3
- norm1_gain: bfloat16 [768], replicated, may hold values from 0.5 to 1.5
- norm1_shift: bfloat16 [768], replicated, may hold values from -1 to 1
- qkv_weight: bfloat16 [768, 2304], replicated, may hold values from -0.21875 to 0.21875
- qv_bias: bfloat16 [2, 768], replicated, may hold values from -1 to 1
- out_weight: bfloat16 [768, 768], replicated, may hold values from -0.625 to 0.625
- out_bias: bfloat16 [768], replicated, may hold values from -1 to 1
- norm2_gain: bfloat16 [768], replicated, may hold values from 0.5 to 1.5
- norm2_shift: bfloat16 [768], replicated, may hold values from -1 to 1
- up_weight: bfloat16 [768, 3072], replicated, may hold values from -0.21875 to 0.21875
- up_bias: bfloat16 [3072], replicated, may hold values from -1 to 1
- down_weight: bfloat16 [3072, 768], replicated, may hold values from -0.109375 to 0.109375
- down_bias: bfloat16 [768], replicated, may hold values from -1 to 1
- cotangent: bfloat16 [20480, 768], P(('batch', 'head')), may hold values from -6 to 6
Outputs:
- mixed: bfloat16 [20480, 768], P(('batch', 'head'))
- input_grad: float32 [20480, 768], P(('batch', 'head'))
- pass_embed_grad: float32 [5, 768], P(None, ('batch', 'head'))
- norm1_gain_grad: float32 [768], P(('batch', 'head'))
- norm1_shift_grad: float32 [768], P(('batch', 'head'))
- qkv_weight_grad: float32 [768, 2304], P(None, ('batch', 'head'))
- qv_bias_grad: float32 [2, 768], P(None, ('batch', 'head'))
- out_weight_grad: float32 [768, 768], P(None, ('batch', 'head'))
- out_bias_grad: float32 [768], P(('batch', 'head'))
- norm2_gain_grad: float32 [768], P(('batch', 'head'))
- norm2_shift_grad: float32 [768], P(('batch', 'head'))
- up_weight_grad: float32 [768, 3072], P(None, ('batch', 'head'))
- up_bias_grad: float32 [3072], P(('batch', 'head'))
- down_weight_grad: float32 [3072, 768], P(None, ('batch', 'head'))
- down_bias_grad: float32 [768], P(('batch', 'head'))
Inputs may be any that keep to these rules, and one draw needn't show every extreme that they name: `segment_ids`: along a sequence the ids never fall; a segment holds at most 640 tokens and one holds exactly that many.
All inputs are finite; a program needn't handle non-finite values.
Results may differ from a plain program's by a relative error of at most 0.0095.
Values may be sent and summed in bfloat16 or wider, within the bound.
No kernel may reach another device: no remote copies, remote signals or barrier semaphores. Data moves between devices by JAX's collectives and lax.ppermute only.
A program may use at most 192 MiB of HBM per device.

v0:
```python
import jax
import jax.numpy as jnp
from jax import lax
from jax.sharding import PartitionSpec as P

HEAD_DIM = 64
SEQ_LEN = 1280


def layer_norm(values, gain, shift):
    center = values - jnp.mean(values, -1, keepdims=True)
    spread = jnp.mean(center * center, -1, keepdims=True)
    return center * lax.rsqrt(spread + 1e-05) * gain + shift


def masked_scores(q_rows, k_rows, seg_row):
    scores = jnp.einsum("qhd,khd->hqk", q_rows, k_rows, preferred_element_type=jnp.float32) * 0.125
    places = jnp.arange(q_rows.shape[0])
    allowed = (places[:, None] >= places[None, :]) & (seg_row[:, None] == seg_row[None, :])
    return jnp.where(allowed[None], scores, -1e30)


def attend_forward(inputs):
    q_rows, k_rows, v_rows, seg_row = inputs
    scores = masked_scores(q_rows, k_rows, seg_row)
    row_max = jnp.max(scores, -1, keepdims=True)
    raw_weights = jnp.exp(scores - row_max)
    row_sum = jnp.sum(raw_weights, -1, keepdims=True)
    probability = raw_weights / row_sum
    attended = jnp.einsum(
        "hqk,khd->qhd", probability.astype(jnp.bfloat16), v_rows, preferred_element_type=jnp.float32
    )
    return (attended.astype(jnp.bfloat16), (row_max + jnp.log(row_sum))[..., 0])


def attend_backward(inputs):
    q_rows, k_rows, v_rows, seg_row, log_sums, grad_rows = inputs
    scores = masked_scores(q_rows, k_rows, seg_row)
    probability = jnp.exp(scores - log_sums[..., None])
    grad_probs = jnp.einsum("qhd,khd->hqk", grad_rows, v_rows, preferred_element_type=jnp.float32)
    center = jnp.sum(probability * grad_probs, -1, keepdims=True)
    grad_scores = (probability * (grad_probs - center)).astype(jnp.bfloat16)
    grad_values = jnp.einsum(
        "hqk,qhd->khd",
        probability.astype(jnp.bfloat16),
        grad_rows,
        preferred_element_type=jnp.float32,
    )
    grad_queries = (
        jnp.einsum("hqk,khd->qhd", grad_scores, k_rows, preferred_element_type=jnp.float32) * 0.125
    )
    grad_keys = (
        jnp.einsum("hqk,qhd->khd", grad_scores, q_rows, preferred_element_type=jnp.float32) * 0.125
    )
    return (
        grad_queries.astype(jnp.bfloat16),
        grad_keys.astype(jnp.bfloat16),
        grad_values.astype(jnp.bfloat16),
    )


def on_device(
    tokens,
    pass_ids,
    segment_ids,
    pass_embed,
    norm1_gain,
    norm1_shift,
    qkv_weight,
    qv_bias,
    out_weight,
    out_bias,
    norm2_gain,
    norm2_shift,
    up_weight,
    up_bias,
    down_weight,
    down_bias,
    cotangent,
):
    rows_dev = tokens.shape[0]
    width = tokens.shape[1]
    groups = lax.axis_size("head")
    local = width // groups
    head_count = local // HEAD_DIM
    group_rows = rows_dev * groups
    seq_count = group_rows // SEQ_LEN
    gain_one = norm1_gain.astype(jnp.float32)
    shift_one = norm1_shift.astype(jnp.float32)
    gain_two = norm2_gain.astype(jnp.float32)
    shift_two = norm2_shift.astype(jnp.float32)
    one_hot = (pass_ids[:, None] == jnp.arange(pass_embed.shape[0])[None, :]).astype(jnp.float32)
    table = pass_embed.astype(jnp.float32)
    hidden = tokens.astype(jnp.float32) + jnp.dot(
        one_hot, table, precision=lax.Precision.HIGHEST, preferred_element_type=jnp.float32
    )
    normed = layer_norm(hidden, gain_one, shift_one).astype(jnp.bfloat16)
    bias_full = jnp.concatenate(
        [
            qv_bias[0].astype(jnp.float32),
            jnp.zeros((width,), jnp.float32),
            qv_bias[1].astype(jnp.float32),
        ]
    )
    joined = (jnp.dot(normed, qkv_weight, preferred_element_type=jnp.float32) + bias_full).astype(
        jnp.bfloat16
    )
    grouped = joined.reshape(rows_dev, 3, groups, local)
    arrived = lax.all_to_all(grouped, "head", split_axis=2, concat_axis=0, tiled=True).reshape(
        group_rows, 3 * local
    )
    q_heads = arrived[:, :local].reshape(seq_count, SEQ_LEN, head_count, HEAD_DIM)
    k_heads = arrived[:, local : 2 * local].reshape(seq_count, SEQ_LEN, head_count, HEAD_DIM)
    v_heads = arrived[:, 2 * local :].reshape(seq_count, SEQ_LEN, head_count, HEAD_DIM)
    outputs, log_sums = lax.map(attend_forward, (q_heads, k_heads, v_heads, segment_ids))
    attended = outputs.reshape(group_rows, local)
    mixed_heads = lax.all_to_all(attended, "head", split_axis=0, concat_axis=1, tiled=True)
    after_attn = (
        hidden
        + jnp.dot(mixed_heads, out_weight, preferred_element_type=jnp.float32)
        + out_bias.astype(jnp.float32)
    )
    normed_two = layer_norm(after_attn, gain_two, shift_two).astype(jnp.bfloat16)
    pre_act = jnp.dot(normed_two, up_weight, preferred_element_type=jnp.float32) + up_bias.astype(
        jnp.float32
    )
    activated = jax.nn.gelu(pre_act, approximate=True).astype(jnp.bfloat16)
    result = (
        after_attn
        + jnp.dot(activated, down_weight, preferred_element_type=jnp.float32)
        + down_bias.astype(jnp.float32)
    ).astype(jnp.bfloat16)
    grad_out = cotangent.astype(jnp.float32)
    down_grad = jnp.einsum("nf,nd->fd", activated, cotangent, preferred_element_type=jnp.float32)
    down_bias_grad = jnp.sum(grad_out, 0)
    grad_act = jnp.einsum("nd,fd->nf", cotangent, down_weight, preferred_element_type=jnp.float32)
    gelu_value, gelu_pull = jax.vjp(lambda inner: jax.nn.gelu(inner, approximate=True), pre_act)
    grad_pre = gelu_pull(grad_act)[0].astype(jnp.bfloat16)
    up_grad = jnp.einsum("nd,nf->df", normed_two, grad_pre, preferred_element_type=jnp.float32)
    up_bias_grad = jnp.sum(grad_pre.astype(jnp.float32), 0)
    grad_normed_two = jnp.einsum(
        "nf,df->nd", grad_pre, up_weight, preferred_element_type=jnp.float32
    )
    norm_two_value, norm_two_pull = jax.vjp(layer_norm, after_attn, gain_two, shift_two)
    grad_resid, gain_two_grad, shift_two_grad = norm_two_pull(grad_normed_two)
    grad_after = grad_out + grad_resid
    grad_branch = grad_after.astype(jnp.bfloat16)
    out_grad = jnp.einsum("nd,ne->de", mixed_heads, grad_branch, preferred_element_type=jnp.float32)
    out_bias_grad = jnp.sum(grad_branch.astype(jnp.float32), 0)
    grad_mixed = jnp.einsum(
        "ne,de->nd", grad_branch, out_weight, preferred_element_type=jnp.float32
    ).astype(jnp.bfloat16)
    grad_attended = lax.all_to_all(
        grad_mixed, "head", split_axis=1, concat_axis=0, tiled=True
    ).reshape(seq_count, SEQ_LEN, head_count, HEAD_DIM)
    grad_queries, grad_keys, grad_values = lax.map(
        attend_backward, (q_heads, k_heads, v_heads, segment_ids, log_sums, grad_attended)
    )
    grad_stack = jnp.stack(
        [
            grad_queries.reshape(group_rows, local),
            grad_keys.reshape(group_rows, local),
            grad_values.reshape(group_rows, local),
        ],
        1,
    )
    returned = lax.all_to_all(
        grad_stack.reshape(group_rows, 3, 1, local), "head", split_axis=0, concat_axis=2, tiled=True
    )
    grad_joined = returned.reshape(rows_dev, 3 * width)
    qkv_grad = jnp.einsum("nd,ne->de", normed, grad_joined, preferred_element_type=jnp.float32)
    bias_grad_full = jnp.sum(grad_joined.astype(jnp.float32), 0)
    grad_normed = jnp.einsum(
        "ne,de->nd", grad_joined, qkv_weight, preferred_element_type=jnp.float32
    )
    qv_grad = jnp.stack([bias_grad_full[:width], bias_grad_full[2 * width :]])
    norm_one_value, norm_one_pull = jax.vjp(layer_norm, hidden, gain_one, shift_one)
    grad_hidden_part, gain_one_grad, shift_one_grad = norm_one_pull(grad_normed)
    grad_hidden = grad_after + grad_hidden_part
    table_grad = jnp.einsum(
        "nr,nd->rd",
        one_hot,
        grad_hidden,
        precision=lax.Precision.HIGHEST,
        preferred_element_type=jnp.float32,
    )
    summed = (
        lax.psum_scatter(table_grad, ("batch", "head"), scatter_dimension=1, tiled=True),
        lax.psum_scatter(gain_one_grad, ("batch", "head"), scatter_dimension=0, tiled=True),
        lax.psum_scatter(shift_one_grad, ("batch", "head"), scatter_dimension=0, tiled=True),
        lax.psum_scatter(qkv_grad, ("batch", "head"), scatter_dimension=1, tiled=True),
        lax.psum_scatter(qv_grad, ("batch", "head"), scatter_dimension=1, tiled=True),
        lax.psum_scatter(out_grad, ("batch", "head"), scatter_dimension=1, tiled=True),
        lax.psum_scatter(out_bias_grad, ("batch", "head"), scatter_dimension=0, tiled=True),
        lax.psum_scatter(gain_two_grad, ("batch", "head"), scatter_dimension=0, tiled=True),
        lax.psum_scatter(shift_two_grad, ("batch", "head"), scatter_dimension=0, tiled=True),
        lax.psum_scatter(up_grad, ("batch", "head"), scatter_dimension=1, tiled=True),
        lax.psum_scatter(up_bias_grad, ("batch", "head"), scatter_dimension=0, tiled=True),
        lax.psum_scatter(down_grad, ("batch", "head"), scatter_dimension=1, tiled=True),
        lax.psum_scatter(down_bias_grad, ("batch", "head"), scatter_dimension=0, tiled=True),
    )
    return (
        result,
        grad_hidden,
        summed[0],
        summed[1],
        summed[2],
        summed[3],
        summed[4],
        summed[5],
        summed[6],
        summed[7],
        summed[8],
        summed[9],
        summed[10],
        summed[11],
        summed[12],
    )


def solution(mesh):
    in_specs = (
        P(("batch", "head"), None),
        P(("batch", "head")),
        P("batch", None),
        P(),
        P(),
        P(),
        P(),
        P(),
        P(),
        P(),
        P(),
        P(),
        P(),
        P(),
        P(),
        P(),
        P(("batch", "head"), None),
    )
    out_specs = (
        P(("batch", "head"), None),
        P(("batch", "head"), None),
        P(None, ("batch", "head")),
        P(("batch", "head")),
        P(("batch", "head")),
        P(None, ("batch", "head")),
        P(None, ("batch", "head")),
        P(None, ("batch", "head")),
        P(("batch", "head")),
        P(("batch", "head")),
        P(("batch", "head")),
        P(None, ("batch", "head")),
        P(("batch", "head")),
        P(None, ("batch", "head")),
        P(("batch", "head")),
    )
    return jax.shard_map(
        on_device, mesh=mesh, in_specs=in_specs, out_specs=out_specs, check_vma=False
    )
```

profile of v0, /device:TPU:0, one launch (start us, length us, event | category | flops | bytes accessed | tf_op | source)
XLA Modules:
  0.0 904.8 jit_solution(17227066216637011802)
XLA Ops:
  13.3 4.2 add_convert_fusion
  17.5 5.5 copy.131
  23.0 3.7 copy.132
  26.7 4.8 all-to-all-start
  31.6 35.5 %all-to-all-done = bf16[640,3,4,192]{0,3,1,2:T(8,128)(2,1)} async-done(((bf16[640,3,4,192]{0,3,1,2:T(8,128)(2,1)}), bf16[640,3,4,192]{0,3,1,2:T(8,128)(2,1)}, u32[]{:S(2)}, u32[]{:S(2)}) %all-to-all-start) | async-done | bytes 2949152 | tf_op jit(solution)/shard_map/all_to_all | solution.py:109
  67.1 4.1 copy.133
  91.1 71.0 %while.26 = (s32[]{:T(128)}, bf16[2,1280,3,64]{1,3,2,0:T(8,128)(2,1)}, f32[2,3,1280]{2,1,0:T(4,128)}, bf16[2,1280,3,64]{1,3,2,0:T(8,128)(2,1)}, s32[2,1280]{1,0:...) while((s32[]{:T(128)}, ...), condition=%wide.region_5.6_spmd, body=%wide.region_2.5_spmd.sunk | while | flops 1302769920 | bytes 64760020 | solution.py:115
  93.2 12.2 %fusion.116 = (f32[3,1280]{1,0:T(4,128)}, f32[3,1280,1280]{1,2,0:T(8,128)}) fusion(bf16[2,1280,3,64]{1,3,2,0:T(8,128)(2,1)} %get-tuple-element.407, s32[]{:T(128)S(6)} %copy.171, bf16[2,1280,3,64]{1,3,2,0:T(8,128)(2,1)} %get-tuple-element.406, pred[1280,1280]{0,1:T(8,128)(4,1)S(1)} %fusion.115), kind=kOutput, calls=%fused_computation.122.clone.1 | convolution fusion | flops 643887360 | bytes 22298624 | tf_op jit(solution)/shard_map/while/body/eval_jaxpr/qhd,khd->hqk/dot_general | solution.py:17
  105.4 9.8 %fusion.117 = f32[3,1280]{1,0:T(4,128)} fusion(f32[3,1280,1280]{1,2,0:T(8,128)} %get-tuple-element.371, f32[3,1280]{1,0:T(4,128)} %get-tuple-element.372), kind=kLoop, calls=%fused_computation.4.clone.1 | loop fusion | flops 9826560 | bytes 19691520 | tf_op jit(solution)/shard_map/while/body/eval_jaxpr/reduce_sum | solution.py:28
  115.2 10.9 %fusion.118 = bf16[2,1280,3,64]{1,3,2,0:T(8,128)(2,1)} fusion(bf16[2,1280,3,64]{1,3,2,0:T(8,128)(2,1)} %get-tuple-element.394, s32[]{:T(128)S(6)} %copy.171, f32[3,1280,1280]{1,2,0:T(8,128)} %get-tuple-element.371, f32[3,1280]{1,0:T(4,128)} %fusion.117, f32[3,1280]{1,0:T(4,128)} %get-tuple-element.372, bf16[2,1280,3,64]{1,3,2,0:T(8,128)(2,1)} %get-tuple-element.404), kind=kOutput, calls=%fused_computation.10.clone.1 | convolution fusion | flops 644136960 | bytes 20685824 | tf_op jit(solution)/shard_map/while/body/eval_jaxpr/hqk,khd->qhd/dot_general | solution.py:30
  128.6 12.2 %fusion.116 = (f32[3,1280]{1,0:T(4,128)}, f32[3,1280,1280]{1,2,0:T(8,128)}) fusion(bf16[2,1280,3,64]{1,3,2,0:T(8,128)(2,1)} %get-tuple-element.407, s32[]{:T(128)S(6)} %copy.171, bf16[2,1280,3,64]{1,3,2,0:T(8,128)(2,1)} %get-tuple-element.406, pred[1280,1280]{0,1:T(8,128)(4,1)S(1)} %fusion.115), kind=kOutput, calls=%fused_computation.122.clone.1 | convolution fusion | flops 643887360 | bytes 22298624 | tf_op jit(solution)/shard_map/while/body/eval_jaxpr/qhd,khd->hqk/dot_general | solution.py:17
  140.8 9.8 %fusion.117 = f32[3,1280]{1,0:T(4,128)} fusion(f32[3,1280,1280]{1,2,0:T(8,128)} %get-tuple-element.371, f32[3,1280]{1,0:T(4,128)} %get-tuple-element.372), kind=kLoop, calls=%fused_computation.4.clone.1 | loop fusion | flops 9826560 | bytes 19691520 | tf_op jit(solution)/shard_map/while/body/eval_jaxpr/reduce_sum | solution.py:28
  150.6 10.9 %fusion.118 = bf16[2,1280,3,64]{1,3,2,0:T(8,128)(2,1)} fusion(bf16[2,1280,3,64]{1,3,2,0:T(8,128)(2,1)} %get-tuple-element.394, s32[]{:T(128)S(6)} %copy.171, f32[3,1280,1280]{1,2,0:T(8,128)} %get-tuple-element.371, f32[3,1280]{1,0:T(4,128)} %fusion.117, f32[3,1280]{1,0:T(4,128)} %get-tuple-element.372, bf16[2,1280,3,64]{1,3,2,0:T(8,128)(2,1)} %get-tuple-element.404), kind=kOutput, calls=%fused_computation.10.clone.1 | convolution fusion | flops 644136960 | bytes 20685824 | tf_op jit(solution)/shard_map/while/body/eval_jaxpr/hqk,khd->qhd/dot_general | solution.py:30
  165.2 14.6 %all_to_all.51 = bf16[4,640,192]{1,0,2:T(4,128)(2,1)} reshape(bf16[2,1280,3,64]{1,0,3,2:T(2,128)(2,1)} %copy.137) | data formatting | bytes 1966080 | tf_op jit(solution)/shard_map/all_to_all | solution.py:117
  182.1 4.2 all-to-all-start.1
  190.9 9.3 %all-to-all-done.1 = bf16[4,640,192]{1,2,0:T(8,128)(2,1)} async-done(((bf16[4,640,192]{1,2,0:T(8,128)(2,1)}), bf16[4,640,192]{1,2,0:T(8,128)(2,1)}, u32[]{:S(2)}, u32[]{:S(2)}) %all-to-all-start.1) | async-done | bytes 983072 | tf_op jit(solution)/shard_map/all_to_all | solution.py:117
  200.2 3.4 fusion.73
  204.0 6.3 fusion.63
  210.4 8.6 convert_reduce_fusion
  219.0 4.1 multiply_reduce_fusion.1
  231.3 4.2 all-to-all-start.2
  235.6 4.0 fusion.74
  239.7 9.7 %all-to-all-done.2 = bf16[640,4,192]{0,2,1:T(8,128)(2,1)} async-done(((bf16[640,4,192]{0,2,1:T(8,128)(2,1)}), bf16[640,4,192]{0,2,1:T(8,128)(2,1)}, u32[]{:S(2)}, u32[]{:S(2)}) %all-to-all-start.2) | async-done | bytes 983072 | tf_op jit(solution)/shard_map/all_to_all | solution.py:153
  261.0 114.7 %while.27 = (s32[]{:T(128)}, bf16[2,1280,3,64]{1,3,2,0:T(8,128)(2,1)}, bf16[2,1280,3,64]{1,3,2,0:T(8,128)(2,1)}, bf16[2,1280,3,64]{1,3,2,0:T(8,128)(2,1)}, bf16[...) while((s32[]{:T(128)}, ...), condition=%wide.region_12.13_spmd, body=%wide.region_10.12_spmd.sunk | while | flops 3196104960 | bytes 195067312 | solution.py:156
  264.0 11.9 %fusion.127 = f32[3,1280,1280]{1,2,0:T(8,128)} fusion(f32[3,1280]{1,0:T(4,128)S(1)} %dynamic-slice_bitcast_fusion.2, pred[1280,1280]{0,1:T(8,128)(4,1)S(1)} %fusion.126, bf16[2,1280,3,64]{1,3,2,0:T(8,128)(2,1)} %get-tuple-element.437, s32[]{:T(128)S(6)} %copy.181, bf16[2,1280,3,64]{1,3,2,0:T(8,128)(2,1)} %get-tuple-element.435), kind=kOutput, calls=%fused_computation.23.clone.1 | convolution fusion | flops 643891200 | bytes 22298624 | tf_op jit(solution)/shard_map/while/body/eval_jaxpr/qhd,khd->hqk/dot_general | solution.py:17
  275.9 10.1 %fusion.130 = bf16[2,1280,3,64]{1,3,2,0:T(8,128)(2,1)S(1)} fusion(bf16[2,1280,3,64]{1,3,2,0:T(8,128)(2,1)S(1)} %copy-done.13, s32[]{:T(128)S(6)} %copy.181, f32[3,1280,1280]{1,2,0:T(8,128)} %fusion.127, bf16[2,1280,3,64]{1,3,2,0:T(8,128)(2,1)S(1)} %copy-done.1), kind=kOutput, calls=%fused_computation.36.clone.1 | convolution fusion | flops 634306560 | bytes 20644864 | tf_op jit(solution)/shard_map/while/body/eval_jaxpr/hqk,qhd->khd/dot_general | solution.py:43
  286.0 12.7 %multiply_reduce_fusion.8 = (f32[3,1280]{1,0:T(4,128)S(1)}, f32[3,1280,1280]{1,2,0:T(8,128)}) fusion(f32[3,1280,1280]{1,2,0:T(8,128)} %fusion.127, bf16[2,1280,3,64]{1,3,2,0:T(8,128)(2,1)S(1)} %copy-done.10, s32[]{:T(128)S(6)} %copy.181, bf16[2,1280,3,64]{1,3,2,0:T(8,128)(2,1)S(1)} %copy-done.1), kind=kOutput, calls=%fused_computation.25.clone.1 | convolution fusion | flops 638972160 | bytes 40321024 | tf_op jit(solution)/shard_map/while/body/eval_jaxpr/qhd,khd->hqk/dot_general | solution.py:40
  298.7 14.1 %multiply_convert_fusion.5 = bf16[3,1280,1280]{1,2,0:T(8,128)(2,1)S(1)} fusion(f32[3,1280,1280]{1,2,0:T(8,128)} %get-tuple-element.383, f32[3,1280,1280]{1,2,0:T(8,128)} %fusion.127, f32[3,1280]{1,0:T(4,128)S(1)} %get-tuple-element.384), kind=kLoop, calls=%fused_computation.24.clone.1 | loop fusion | flops 14745600 | bytes 49167360 | tf_op jit(solution)/shard_map/while/body/eval_jaxpr/convert_element_type | solution.py:42
  321.3 11.8 %fusion.127 = f32[3,1280,1280]{1,2,0:T(8,128)} fusion(f32[3,1280]{1,0:T(4,128)S(1)} %dynamic-slice_bitcast_fusion.2, pred[1280,1280]{0,1:T(8,128)(4,1)S(1)} %fusion.126, bf16[2,1280,3,64]{1,3,2,0:T(8,128)(2,1)} %get-tuple-element.437, s32[]{:T(128)S(6)} %copy.181, bf16[2,1280,3,64]{1,3,2,0:T(8,128)(2,1)} %get-tuple-element.435), kind=kOutput, calls=%fused_computation.23.clone.1 | convolution fusion | flops 643891200 | bytes 22298624 | tf_op jit(solution)/shard_map/while/body/eval_jaxpr/qhd,khd->hqk/dot_general | solution.py:17
  333.1 9.9 %fusion.130 = bf16[2,1280,3,64]{1,3,2,0:T(8,128)(2,1)S(1)} fusion(bf16[2,1280,3,64]{1,3,2,0:T(8,128)(2,1)S(1)} %copy-done.13, s32[]{:T(128)S(6)} %copy.181, f32[3,1280,1280]{1,2,0:T(8,128)} %fusion.127, bf16[2,1280,3,64]{1,3,2,0:T(8,128)(2,1)S(1)} %copy-done.1), kind=kOutput, calls=%fused_computation.36.clone.1 | convolution fusion | flops 634306560 | bytes 20644864 | tf_op jit(solution)/shard_map/while/body/eval_jaxpr/hqk,qhd->khd/dot_general | solution.py:43
  343.1 12.6 %multiply_reduce_fusion.8 = (f32[3,1280]{1,0:T(4,128)S(1)}, f32[3,1280,1280]{1,2,0:T(8,128)}) fusion(f32[3,1280,1280]{1,2,0:T(8,128)} %fusion.127, bf16[2,1280,3,64]{1,3,2,0:T(8,128)(2,1)S(1)} %copy-done.10, s32[]{:T(128)S(6)} %copy.181, bf16[2,1280,3,64]{1,3,2,0:T(8,128)(2,1)S(1)} %copy-done.1), kind=kOutput, calls=%fused_computation.25.clone.1 | convolution fusion | flops 638972160 | bytes 40321024 | tf_op jit(solution)/shard_map/while/body/eval_jaxpr/qhd,khd->hqk/dot_general | solution.py:40
  355.7 13.8 %multiply_convert_fusion.5 = bf16[3,1280,1280]{1,2,0:T(8,128)(2,1)S(1)} fusion(f32[3,1280,1280]{1,2,0:T(8,128)} %get-tuple-element.383, f32[3,1280,1280]{1,2,0:T(8,128)} %fusion.127, f32[3,1280]{1,0:T(4,128)S(1)} %get-tuple-element.384), kind=kLoop, calls=%fused_computation.24.clone.1 | loop fusion | flops 14745600 | bytes 49167360 | tf_op jit(solution)/shard_map/while/body/eval_jaxpr/convert_element_type | solution.py:42
  378.8 3.5 stack_reshape.11
  385.5 3.5 stack_reshape.9
  392.2 3.5 stack_reshape.10
  395.7 3.7 maximum_bitcast_fusion
  399.4 8.4 copy.148
  407.8 65.5 %all_to_all.65 = bf16[2560,3,1,192]{3,1,2,0:T(4,128)(2,1)} all-to-all(bf16[2560,3,1,192]{3,1,2,0:T(4,128)(2,1)} %copy.148), channel_id=1, replica_groups=mesh['batch'=8,'head'=4] {'head'}, dimensions={0} | all-to-all | bytes 5898240 | tf_op jit(solution)/shard_map/all_to_all | solution.py:167
  473.3 9.0 copy.157
  486.3 5.3 fusion.61
  491.7 11.4 %fusion.64 = f32[3072,768]{0,1:T(8,128)} fusion(bf16[640,768]{1,0:T(8,128)(2,1)} %param.37, f32[640,3072]{1,0:T(8,128)} %copy-done.52, f32[3072]{0:T(1024)} %convert_element_type.121), kind=kOutput, calls=%fused_computation.119 | convolution fusion | flops 3039559680 | bytes 18296832 | tf_op jit(solution)/shard_map/nf,nd->fd/dot_general | solution.py:134
  503.8 10.6 %fusion.62 = f32[768,3072]{0,1:T(8,128)} fusion(bf16[640,3072]{1,0:T(8,128)(2,1)} %copy-done.53, f32[640,768]{1,0:T(8,128)} %copy-done.11, f32[768]{0:T(1024)} %convert_element_type.119, f32[768]{0:T(1024)S(1)} %copy-done.43, f32[640]{0:T(1024)} %copy-done.44, f32[640]{0:T(1024)S(1)} %copy-done.31), kind=kOutput, calls=%fused_computation.117 | convolution fusion | flops 3022356480 | bytes 15346688 | tf_op jit(solution)/shard_map/nd,nf->df/dot_general | solution.py:139
  515.1 11.6 %add_convert_fusion.1 = bf16[640,768]{1,0:T(8,128)(2,1)} fusion(f32[640,768]{1,0:T(8,128)} %copy-done.11, bf16[3072,768]{1,0:T(8,128)(2,1)} %param.35, f32[768]{0:T(1024)S(1)} %convert_element_type.123, f32[640,3072]{1,0:T(8,128)} %copy-done.52, f32[3072]{0:T(1024)} %convert_element_type.121), kind=kOutput, calls=%fused_computation.87 | convolution fusion | flops 3041034240 | bytes 15547392 | tf_op jit(solution)/shard_map/dot_general | solution.py:130
  532.8 6.7 multiply_reduce_fusion.2
  544.5 44.9 %all-reduce.9 = (f32[5,768]{1,0:T(8,128)}, f32[768]{0:T(1024)}, f32[768]{0:T(1024)}, f32[2,768]{1,0:T(2,128)}, f32[768]{0:T(1024)}, /*index=5*/f32[768]{0:T(1024)}, f32[768]{0:T(1024)}, f32[3072]{0:T(1024)}, f32[768]{0:T(1024)}) all-reduce(f32[5,768]{1,0:T(8,128)} %fusion.56, ...), channel_id=2, replica_groups=mesh['batch'=8,'head'=4] {'batch','head'}, use_global_device_ids=true, to_apply=%region_15.16.clone | all-reduce | flops 13056 | bytes 104448
  600.9 13.9 %reduce-scatter.7.cloned.1.call-done = f32[768,72]{0,1:T(8,128)} async-done(((f32[768,2304]{0,1:T(8,128)}), f32[768,72]{0,1:T(8,128)}) %reduce-scatter.7.cloned.1.call-update) | async-done | bytes 221200 | tf_op jit(solution)/shard_map/reduce_scatter | solution.py:191
  614.8 141.5 %reduce-scatter.13.cloned.1.call-done = f32[3072,24]{0,1:T(8,128)} async-done(((f32[3072,768]{0,1:T(8,128)}), f32[3072,24]{0,1:T(8,128)}) %reduce-scatter.13.cloned.1.call-update) | async-done | bytes 294928 | tf_op jit(solution)/shard_map/reduce_scatter | solution.py:199
  756.3 141.5 %reduce-scatter.11.cloned.1.call-done = f32[768,96]{0,1:T(8,128)} async-done(((f32[768,3072]{0,1:T(8,128)}), f32[768,96]{0,1:T(8,128)}) %reduce-scatter.11.cloned.1.call-update) | async-done | bytes 294928 | tf_op jit(solution)/shard_map/reduce_scatter | solution.py:197
  (237 shorter events, 115.4 us)
Async XLA Ops:
  7.2 6.1 copy-start
  8.0 4.7 copy-start.37
  26.7 40.4 %all-to-all-start = ((bf16[640,3,4,192]{0,3,1,2:T(8,128)(2,1)}), bf16[640,3,4,192]{0,3,1,2:T(8,128)(2,1)}, u32[]{:S(2)}, u32[]{:S(2)}) async-start(bf16[640,3,4,192]{0,3,1,2:T(8,128)(2,1)} %copy.132), calls=%async_computation | async-start | bytes 5898240 | tf_op jit(solution)/shard_map/all_to_all | solution.py:109
  82.2 8.9 copy-start.25
  115.2 10.9 %copy-start.22 = (f32[3,1280]{1,0:T(4,128)S(1)}, f32[3,1280]{1,0:T(4,128)}, u32[]{:S(2)}) copy-start(f32[3,1280]{1,0:T(4,128)} %get-tuple-element.372) | copy-start | bytes 46084 | tf_op jit(solution)/shard_map/while
  115.2 10.9 %copy-start.23 = (f32[3,1280]{1,0:T(4,128)S(1)}, f32[3,1280]{1,0:T(4,128)}, u32[]{:S(2)}) copy-start(f32[3,1280]{1,0:T(4,128)} %fusion.117) | copy-start | bytes 46084 | tf_op jit(solution)/shard_map/while
  115.2 10.9 %copy-start.26 = (f32[2,3,1280]{2,1,0:T(4,128)S(1)}, f32[2,3,1280]{2,1,0:T(4,128)}, u32[]{:S(2)}) copy-start(f32[2,3,1280]{2,1,0:T(4,128)} %get-tuple-element.395) | copy-start | bytes 92164 | tf_op jit(solution)/shard_map/while
  150.6 10.9 %copy-start.22 = (f32[3,1280]{1,0:T(4,128)S(1)}, f32[3,1280]{1,0:T(4,128)}, u32[]{:S(2)}) copy-start(f32[3,1280]{1,0:T(4,128)} %get-tuple-element.372) | copy-start | bytes 46084 | tf_op jit(solution)/shard_map/while
  150.6 10.9 %copy-start.23 = (f32[3,1280]{1,0:T(4,128)S(1)}, f32[3,1280]{1,0:T(4,128)}, u32[]{:S(2)}) copy-start(f32[3,1280]{1,0:T(4,128)} %fusion.117) | copy-start | bytes 46084 | tf_op jit(solution)/shard_map/while
  150.6 10.9 %copy-start.26 = (f32[2,3,1280]{2,1,0:T(4,128)S(1)}, f32[2,3,1280]{2,1,0:T(4,128)}, u32[]{:S(2)}) copy-start(f32[2,3,1280]{2,1,0:T(4,128)} %get-tuple-element.395) | copy-start | bytes 92164 | tf_op jit(solution)/shard_map/while
  182.1 18.0 %all-to-all-start.1 = ((bf16[4,640,192]{1,2,0:T(8,128)(2,1)}), bf16[4,640,192]{1,2,0:T(8,128)(2,1)}, u32[]{:S(2)}, u32[]{:S(2)}) async-start(bf16[4,640,192]{1,2,0:T(8,128)(2,1)} %copy.138), calls=%async_computation.1 | async-start | bytes 1966080 | tf_op jit(solution)/shard_map/all_to_all | solution.py:117
  187.1 36.0 %copy-start.42 = (f32[768]{0:T(1024)}, f32[768]{0:T(1024)S(1)}, u32[]{:S(2)}) copy-start(f32[768]{0:T(1024)S(1)} %convert_element_type.118) | copy-start | bytes 9220
  203.5 19.6 %copy-start.11 = (f32[640,768]{1,0:T(8,128)}, f32[640,768]{1,0:T(8,128)S(1)}, u32[]{:S(2)}) copy-start(f32[640,768]{1,0:T(8,128)S(1)} %get-tuple-element.270) | copy-start | bytes 5898244
  203.6 19.6 %copy-start.30 = (f32[640]{0:T(1024)}, f32[640]{0:T(1024)S(1)}, u32[]{:S(2)}) copy-start(f32[640]{0:T(1024)S(1)} %broadcast_multiply_fusion) | copy-start | bytes 7684
  203.6 6.8 slice-start.2
  204.0 19.2 %copy-start.44 = (f32[640]{0:T(1024)}, f32[640]{0:T(1024)S(1)}, u32[]{:S(2)}) copy-start(f32[640]{0:T(1024)S(1)} %fusion.60) | copy-start | bytes 7684
  204.0 6.4 copy-start.19
  204.0 6.4 copy-start.46
  204.0 6.4 slice-start.3
  204.0 15.0 %slice-start = ((s8[4718592]{0:T(1024)(128)(4,1)}), s8[4194304]{0:T(1024)(128)(4,1)S(1)}, s32[]{:S(2)}) async-start(s8[4718592]{0:T(1024)(128)(4,1)} %bitcast.169), calls=%async_computation.12 | async-start | bytes 8388608
  210.4 8.6 copy-start.52
  210.4 8.6 slice-start.1
  219.0 4.1 copy-start.53
  223.2 4.0 copy-start.51
  231.3 18.0 %all-to-all-start.2 = ((bf16[640,4,192]{0,2,1:T(8,128)(2,1)}), bf16[640,4,192]{0,2,1:T(8,128)(2,1)}, u32[]{:S(2)}, u32[]{:S(2)}) async-start(bf16[640,4,192]{0,2,1:T(8,128)(2,1)} %bitcast.166), calls=%async_computation.2 | async-start | bytes 1966080 | tf_op jit(solution)/shard_map/all_to_all | solution.py:153
  235.6 365.3 %reduce-scatter.9.cloned.1.call-start = ((), (), s32[]{:S(2)}) async-start(), calls=%async_computation.9 | async-start | bytes 2433024 | tf_op jit(solution)/shard_map/reduce_scatter | solution.py:193
  239.7 375.1 %reduce-scatter.7.cloned.1.call-start = ((), (), s32[]{:S(2)}) async-start(), calls=%async_computation.8 | async-start | bytes 7299072 | tf_op jit(solution)/shard_map/reduce_scatter | solution.py:191
  263.9 11.9 %copy-start.1 = (bf16[2,1280,3,64]{1,3,2,0:T(8,128)(2,1)S(1)}, bf16[2,1280,3,64]{1,3,2,0:T(8,128)(2,1)}, u32[]{:S(2)}) copy-start(bf16[2,1280,3,64]{1,3,2,0:T(8,128)(2,1)} %get-tuple-element.439) | copy-start | bytes 2949124 | tf_op jit(solution)/shard_map/while
  264.0 11.9 %copy-start.13 = (bf16[2,1280,3,64]{1,3,2,0:T(8,128)(2,1)S(1)}, bf16[2,1280,3,64]{1,3,2,0:T(8,128)(2,1)}, u32[]{:S(2)}) copy-start(bf16[2,1280,3,64]{1,3,2,0:T(8,128)(2,1)} %get-tuple-element.423) | copy-start | bytes 2949124 | tf_op jit(solution)/shard_map/while
  275.9 10.1 %copy-start.10 = (bf16[2,1280,3,64]{1,3,2,0:T(8,128)(2,1)S(1)}, bf16[2,1280,3,64]{1,3,2,0:T(8,128)(2,1)}, u32[]{:S(2)}) copy-start(bf16[2,1280,3,64]{1,3,2,0:T(8,128)(2,1)} %get-tuple-element.440) | copy-start | bytes 2949124 | tf_op jit(solution)/shard_map/while
  286.0 12.7 %copy-start.14 = (bf16[2,1280,3,64]{1,3,2,0:T(8,128)(2,1)}, bf16[2,1280,3,64]{1,3,2,0:T(8,128)(2,1)S(1)}, u32[]{:S(2)}) copy-start(bf16[2,1280,3,64]{1,3,2,0:T(8,128)(2,1)S(1)} %fusion.130) | copy-start | bytes 2949124 | tf_op jit(solution)/shard_map/while
  298.7 14.1 %copy-start.8 = (bf16[2,1280,3,64]{1,3,2,0:T(8,128)(2,1)S(1)}, bf16[2,1280,3,64]{1,3,2,0:T(8,128)(2,1)}, u32[]{:S(2)}) copy-start(bf16[2,1280,3,64]{1,3,2,0:T(8,128)(2,1)} %get-tuple-element.437) | copy-start | bytes 2949124 | tf_op jit(solution)/shard_map/while
  298.7 14.1 %copy-start.15 = (bf16[2,1280,3,64]{1,3,2,0:T(8,128)(2,1)S(1)}, bf16[2,1280,3,64]{1,3,2,0:T(8,128)(2,1)}, u32[]{:S(2)}) copy-start(bf16[2,1280,3,64]{1,3,2,0:T(8,128)(2,1)} %get-tuple-element.422) | copy-start | bytes 2949124 | tf_op jit(solution)/shard_map/while
  321.3 11.8 %copy-start.1 = (bf16[2,1280,3,64]{1,3,2,0:T(8,128)(2,1)S(1)}, bf16[2,1280,3,64]{1,3,2,0:T(8,128)(2,1)}, u32[]{:S(2)}) copy-start(bf16[2,1280,3,64]{1,3,2,0:T(8,128)(2,1)} %get-tuple-element.439) | copy-start | bytes 2949124 | tf_op jit(solution)/shard_map/while
  321.3 11.8 %copy-start.13 = (bf16[2,1280,3,64]{1,3,2,0:T(8,128)(2,1)S(1)}, bf16[2,1280,3,64]{1,3,2,0:T(8,128)(2,1)}, u32[]{:S(2)}) copy-start(bf16[2,1280,3,64]{1,3,2,0:T(8,128)(2,1)} %get-tuple-element.423) | copy-start | bytes 2949124 | tf_op jit(solution)/shard_map/while
  333.1 9.9 %copy-start.10 = (bf16[2,1280,3,64]{1,3,2,0:T(8,128)(2,1)S(1)}, bf16[2,1280,3,64]{1,3,2,0:T(8,128)(2,1)}, u32[]{:S(2)}) copy-start(bf16[2,1280,3,64]{1,3,2,0:T(8,128)(2,1)} %get-tuple-element.440) | copy-start | bytes 2949124 | tf_op jit(solution)/shard_map/while
  343.1 12.7 %copy-start.14 = (bf16[2,1280,3,64]{1,3,2,0:T(8,128)(2,1)}, bf16[2,1280,3,64]{1,3,2,0:T(8,128)(2,1)S(1)}, u32[]{:S(2)}) copy-start(bf16[2,1280,3,64]{1,3,2,0:T(8,128)(2,1)S(1)} %fusion.130) | copy-start | bytes 2949124 | tf_op jit(solution)/shard_map/while
  355.7 13.8 %copy-start.8 = (bf16[2,1280,3,64]{1,3,2,0:T(8,128)(2,1)S(1)}, bf16[2,1280,3,64]{1,3,2,0:T(8,128)(2,1)}, u32[]{:S(2)}) copy-start(bf16[2,1280,3,64]{1,3,2,0:T(8,128)(2,1)} %get-tuple-element.437) | copy-start | bytes 2949124 | tf_op jit(solution)/shard_map/while
  355.7 13.9 %copy-start.15 = (bf16[2,1280,3,64]{1,3,2,0:T(8,128)(2,1)S(1)}, bf16[2,1280,3,64]{1,3,2,0:T(8,128)(2,1)}, u32[]{:S(2)}) copy-start(bf16[2,1280,3,64]{1,3,2,0:T(8,128)(2,1)} %get-tuple-element.422) | copy-start | bytes 2949124 | tf_op jit(solution)/shard_map/while
  482.3 4.0 copy-start.38
  482.3 4.0 copy-start.40
  482.3 4.0 copy-start.48
  491.7 264.6 %reduce-scatter.13.cloned.1.call-start = ((), (), s32[]{:S(2)}) async-start(), calls=%async_computation.11 | async-start | bytes 9732096 | tf_op jit(solution)/shard_map/reduce_scatter | solution.py:199
  503.1 394.7 %reduce-scatter.11.cloned.1.call-start = ((), (), s32[]{:S(2)}) async-start(), calls=%async_computation.10 | async-start | bytes 9732096 | tf_op jit(solution)/shard_map/reduce_scatter | solution.py:197
  515.1 11.6 %copy-start.2 = (bf16[4,640,3,1,192]{1,0,4,2,3:T(4,128)(2,1)S(1)}, bf16[4,640,3,1,192]{1,0,4,2,3:T(4,128)(2,1)}, u32[]{:S(2)}) copy-start(bf16[4,640,3,1,192]{1,0,4,2,3:T(4,128)(2,1)} %copy.157) | copy-start | bytes 8847364
  532.7 6.7 copy-start.33
  532.7 6.8 copy-start.5
  532.8 6.8 copy-start.41
  (31 other events, 59.4 us)
Sparse Core Ops, SparseCore 0:
  242.2 102.1 reduce-scatter.8
  491.8 122.8 reduce-scatter.6
  621.2 135.0 reduce-scatter.12
  762.6 135.1 reduce-scatter.10
where the time goes:
time: 911 us; the launch traced here: 905 us
  waiting for transfers between devices  351 us (39%)
  matrix products  206 us (23%)
  local copies, waits for them, and re-layouts  136 us (15%)
  blocking collectives  110 us (12%)
  other arithmetic  71.1 us (8%)
  between operations  14.8 us (2%)
  starting transfers between devices  13.7 us (2%)
    reduce_scatter x1, waiting for transfers between devices, on_device(): lax.psum_scatter(down_grad, ('batch', 'head'), scatter_dimension=1, tiled...  142 us
    reduce_scatter x1, waiting for transfers between devices, on_device(): lax.psum_scatter(up_grad, ('batch', 'head'), scatter_dimension=1, tiled=T...  142 us
    all_to_all x1, blocking collectives, on_device(): lax.all_to_all(grad_stack.reshape(group_rows, 3, 1, local), 'head', split...  65.5 us
    dot_general x4, matrix products, masked_scores(): jnp.einsum('qhd,khd->hqk', q_rows, k_rows, preferred_element_type=jnp.flo...  48.1 us
    unnamed x1, blocking collectives  44.9 us
    all_to_all x1, waiting for transfers between devices, on_device(): lax.all_to_all(grouped, 'head', split_axis=2, concat_axis=0, tiled=True)  35.5 us
    convert_element_type x2, other arithmetic, attend_backward(): grad_scores = (probability * (grad_probs - center)).astype(jnp.bfloat16)  27.9 us
    dot_general x2, matrix products, attend_backward(): jnp.einsum('qhd,khd->hqk', grad_rows, v_rows, preferred_element_type=jnp....  25.3 us
  transfers between devices with their start and end apart: 7, of which 6 were waited for; matrix products, arithmetic and copies ran while one was open for 27% of the time, Pallas kernels for 0%

commit v1 on v0

v1 whole, which is shorter than its diff:
```python
import jax
import jax.numpy as jnp
from jax import lax
from jax.experimental import pallas as pl
from jax.experimental.pallas import tpu as pltpu
from jax.sharding import PartitionSpec as P

HEAD_DIM = 64
SEQ_LEN = 1280
PAIR = 2 * HEAD_DIM
BQ = 256
BK = 128
BLOCKS = 8
NEG = -1e30
F32 = jnp.float32
BF16 = jnp.bfloat16
VMEM_LIMIT = 56 * 1024 * 1024


def dot(left, right):
    return lax.dot_general(left, right, (((1,), (0,)), ((), ())), preferred_element_type=F32)


def dot_nt(left, right):
    return lax.dot_general(left, right, (((1,), (1,)), ((), ())), preferred_element_type=F32)


def center_and_scale(values):
    center = values - jnp.mean(values, -1, keepdims=True)
    spread = jnp.mean(center * center, -1, keepdims=True)
    scale = lax.rsqrt(spread + 1e-05)
    return center * scale, scale


def embed_tokens(tok_ref, ids_ref, emb_ref):
    ids = ids_ref[...]
    hidden = tok_ref[...].astype(F32)
    for row in range(emb_ref.shape[0]):
        hidden = hidden + jnp.where(ids == row, emb_ref[row : row + 1, :].astype(F32), 0.0)
    return hidden


def whole(shape):
    return pl.BlockSpec(shape, lambda *_: (0,) * len(shape))


def params():
    return pltpu.CompilerParams(vmem_limit_bytes=VMEM_LIMIT)


def cost(flops, moved):
    return pl.CostEstimate(flops=int(flops), transcendentals=0, bytes_accessed=int(moved))


def qkv_send_kernel(pos, tok, ids, emb, gain, shift, weight, bias, normed_out, out):
    @pl.when(pl.program_id(0) == 0)
    def _():
        scaled, _ = center_and_scale(embed_tokens(tok, ids, emb))
        normed_out[...] = (scaled * gain[...] + shift[...]).astype(BF16)

    out[0] = (dot(normed_out[...], weight[...]) + bias[...]).astype(BF16)


def qkv_keep_kernel(pos, normed, weight, bias, out):
    out[0] = (dot(normed[...], weight[...]) + bias[...]).astype(BF16)


def qkv_send(pos, tok, ids, emb, gain, shift, weight, bias):
    rows, width = tok.shape
    half = width // 2
    return pl.pallas_call(
        qkv_send_kernel,
        grid_spec=pltpu.PrefetchScalarGridSpec(
            num_scalar_prefetch=1,
            grid=(3,),
            in_specs=[
                whole(tok.shape),
                whole(ids.shape),
                whole(emb.shape),
                whole(gain.shape),
                whole(shift.shape),
                pl.BlockSpec((width, half), lambda t, s: (0, 2 * t + 1 - s[0])),
                pl.BlockSpec((1, half), lambda t, s: (0, 2 * t + 1 - s[0])),
            ],
            out_specs=[
                whole(tok.shape),
                pl.BlockSpec((1, rows, half), lambda t, s: (t, 0, 0)),
            ],
        ),
        out_shape=[
            jax.ShapeDtypeStruct(tok.shape, BF16),
            jax.ShapeDtypeStruct((3, rows, half), BF16),
        ],
        compiler_params=params(),
        cost_estimate=cost(3 * rows * width * width, 6e6),
        name="qkv_send",
    )(pos, tok, ids, emb, gain, shift, weight, bias)


def qkv_keep(pos, normed, weight, bias):
    rows, width = normed.shape
    half = width // 2
    return pl.pallas_call(
        qkv_keep_kernel,
        grid_spec=pltpu.PrefetchScalarGridSpec(
            num_scalar_prefetch=1,
            grid=(3,),
            in_specs=[
                whole(normed.shape),
                pl.BlockSpec((width, half), lambda t, s: (0, 2 * t + s[0])),
                pl.BlockSpec((1, half), lambda t, s: (0, 2 * t + s[0])),
            ],
            out_specs=pl.BlockSpec((1, rows, half), lambda t, s: (t, 0, 0)),
        ),
        out_shape=jax.ShapeDtypeStruct((3, rows, half), BF16),
        compiler_params=params(),
        cost_estimate=cost(3 * rows * width * width, 4e6),
        name="qkv_keep",
    )(pos, normed, weight, bias)


def lane_masks():
    lane = lax.broadcasted_iota(jnp.int32, (1, PAIR), 1)
    first = (lane < HEAD_DIM).astype(F32).astype(BF16)
    return first, (1 - first).astype(BF16)


def row_split(values):
    row = lax.broadcasted_iota(jnp.int32, values.shape, 0)
    keep = row < HEAD_DIM
    wide = values.astype(F32)
    return jnp.concatenate(
        [jnp.where(keep, wide, 0.0).astype(BF16), jnp.where(keep, 0.0, wide).astype(BF16)], axis=1
    )


def gather_rows(mine, other, target, sems, core, rows):
    own = pl.ds(pl.multiple_of(core * rows, 128), rows)
    far = pl.ds(pl.multiple_of((1 - core) * rows, 128), rows)
    if len(mine.shape) == 3:
        return (
            pltpu.make_async_copy(mine, target.at[:, own, :], sems.at[0]),
            pltpu.make_async_copy(other, target.at[:, far, :], sems.at[1]),
        )
    return (
        pltpu.make_async_copy(mine, target.at[own, :], sems.at[0]),
        pltpu.make_async_copy(other, target.at[far, :], sems.at[1]),
    )


def valid_keys(start, q0, kb):
    key_at = lax.broadcasted_iota(jnp.int32, (BK, BQ), 0) + kb * BK
    query_at = lax.broadcasted_iota(jnp.int32, (BK, BQ), 1) + q0
    inside = (key_at >= start) & (key_at <= query_at)
    return jnp.concatenate([inside, inside], axis=1)


def attend_kernel(pos, start_ref, keep, recv, own_out, far_out, lse_out, qkv, qq, vm, sc, acc, joined, sems):
    core = pos[0]
    rows = own_out.shape[0]
    pairs = own_out.shape[1] // PAIR
    copies = gather_rows(keep, recv, qkv, sems, core, rows)
    for item in copies:
        item.start()
    for item in copies:
        item.wait()
    first, second = lane_masks()

    def prepare(kb, _):
        at = pl.ds(pl.multiple_of(kb * BK, BK), BK)
        for p in range(pairs):
            vm[kb, p] = row_split(qkv[2, at, p * PAIR : (p + 1) * PAIR].T)
        return 0

    lax.fori_loop(0, SEQ_LEN // BK, prepare, 0)

    def one_block(qi, _):
        q0 = pl.multiple_of(qi * BQ, BQ)
        at = pl.ds(q0, BQ)
        start = start_ref[:, at]
        low = pos[8 + qi]
        high = (qi + 1) * (BQ // BK)
        for p in range(pairs):
            q = qkv[0, at, p * PAIR : (p + 1) * PAIR] * jnp.asarray(0.125, BF16)
            qq[p, :BQ] = q * first
            qq[p, BQ:] = q * second
            acc[p] = jnp.zeros((PAIR, BQ), F32)

        def scores(kb, tops):
            inside = valid_keys(start, q0, kb)
            rows_at = pl.ds(pl.multiple_of(kb * BK, BK), BK)
            grown = []
            for p in range(pairs):
                s = dot_nt(qkv[1, rows_at, p * PAIR : (p + 1) * PAIR], qq[p])
                s = jnp.where(inside, s, NEG)
                sc[kb - low, p] = s
                grown.append(jnp.maximum(tops[p], jnp.max(s, axis=0, keepdims=True)))
            return tuple(grown)

        tops = lax.fori_loop(
            low, high, scores, tuple(jnp.full((1, 2 * BQ), NEG, F32) for _ in range(pairs))
        )

        def weigh(kb, sums):
            grown = []
            for p in range(pairs):
                raw = jnp.exp(sc[kb - low, p] - tops[p])
                grown.append(sums[p] + jnp.sum(raw, axis=0, keepdims=True))
                raw = raw.astype(BF16)
                acc[p] += dot(vm[kb, p], jnp.concatenate([raw[:, :BQ], raw[:, BQ:]], axis=0))
            return tuple(grown)

        sums = lax.fori_loop(
            low, high, weigh, tuple(jnp.zeros((1, 2 * BQ), F32) for _ in range(pairs))
        )
        for p in range(pairs):
            inv = 1.0 / sums[p]
            out = jnp.concatenate(
                [acc[p, :HEAD_DIM] * inv[:, :BQ], acc[p, HEAD_DIM:] * inv[:, BQ:]], axis=0
            )
            joined[at, p * PAIR : (p + 1) * PAIR] = out.T.astype(BF16)
            lse_out[qi, p] = tops[p] + jnp.log(sums[p])
        return 0

    lax.fori_loop(0, SEQ_LEN // BQ, one_block, 0)
    own_out[...] = joined[pl.ds(pl.multiple_of(core * rows, 128), rows), :]
    far_out[...] = joined[pl.ds(pl.multiple_of((1 - core) * rows, 128), rows), :]


def attend(pos, start, keep, recv):
    _, rows, half = keep.shape
    pairs = half // PAIR
    window = SEQ_LEN // BK
    return pl.pallas_call(
        attend_kernel,
        grid_spec=pltpu.PrefetchScalarGridSpec(
            num_scalar_prefetch=1,
            grid=(1,),
            in_specs=[
                whole(start.shape),
                pl.BlockSpec(memory_space=pl.ANY),
                pl.BlockSpec(memory_space=pl.ANY),
            ],
            out_specs=[
                whole((rows, half)),
                whole((rows, half)),
                whole((SEQ_LEN // BQ, pairs, 1, 2 * BQ)),
            ],
            scratch_shapes=[
                pltpu.VMEM((3, SEQ_LEN, half), BF16),
                pltpu.VMEM((pairs, 2 * BQ, PAIR), BF16),
                pltpu.VMEM((SEQ_LEN // BK, pairs, PAIR, 2 * BK), BF16),
                pltpu.VMEM((window, pairs, BK, 2 * BQ), F32),
                pltpu.VMEM((pairs, PAIR, BQ), F32),
                pltpu.VMEM((SEQ_LEN, half), BF16),
                pltpu.SemaphoreType.DMA((2,)),
            ],
        ),
        out_shape=[
            jax.ShapeDtypeStruct((rows, half), BF16),
            jax.ShapeDtypeStruct((rows, half), BF16),
            jax.ShapeDtypeStruct((SEQ_LEN // BQ, pairs, 1, 2 * BQ), F32),
        ],
        compiler_params=params(),
        cost_estimate=cost(8e9, 5e6),
        name="attend",
    )(pos, start, keep, recv)


def attend_back_kernel(
    pos, start_ref, lse_ref, keep, recv, own, far, grad_own, grad_far,
    keep_out, send_out,
    qkv, att, dout, qq, dd, km, delta, dq_t, dq, dk, dv, sems,
):
    core = pos[0]
    rows, half = own.shape
    pairs = half // PAIR
    copies = (
        gather_rows(keep, recv, qkv, sems.at[0], core, rows)
        + gather_rows(own, far, att, sems.at[1], core, rows)
        + gather_rows(grad_own, grad_far, dout, sems.at[2], core, rows)
    )
    for item in copies:
        item.start()
    for item in copies:
        item.wait()
    first, second = lane_masks()
    dk[...] = jnp.zeros_like(dk)
    dv[...] = jnp.zeros_like(dv)

    def prepare(kb, _):
        at = pl.ds(pl.multiple_of(kb * BK, BK), BK)
        for p in range(pairs):
            km[kb, p] = row_split(qkv[1, at, p * PAIR : (p + 1) * PAIR].T)
        return 0

    lax.fori_loop(0, SEQ_LEN // BK, prepare, 0)

    def one_block(qi, _):
        q0 = pl.multiple_of(qi * BQ, BQ)
        at = pl.ds(q0, BQ)
        start = start_ref[:, at]
        low = pos[8 + qi]
        high = (qi + 1) * (BQ // BK)
        for p in range(pairs):
            lanes = slice(p * PAIR, (p + 1) * PAIR)
            q = qkv[0, at, lanes] * jnp.asarray(0.125, BF16)
            qq[p, :BQ] = q * first
            qq[p, BQ:] = q * second
            g = dout[at, lanes]
            dd[p, :BQ] = g * first
            dd[p, BQ:] = g * second
            both = (g.astype(F32) * att[at, lanes].astype(F32)).T
            delta[p] = jnp.concatenate(
                [
                    jnp.sum(both[:HEAD_DIM], axis=0, keepdims=True),
                    jnp.sum(both[HEAD_DIM:], axis=0, keepdims=True),
                ],
                axis=1,
            )
            dq_t[p] = jnp.zeros((PAIR, BQ), F32)

        def step(kb, _):
            inside = valid_keys(start, q0, kb)
            rows_at = pl.ds(pl.multiple_of(kb * BK, BK), BK)
            for p in range(pairs):
                lanes = slice(p * PAIR, (p + 1) * PAIR)
                s = dot_nt(qkv[1, rows_at, lanes], qq[p])
                prob = jnp.where(inside, jnp.exp(s - lse_ref[qi, p]), 0.0)
                grad_prob = dot_nt(qkv[2, rows_at, lanes], dd[p])
                grad_s = (prob * (grad_prob - delta[p])).astype(BF16)
                dv[rows_at, lanes] += dot(prob.astype(BF16), dd[p])
                dk[rows_at, lanes] += dot(grad_s, qq[p])
                dq_t[p] += dot(km[kb, p], jnp.concatenate([grad_s[:, :BQ], grad_s[:, BQ:]], axis=0))
            return 0

        lax.fori_loop(low, high, step, 0)
        for p in range(pairs):
            dq[at, p * PAIR : (p + 1) * PAIR] = (dq_t[p] * 0.125).T.astype(BF16)
        return 0

    lax.fori_loop(0, SEQ_LEN // BQ, one_block, 0)
    here = pl.ds(pl.multiple_of(core * rows, 128), rows)
    there = pl.ds(pl.multiple_of((1 - core) * rows, 128), rows)
    for target, at in ((keep_out, here), (send_out, there)):
        target[0] = dq[at, :]
        target[1] = dk[at, :].astype(BF16)
        target[2] = dv[at, :].astype(BF16)


def attend_back(pos, start, lse, keep, recv, own, far, grad_own, grad_far):
    _, rows, half = keep.shape
    pairs = half // PAIR
    hbm = pl.BlockSpec(memory_space=pl.ANY)
    return pl.pallas_call(
        attend_back_kernel,
        grid_spec=pltpu.PrefetchScalarGridSpec(
            num_scalar_prefetch=1,
            grid=(1,),
            in_specs=[whole(start.shape), whole(lse.shape), hbm, hbm, hbm, hbm, hbm, hbm],
            out_specs=[whole(keep.shape), whole(keep.shape)],
            scratch_shapes=[
                pltpu.VMEM((3, SEQ_LEN, half), BF16),
                pltpu.VMEM((SEQ_LEN, half), BF16),
                pltpu.VMEM((SEQ_LEN, half), BF16),
                pltpu.VMEM((pairs, 2 * BQ, PAIR), BF16),
                pltpu.VMEM((pairs, 2 * BQ, PAIR), BF16),
                pltpu.VMEM((SEQ_LEN // BK, pairs, PAIR, 2 * BK), BF16),
                pltpu.VMEM((pairs, 1, 2 * BQ), F32),
                pltpu.VMEM((pairs, PAIR, BQ), F32),
                pltpu.VMEM((SEQ_LEN, half), BF16),
                pltpu.VMEM((SEQ_LEN, half), F32),
                pltpu.VMEM((SEQ_LEN, half), F32),
                pltpu.SemaphoreType.DMA((3, 2)),
            ],
        ),
        out_shape=[jax.ShapeDtypeStruct(keep.shape, BF16)] * 2,
        compiler_params=params(),
        cost_estimate=cost(20e9, 8e6),
        name="attend_back",
    )(pos, start, lse, keep, recv, own, far, grad_own, grad_far)


def out_proj_kernel(pos, tok, ids, emb, own, far, weight, bias, gain, shift, after_out, normed_out):
    core = pos[0]
    half = own.shape[1]
    here = pl.ds(pl.multiple_of(core * half, 128), half)
    there = pl.ds(pl.multiple_of((1 - core) * half, 128), half)
    after = (
        embed_tokens(tok, ids, emb)
        + (dot(own[...], weight[here, :]) + dot(far[...], weight[there, :]))
        + bias[...]
    )
    after_out[...] = after
    scaled, _ = center_and_scale(after)
    normed_out[...] = (scaled * gain[...] + shift[...]).astype(BF16)


def simple_call(kernel, outs, flops, name, scratch=()):
    def call(pos, *operands):
        return pl.pallas_call(
            kernel,
            grid_spec=pltpu.PrefetchScalarGridSpec(
                num_scalar_prefetch=1,
                grid=(1,),
                in_specs=[whole(item.shape) for item in operands],
                out_specs=[whole(item.shape) for item in outs],
                scratch_shapes=list(scratch),
            ),
            out_shape=outs,
            compiler_params=params(),
            cost_estimate=cost(flops, sum(o.size * o.dtype.itemsize for o in list(operands) + outs)),
            name=name,
        )(pos, *operands)

    return call


def ff_first_kernel(
    pos, normed, cot, perm, up, up_bias, down, act_out, grad_out, keep_out, send_out, bias_grad, cot_t
):
    @pl.when(pl.program_id(0) == 0)
    def _():
        cot_t[...] = dot_nt(perm[...], cot[...]).astype(BF16)

    u = dot(normed[...], up[...]) + up_bias[...]
    grad_act = dot_nt(cot[...], down[...])
    square = u * u
    t = jnp.tanh(0.7978845608028654 * u * (1.0 + 0.044715 * square))
    half = 0.5 * (1.0 + t)
    act = (u * half).astype(BF16)
    act_out[...] = act
    slope = half + 0.5 * u * (1.0 - t * t) * (0.7978845608028654 * (1.0 + 0.134145 * square))
    grad = (grad_act * slope).astype(BF16)
    grad_out[...] = grad
    bias_grad[...] = jnp.sum(grad.astype(F32), axis=0, keepdims=True)
    down_t = dot(cot_t[...], act).astype(BF16)
    part = keep_out.shape[0]
    keep_out[...] = down_t[:part]
    send_out[...] = down_t[part:]


def ff_first(pos, normed, cot, perm, up, up_bias, down):
    rows, width = normed.shape
    hidden = up.shape[1]
    block = hidden // BLOCKS
    half = width // 2
    cols = pl.BlockSpec((rows, block), lambda i, s: (0, i))
    grads = pl.BlockSpec((half, block), lambda i, s: (0, i))
    return pl.pallas_call(
        ff_first_kernel,
        grid_spec=pltpu.PrefetchScalarGridSpec(
            num_scalar_prefetch=1,
            grid=(BLOCKS,),
            in_specs=[
                whole(normed.shape),
                whole(cot.shape),
                whole(perm.shape),
                pl.BlockSpec((width, block), lambda i, s: (0, i)),
                pl.BlockSpec((1, block), lambda i, s: (0, i)),
                pl.BlockSpec((block, width), lambda i, s: (i, 0)),
            ],
            out_specs=[cols, cols, grads, grads, pl.BlockSpec((1, block), lambda i, s: (0, i))],
            scratch_shapes=[pltpu.VMEM((width, rows), BF16)],
        ),
        out_shape=[
            jax.ShapeDtypeStruct((rows, hidden), BF16),
            jax.ShapeDtypeStruct((rows, hidden), BF16),
            jax.ShapeDtypeStruct((half, hidden), BF16),
            jax.ShapeDtypeStruct((half, hidden), BF16),
            jax.ShapeDtypeStruct((1, hidden), F32),
        ],
        compiler_params=params(),
        cost_estimate=cost(6 * rows * width * hidden, 24e6),
        name="ff_first",
    )(pos, normed, cot, perm, up, up_bias, down)


def place_rows(pos, rows_f32, keep_out, send_out):
    core, x_bit = pos[1], pos[2]
    per = keep_out.shape[2]
    for rel in range(2):
        x = rel ^ x_bit
        keep_out[rel, 0] = rows_f32[pl.ds(pl.multiple_of((2 * x + core) * per, 8), per), :].astype(BF16)
        send_out[rel, 0] = rows_f32[pl.ds(pl.multiple_of((2 * x + 1 - core) * per, 8), per), :].astype(BF16)


def ff_second_kernel(pos, grad, normed, up, total, keep_out, send_out, rows_f32):
    part = dot_nt(grad[...], up[...])

    @pl.when(pl.program_id(0) == 0)
    def _():
        total[...] = part

    @pl.when(pl.program_id(0) > 0)
    def _():
        total[...] += part

    rows_f32[...] = dot(grad[...].T, normed[...])
    place_rows(pos, rows_f32, keep_out, send_out)


def ff_second(pos, grad, normed, up):
    rows, width = normed.shape
    hidden = up.shape[1]
    block = hidden // BLOCKS
    shard = pl.BlockSpec((2, 1, block // 4, width), lambda i, s: (0, i ^ s[3], 0, 0))
    return pl.pallas_call(
        ff_second_kernel,
        grid_spec=pltpu.PrefetchScalarGridSpec(
            num_scalar_prefetch=1,
            grid=(BLOCKS,),
            in_specs=[
                pl.BlockSpec((rows, block), lambda i, s: (0, i)),
                whole(normed.shape),
                pl.BlockSpec((width, block), lambda i, s: (0, i)),
            ],
            out_specs=[whole((rows, width)), shard, shard],
            scratch_shapes=[pltpu.VMEM((block, width), F32)],
        ),
        out_shape=[
            jax.ShapeDtypeStruct((rows, width), F32),
            jax.ShapeDtypeStruct((2, BLOCKS, block // 4, width), BF16),
            jax.ShapeDtypeStruct((2, BLOCKS, block // 4, width), BF16),
        ],
        compiler_params=params(),
        cost_estimate=cost(4 * rows * width * hidden, 16e6),
        name="ff_second",
    )(pos, grad, normed, up)


def mixed_kernel(pos, act, down, after, bias, out, total):
    part = dot(act[...], down[...])
    step = pl.program_id(0)

    @pl.when(step == 0)
    def _():
        total[...] = part + (after[...] + bias[...])

    @pl.when(step > 0)
    def _():
        total[...] += part

    @pl.when(step == pl.num_programs(0) - 1)
    def _():
        out[...] = total[...].astype(BF16)


def mixed_call(pos, act, down, after, bias):
    rows, width = after.shape
    hidden = down.shape[0]
    steps = 4
    block = hidden // steps
    return pl.pallas_call(
        mixed_kernel,
        grid_spec=pltpu.PrefetchScalarGridSpec(
            num_scalar_prefetch=1,
            grid=(steps,),
            in_specs=[
                pl.BlockSpec((rows, block), lambda i, s: (0, i)),
                pl.BlockSpec((block, width), lambda i, s: (i, 0)),
                whole(after.shape),
                whole(bias.shape),
            ],
            out_specs=whole((rows, width)),
            scratch_shapes=[pltpu.VMEM((rows, width), F32)],
        ),
        out_shape=jax.ShapeDtypeStruct((rows, width), BF16),
        compiler_params=params(),
        cost_estimate=cost(2 * rows * width * hidden, 12e6),
        name="mixed",
    )(pos, act, down, after, bias)


def out_back_kernel(pos, grad_normed, after, cot, gain, weight, grad_after, branch_out, own_out, far_out, sums):
    core = pos[0]
    half = own_out.shape[1]
    scaled, scale = center_and_scale(after[...])
    grad = grad_normed[...]
    inner = grad * gain[...]
    shift = jnp.mean(inner, -1, keepdims=True)
    slope = jnp.mean(inner * scaled, -1, keepdims=True)
    cot_f32 = cot[...].astype(F32)
    total = cot_f32 + scale * (inner - shift - scaled * slope)
    grad_after[...] = total
    branch = total.astype(BF16)
    branch_out[...] = branch
    far_out[...] = dot_nt(
        branch, weight[pl.ds(pl.multiple_of((1 - core) * half, 128), half), :]
    ).astype(BF16)
    own_out[...] = dot_nt(branch, weight[pl.ds(pl.multiple_of(core * half, 128), half), :]).astype(BF16)
    sums[0:1] = jnp.sum(grad * scaled, axis=0, keepdims=True)
    sums[1:2] = jnp.sum(grad, axis=0, keepdims=True)
    sums[2:3] = jnp.sum(branch.astype(F32), axis=0, keepdims=True)
    sums[3:4] = jnp.sum(cot_f32, axis=0, keepdims=True)


def out_weight_kernel(pos, branch, perm, own, far, keep_out, send_out):
    core = pos[0]
    half = own.shape[1]
    turned = dot_nt(perm[...], branch[...]).astype(BF16)
    for part, at in ((own, core), (far, 1 - core)):
        got = dot(turned, part[...]).astype(BF16)
        lanes = pl.ds(pl.multiple_of(at * half, 128), half)
        keep_out[:, lanes] = got[:half]
        send_out[:, lanes] = got[half:]


def qkv_weight_kernel(pos, own, far, normed, keep_out, send_out, sums, turned, rows_f32):
    core = pos[0]
    half = own.shape[2]
    block = rows_f32.shape[0]

    @pl.when(pl.program_id(0) == 0)
    def _():
        for part, at in ((own, core), (far, 1 - core)):
            lanes = pl.ds(pl.multiple_of(at * half, 128), half)
            for t in range(3):
                turned[pl.ds(pl.multiple_of(t * 2 * half + at * half, 128), half), :] = part[t].T
                sums[t : t + 1, lanes] = jnp.sum(part[t].astype(F32), axis=0, keepdims=True)

    at = pl.ds(pl.multiple_of(pl.program_id(0) * block, 32), block)
    rows_f32[...] = dot(turned[at, :], normed[...])
    place_rows(pos, rows_f32, keep_out, send_out)


def qkv_weight_call(pos, own, far, normed):
    rows, width = normed.shape
    block = 3 * width // BLOCKS
    shard = pl.BlockSpec((2, 1, block // 4, width), lambda i, s: (0, i ^ s[3], 0, 0))
    return pl.pallas_call(
        qkv_weight_kernel,
        grid_spec=pltpu.PrefetchScalarGridSpec(
            num_scalar_prefetch=1,
            grid=(BLOCKS,),
            in_specs=[whole(own.shape), whole(far.shape), whole(normed.shape)],
            out_specs=[shard, shard, whole((3, width))],
            scratch_shapes=[pltpu.VMEM((3 * width, rows), BF16), pltpu.VMEM((block, width), F32)],
        ),
        out_shape=[
            jax.ShapeDtypeStruct((2, BLOCKS, block // 4, width), BF16),
            jax.ShapeDtypeStruct((2, BLOCKS, block // 4, width), BF16),
            jax.ShapeDtypeStruct((3, width), F32),
        ],
        compiler_params=params(),
        cost_estimate=cost(6 * rows * width * width, 8e6),
        name="qkv_weight",
    )(pos, own, far, normed)


def input_back_kernel(pos, own, far, weight, tok, ids, emb, gain, grad_after, out, sums):
    core = pos[0]
    half = own.shape[2]
    grad = None
    for t in range(3):
        for part, at in ((own, core), (far, 1 - core)):
            lanes = pl.ds(pl.multiple_of(t * 2 * half + at * half, 128), half)
            got = dot_nt(part[t], weight[:, lanes])
            grad = got if grad is None else grad + got
    scaled, scale = center_and_scale(embed_tokens(tok, ids, emb))
    inner = grad * gain[...]
    shift = jnp.mean(inner, -1, keepdims=True)
    slope = jnp.mean(inner * scaled, -1, keepdims=True)
    total = grad_after[...] + scale * (inner - shift - scaled * slope)
    out[...] = total
    passes = emb.shape[0]
    for row in range(passes):
        sums[row : row + 1] = jnp.sum(jnp.where(ids[...] == row, total, 0.0), axis=0, keepdims=True)
    sums[passes : passes + 1] = jnp.sum(grad * scaled, axis=0, keepdims=True)
    sums[passes + 1 : passes + 2] = jnp.sum(grad, axis=0, keepdims=True)


def add(left, right):
    return (left.astype(F32) + right.astype(F32)).astype(BF16)


def swap_head(values, bit):
    size = lax.axis_size("head")
    return lax.ppermute(values, "head", [(i, i ^ bit) for i in range(size)])


def swap_batch(values, bit):
    size = lax.axis_size("batch")
    return lax.ppermute(values, "batch", [(i, i ^ bit) for i in range(size)])


def over_x(values):
    return add(values[0], swap_head(values[1], 2))


def over_y(values):
    shape = values.shape
    split = values.reshape(shape[:-3] + (shape[-3] // 2, 2) + shape[-2:])
    return add(split[..., 0, :, :], swap_batch(split[..., 1, :, :], 1))


def over_z(values):
    got = [swap_batch(values[k], 2 * k) for k in range(1, values.shape[0])]
    total = values[0].astype(F32)
    for item in got:
        total = total + item.astype(F32)
    return total


def scatter_sum(keep, send, order):
    both = add(keep, swap_head(send, 1))
    if order == "xy":
        return over_z(over_y(over_x(both)))
    if order == "yx":
        return over_z(over_x(over_y(both)))
    cut = both.shape[-1] // 2
    left = over_y(over_x(both[..., :cut]))
    right = over_x(over_y(both[..., cut:]))
    return over_z(jnp.concatenate([left, right], axis=-1))


def scatter_any(keep, send):
    both = jnp.stack([keep, send], 0)
    both = both.transpose(2, 1, 0, 3, 4)
    both = both.reshape(-1, both.shape[-1])
    return lax.psum_scatter(both.astype(F32), ("batch", "head"), scatter_dimension=0, tiled=True)


def sum_small(items):
    count = lax.axis_size("batch") * lax.axis_size("head")
    flat = [
        item.reshape(item.shape[0], count, -1).transpose(1, 0, 2).reshape(count, -1)
        for item in items
    ]
    sizes = [item.shape[1] for item in flat]
    joined = jnp.concatenate(flat, 1)
    got = lax.all_to_all(joined, ("batch", "head"), split_axis=0, concat_axis=0, tiled=True)
    total = jnp.sum(got, 0)
    out, at = [], 0
    for item, size in zip(items, sizes):
        out.append(total[at : at + size].reshape(item.shape[0], -1))
        at += size
    return out


def relative_rows(pos, width, rows):
    at = jnp.arange(width, dtype=jnp.int32)
    inner = at % rows
    block = at // rows
    batch = (block % BLOCKS) ^ pos[3]
    x = ((block // BLOCKS) % 2) ^ pos[2]
    core = (block // (2 * BLOCKS)) ^ pos[1]
    return (batch * 4 + x * 2 + core) * rows + inner


def on_device(
    tokens,
    pass_ids,
    segment_ids,
    pass_embed,
    norm1_gain,
    norm1_shift,
    qkv_weight,
    qv_bias,
    out_weight,
    out_bias,
    norm2_gain,
    norm2_shift,
    up_weight,
    up_bias,
    down_weight,
    down_bias,
    cotangent,
):
    rows, width = tokens.shape
    half = width // 2
    hidden_units = up_weight.shape[1]
    passes = pass_embed.shape[0]
    assert 2 * rows == SEQ_LEN and lax.axis_size("head") == 4
    direct = lax.axis_size("batch") == BLOCKS

    head = lax.axis_index("head").astype(jnp.int32)
    batch = lax.axis_index("batch").astype(jnp.int32)
    core, x_bit = head % 2, head // 2
    segments = lax.dynamic_index_in_dim(segment_ids, x_bit, 0, keepdims=False)
    start = jnp.zeros((SEQ_LEN,), jnp.int32)
    for number in range(1, 4):
        before = jnp.sum((segments < number).astype(jnp.int32))
        start = jnp.where(segments == number, before, start)
    low = start[::BQ] // BK
    zero = jnp.zeros((), jnp.int32)
    place = [core, x_bit, batch] if direct else [zero, zero, zero]
    pos = jnp.concatenate([jnp.stack([core] + place + [zero] * 4), low])
    start = start.reshape(1, SEQ_LEN)

    ids = pass_ids.reshape(rows, 1)
    row = lambda item: item.astype(F32).reshape(1, -1)
    gain_one, shift_one = row(norm1_gain), row(norm1_shift)
    gain_two, shift_two = row(norm2_gain), row(norm2_shift)
    zeros = jnp.zeros((width,), F32)
    bias_full = jnp.concatenate([qv_bias[0].astype(F32), zeros, qv_bias[1].astype(F32)]).reshape(1, -1)
    shard_rows = width // (4 * BLOCKS)
    perm = (
        relative_rows(pos, width, shard_rows)[:, None] == jnp.arange(width, dtype=jnp.int32)[None, :]
    ).astype(BF16)

    shape = jax.ShapeDtypeStruct
    normed, send = qkv_send(pos, tokens, ids, pass_embed, gain_one, shift_one, qkv_weight, bias_full)
    recv = swap_head(send, 1)
    keep = qkv_keep(pos, normed, qkv_weight, bias_full)
    own, far_send, lse = attend(pos, start, keep, recv)
    far = swap_head(far_send, 1)
    after, normed_two = simple_call(
        out_proj_kernel,
        [shape((rows, width), F32), shape((rows, width), BF16)],
        2 * rows * width * width,
        "out_proj",
    )(pos, tokens, ids, pass_embed, own, far, out_weight, row(out_bias), gain_two, shift_two)
    activated, grad_pre, down_keep, down_send, up_bias_grad = ff_first(
        pos, normed_two, cotangent, perm, up_weight, row(up_bias), down_weight
    )
    grad_normed_two, up_keep, up_send = ff_second(pos, grad_pre, normed_two, up_weight)
    grad_after, branch, grad_own, grad_send, sums_two = simple_call(
        out_back_kernel,
        [
            shape((rows, width), F32),
            shape((rows, width), BF16),
            shape((rows, half), BF16),
            shape((rows, half), BF16),
            shape((4, width), F32),
        ],
        2 * rows * width * width,
        "out_back",
    )(pos, grad_normed_two, after, cotangent, gain_two, out_weight)
    grad_far = swap_head(grad_send, 1)
    out_keep, out_send = simple_call(
        out_weight_kernel,
        [shape((half, width), BF16), shape((half, width), BF16)],
        4 * rows * width * width,
        "out_weight",
    )(pos, branch, perm, own, far)
    joined_keep, joined_send = attend_back(
        pos, start, lse, keep, recv, own, far_send, grad_own, grad_far
    )
    joined_recv = swap_head(joined_send, 1)
    qkv_keep_grad, qkv_send_grad, bias_sums = qkv_weight_call(pos, joined_keep, joined_recv, normed)
    input_grad, sums_one = simple_call(
        input_back_kernel,
        [shape((rows, width), F32), shape((passes + 2, width), F32)],
        6 * rows * width * width,
        "input_back",
    )(pos, joined_keep, joined_recv, qkv_weight, tokens, ids, pass_embed, gain_one, grad_after)
    result = mixed_call(pos, activated, down_weight, after, row(down_bias))

    def spread(item):
        return item.reshape(2, BLOCKS, shard_rows, -1)

    down_keep, down_send = spread(down_keep), spread(down_send)
    out_keep, out_send = spread(out_keep), spread(out_send)
    if direct:
        down_grad = scatter_sum(down_keep, down_send, "xy")
        up_grad = scatter_sum(up_keep, up_send, "yx")
        out_grad = scatter_sum(out_keep, out_send, "yx")
        qkv_grad = scatter_sum(qkv_keep_grad, qkv_send_grad, "both")
    else:
        down_grad = scatter_any(down_keep, down_send)
        up_grad = scatter_any(up_keep, up_send)
        out_grad = scatter_any(out_keep, out_send)
        qkv_grad = scatter_any(qkv_keep_grad, qkv_send_grad)
    small = sum_small([sums_one, bias_sums, sums_two, up_bias_grad])
    return (
        result,
        input_grad,
        small[0][:passes],
        small[0][passes],
        small[0][passes + 1],
        qkv_grad.T,
        jnp.stack([small[1][0], small[1][2]]),
        out_grad.T,
        small[2][2],
        small[2][0],
        small[2][1],
        up_grad.T,
        small[3][0],
        down_grad.T,
        small[2][3],
    )


def solution(mesh):
    both = ("batch", "head")
    copied = P()
    in_specs = (P(both, None), P(both), P("batch", None)) + (copied,) * 13 + (P(both, None),)
    out_specs = (
        P(both, None),
        P(both, None),
        P(None, both),
        P(both),
        P(both),
        P(None, both),
        P(None, both),
        P(None, both),
        P(both),
        P(both),
        P(both),
        P(None, both),
        P(both),
        P(None, both),
        P(both),
    )
    return jax.shard_map(
        on_device, mesh=mesh, in_specs=in_specs, out_specs=out_specs, check_vma=False
    )
```

time: 911 us -> 292 us (0.32)
  waiting for transfers between devices: 351 us -> 44.6 us
  matrix products: 206 us -> 0 us
  Pallas kernels: 0 us -> 143 us
  local copies, waits for them, and re-layouts: 136 us -> 23 us
  blocking collectives: 110 us -> 0 us
  other arithmetic: 71.1 us -> 25.8 us
  starting transfers between devices: 13.7 us -> 53.9 us
  between operations: 14.8 us -> 1.07 us
    reduce_scatter x4 -> x0, waiting for transfers between devices: 297 us -> none  [the longest x1 142 us: on_device(): lax.psum_scatter(down_grad, ('batch', 'head'), scatter_dimension=1, tiled...]
    dot_general x28 -> x0, matrix products: 206 us -> none  [the longest x4 48.1 us: masked_scores(): jnp.einsum('qhd,khd->hqk', q_rows, k_rows, preferred_element_type=jnp.flo...]
    pallas_call x0 -> x12, Pallas kernels: none -> 143 us  [the longest x4 30.5 us: call(): pl.pallas_call(kernel, grid_spec=pltpu.PrefetchScalarGridSpec(num_scalar_...]
    all_to_all x1 -> x0, blocking collectives: 65.5 us -> none  [on_device(): lax.all_to_all(grad_stack.reshape(group_rows, 3, 1, local), 'head', split...]
    all_to_all x3 -> x1, waiting for transfers between devices: 54.4 us -> 0.01 us  [sum_small(): lax.all_to_all(joined, ('batch', 'head'), split_axis=0, concat_axis=0, ti...]
    ppermute x0 -> x30, starting transfers between devices: none -> 49.6 us  [the longest x17 43.2 us: swap_batch(): return lax.ppermute(values, 'batch', [(i, i ^ bit) for i in range(size)])]
    unnamed x1 -> x0, blocking collectives: 44.9 us -> none
    ppermute x0 -> x30, waiting for transfers between devices: none -> 44.6 us  [the longest x13 23.6 us: swap_head(): return lax.ppermute(values, 'head', [(i, i ^ bit) for i in range(size)])]
  transfers between devices with their start and end apart: 7 -> 31, of which waited for: 6 -> 11; matrix products, arithmetic and copies ran while one was open for 27% -> 11% of each run, Pallas kernels for 0% -> 21%
where the time goes in v1:
time: 292 us
  Pallas kernels  143 us (49%)
  starting transfers between devices  53.9 us (18%)
  waiting for transfers between devices  44.6 us (15%)
  other arithmetic  25.8 us (9%)
  local copies, waits for them, and re-layouts  23 us (8%)
    ppermute x17, starting transfers between devices, swap_batch(): return lax.ppermute(values, 'batch', [(i, i ^ bit) for i in range(size)])  43.2 us
    pallas_call x4, Pallas kernels, call(): pl.pallas_call(kernel, grid_spec=pltpu.PrefetchScalarGridSpec(num_scalar_...  30.5 us
    pallas_call x1, Pallas kernels, attend_back(): pl.pallas_call(attend_back_kernel, grid_spec=pltpu.PrefetchScalarGridSpec...  26 us
    ppermute x13, waiting for transfers between devices, swap_head(): return lax.ppermute(values, 'head', [(i, i ^ bit) for i in range(size)])  23.6 us
    ppermute x17, waiting for transfers between devices, swap_batch(): return lax.ppermute(values, 'batch', [(i, i ^ bit) for i in range(size)])  21 us
    pallas_call x1, Pallas kernels, ff_first(): pl.pallas_call(ff_first_kernel, grid_spec=pltpu.PrefetchScalarGridSpec(nu...  19.7 us
    pallas_call x1, Pallas kernels, ff_second(): pl.pallas_call(ff_second_kernel, grid_spec=pltpu.PrefetchScalarGridSpec(n...  18.8 us
    pallas_call x1, Pallas kernels, attend(): pl.pallas_call(attend_kernel, grid_spec=pltpu.PrefetchScalarGridSpec(num_...  17 us
  transfers between devices with their start and end apart: 31, of which 11 were waited for; matrix products, arithmetic and copies ran while one was open for 11% of the time, Pallas kernels for 21%

profile of v1, /device:TPU:0, one launch (start us, length us, event | category | flops | bytes accessed | tf_op | source)
XLA Modules:
  0.0 291.7 jit_solution(6932085012881035652)
XLA Ops:
  0.7 1.4 fusion.36
  2.1 3.3 %fusion.57 = (s32[1280]{0:T(1024)S(1)}, s32[1,1280]{1,0:T(1,128)}) fusion(s32[]{:T(128)} %get-tuple-element.74, s32[]{:T(128)} %get-tuple-element.75, s32[]{:T(128)} %get-tuple-element.73, s32[2,1280]{1,0:T(2,128)} %param.19, s32[]{:T(128)S(6)} %select_n.93), kind=kLoop, calls=%fused_computation.149 | loop fusion | flops 7680 | bytes 15376 | tf_op jit(solution)/shard_map/jit(_where)/select_n | solution.py:784
  6.8 1.6 reshape.334.ids
  11.5 7.2 %qkv_send.1 = (bf16[640,768]{1,0:T(8,128)(2,1)}, bf16[3,640,384]{2,1,0:T(8,128)(2,1)}) custom-call(s32[13]{0:T(128)} %concatenate.12.pos, bf16[640,768]{1,0:T(8,128)(2,1)} %tok.5, s32[640,1]{1,0:T(8,128)} %reshape.334.ids, bf16[5,768]{1,0:T(8,128)(2,1)} %emb.5, f32[1,768]{1,0:T(1,128)} %reshape.303.gain, f32[1,768]{1,0:T(1,128)} %reshape.305.shift, ...), custom_call_target="tpu_custom_call" | custom-call | flops 1132462080 | bytes 6000000 | tf_op jit(solution)/shard_map/qkv_send/pallas_call | solution.py:71
  19.2 5.5 %qkv_keep.1.keep = bf16[3,640,384]{2,1,0:T(8,128)(2,1)} custom-call(s32[13]{0:T(128)} %concatenate.12.pos, bf16[640,768]{1,0:T(8,128)(2,1)} %get-tuple-element.44.normed, bf16[768,2304]{1,0:T(8,128)(2,1)} %weight.9, f32[1,2304]{1,0:T(1,128)} %reshape.278.bias), custom_call_target="tpu_custom_call" | custom-call | flops 1132462080 | bytes 4000000 | tf_op jit(solution)/shard_map/qkv_keep/pallas_call | solution.py:103
  25.8 17.0 %attend.1 = (bf16[640,384]{1,0:T(8,128)(2,1)}, bf16[640,384]{1,0:T(8,128)(2,1)}, f32[5,3,1,512]{3,2,1,0:T(1,128)}) custom-call(s32[13]{0:T(128)} %concatenate.12.pos, s32[1,1280]{1,0:T(1,128)} %get-tuple-element.79.start_ref, bf16[3,640,384]{2,1,0:T(8,128)(2,1)} %qkv_keep.1.keep, bf16[3,640,384]{2,1,0:T(8,128)(2,1)} %copy-done.12), custom_call_target="tpu_custom_call" | custom-call | flops 8000000000 | bytes 5000000 | tf_op jit(solution)/shard_map/attend/pallas_call | solution.py:234
  45.3 1.3 fusion.3.perm
  47.4 5.9 %out_proj.1 = (f32[640,768]{1,0:T(8,128)}, bf16[640,768]{1,0:T(8,128)(2,1)}) custom-call(s32[13]{0:T(128)} %concatenate.12.pos, bf16[640,768]{1,0:T(8,128)(2,1)} %tok.5, s32[640,1]{1,0:T(8,128)} %reshape.334.ids, bf16[5,768]{1,0:T(8,128)(2,1)} %emb.5, bf16[640,384]{1,0:T(8,128)(2,1)} %get-tuple-element.46.own, bf16[640,384]{1,0:T(8,128)(2,1)} %copy-done.3, ...), custom_call_target="tpu_custom_call" | custom-call | flops 754974720 | bytes 6114304 | tf_op jit(solution)/shard_map/out_proj/pallas_call | solution.py:401
  53.3 19.7 %ff_first.1 = (bf16[640,3072]{1,0:T(8,128)(2,1)}, bf16[640,3072]{1,0:T(8,128)(2,1)}, bf16[384,3072]{1,0:T(8,128)(2,1)}, bf16[384,3072]{1,0:T(8,128)(2,1)}, f32[1,3072]{1,0:T(1,128)}) custom-call(s32[13]{0:T(128)} %concatenate.12.pos, bf16[640,768]{1,0:T(8,128)(2,1)} %get-tuple-element.48.normed, bf16[640,768]{1,0:T(8,128)(2,1)} %cot.3, ...), custom_call_target="tpu_custom_call" | custom-call | flops 9059696640 | bytes 24000000 | tf_op jit(solution)/shard_map/ff_first/pallas_call | solution.py:450
  73.1 18.8 %ff_second.1 = (f32[640,768]{1,0:T(8,128)}, bf16[2,8,96,768]{3,2,1,0:T(8,128)(2,1)}, bf16[2,8,96,768]{3,2,1,0:T(8,128)(2,1)}) custom-call(s32[13]{0:T(128)} %concatenate.12.pos, bf16[640,3072]{1,0:T(8,128)(2,1)} %get-tuple-element.52.grad, bf16[640,768]{1,0:T(8,128)(2,1)} %get-tuple-element.48.normed, bf16[768,3072]{1,0:T(8,128)(2,1)} %up.3), custom_call_target="tpu_custom_call" | custom-call | flops 6039797760 | bytes 16000000 | tf_op jit(solution)/shard_map/ff_second/pallas_call | solution.py:508
  91.9 7.1 %out_back.1 = (f32[640,768]{1,0:T(8,128)}, bf16[640,768]{1,0:T(8,128)(2,1)}, bf16[640,384]{1,0:T(8,128)(2,1)}, bf16[640,384]{1,0:T(8,128)(2,1)}, f32[4,768]{1,0:T(4,128)}) custom-call(s32[13]{0:T(128)} %concatenate.12.pos, f32[640,768]{1,0:T(8,128)} %get-tuple-element.53.grad_normed, f32[640,768]{1,0:T(8,128)} %get-tuple-element.50.after, ...), custom_call_target="tpu_custom_call" | custom-call | flops 754974720 | bytes 10042368 | tf_op jit(solution)/shard_map/out_back/pallas_call | solution.py:401
  98.9 6.0 %out_weight.1 = (bf16[384,768]{1,0:T(8,128)(2,1)}, bf16[384,768]{1,0:T(8,128)(2,1)}) custom-call(s32[13]{0:T(128)} %concatenate.12.pos, bf16[640,768]{1,0:T(8,128)(2,1)} %get-tuple-element.66.branch, bf16[768,768]{1,0:T(8,128)(2,1)} %fusion.3.perm, bf16[640,384]{1,0:T(8,128)(2,1)} %get-tuple-element.46.own, bf16[640,384]{1,0:T(8,128)(2,1)} %copy-done.3), custom_call_target="tpu_custom_call" | custom-call | flops 1509949440 | bytes 4325376 | tf_op jit(solution)/shard_map/out_weight/pallas_call | solution.py:401
  108.5 1.8 collective-permute-start.13
  112.1 26.0 %attend_back.1 = (bf16[3,640,384]{2,1,0:T(8,128)(2,1)}, bf16[3,640,384]{2,1,0:T(8,128)(2,1)}) custom-call(s32[13]{0:T(128)} %concatenate.12.pos, s32[1,1280]{1,0:T(1,128)} %get-tuple-element.79.start_ref, f32[5,3,1,512]{3,2,1,0:T(1,128)} %get-tuple-element.51.lse_ref, bf16[3,640,384]{2,1,0:T(8,128)(2,1)} %qkv_keep.1.keep, bf16[3,640,384]{2,1,0:T(8,128)(2,1)} %copy-done.12, ...), custom_call_target="tpu_custom_call" | custom-call | flops 20000000000 | bytes 8000000 | tf_op jit(solution)/shard_map/attend_back/pallas_call | solution.py:355
  140.0 1.5 copy.58
  143.0 2.0 reduce.12
  145.0 1.4 reshape_transpose_reshape.3
  146.5 9.0 %mixed.1 = bf16[640,768]{1,0:T(8,128)(2,1)} custom-call(s32[13]{0:T(128)} %concatenate.12.pos, bf16[640,3072]{1,0:T(8,128)(2,1)} %get-tuple-element.49.act, bf16[3072,768]{1,0:T(8,128)(2,1)} %down.3, f32[640,768]{1,0:T(8,128)} %get-tuple-element.50.after, f32[1,768]{1,0:T(1,128)} %reshape.317.bias), custom_call_target="tpu_custom_call" | custom-call | flops 3019898880 | bytes 12000000 | tf_op jit(solution)/shard_map/mixed/pallas_call | solution.py:554
  156.3 5.8 %collective-permute-start.15 = (bf16[24,768]{1,0:T(8,128)(2,1)}, bf16[24,768]{1,0:T(8,128)(2,1)}, u32[]{:S(2)}, u32[]{:S(2)}) collective-permute-start(bf16[24,768]{1,0:T(8,128)(2,1)} %get-tuple-element.89), channel_id=1, source_target_pairs={{0,8},{4,12},{8,0},{12,4},{16,24},{20,28},{24,16},{28,20},{1,9},{5... | collective-permute-start | bytes 110600 | tf_op jit(solution)/shard_map/ppermute | solution.py:684
  162.1 4.0 %collective-permute-start.16 = (bf16[24,768]{1,0:T(8,128)(2,1)}, bf16[24,768]{1,0:T(8,128)(2,1)}, u32[]{:S(2)}, u32[]{:S(2)}) collective-permute-start(bf16[24,768]{1,0:T(8,128)(2,1)} %get-tuple-element.91), channel_id=1, source_target_pairs={{0,16},{4,20},{8,24},{12,28},{16,0},{20,4},{24,8},{28,12},{1,17},{... | collective-permute-start | bytes 110600 | tf_op jit(solution)/shard_map/ppermute | solution.py:684
  166.2 9.7 %qkv_weight.1 = (bf16[2,8,72,768]{3,2,1,0:T(8,128)(2,1)}, bf16[2,8,72,768]{3,2,1,0:T(8,128)(2,1)}, f32[3,768]{1,0:T(4,128)}) custom-call(s32[13]{0:T(128)} %concatenate.12.pos, bf16[3,640,384]{2,1,0:T(8,128)(2,1)} %get-tuple-element.56.own, bf16[3,640,384]{2,1,0:T(8,128)(2,1)} %collective-permute-done.3.far, bf16[640,768]{1,0:T(8,128)(2,1)} %get-tuple-element.44.normed), custom_call_target="tpu_custom_call" | custom-call | flops 2264924160 | bytes 8000000 | tf_op jit(solution)/shard_map/qkv_weight/pallas_call | solution.py:631
  175.9 11.5 %input_back.1 = (f32[640,768]{1,0:T(8,128)}, f32[7,768]{1,0:T(8,128)}) custom-call(s32[13]{0:T(128)} %concatenate.12.pos, bf16[3,640,384]{2,1,0:T(8,128)(2,1)} %get-tuple-element.56.own, bf16[3,640,384]{2,1,0:T(8,128)(2,1)} %collective-permute-done.3.far, bf16[768,2304]{1,0:T(8,128)(2,1)} %weight.9, bf16[640,768]{1,0:T(8,128)(2,1)} %tok.5, ...), custom_call_target="tpu_custom_call" | custom-call | flops 2264924160 | bytes 11438080 | tf_op jit(solution)/shard_map/input_back/pallas_call | solution.py:401
  189.5 4.4 %all-to-all-start = ((f32[32,1,432]{2,1,0:T(1,128)}), f32[32,1,432]{2,1,0:T(1,128)}, u32[]{:S(2)}, u32[]{:S(2)}) async-start(f32[32,1,432]{2,1,0:T(1,128)} %copy.60), calls=%async_computation | async-start | bytes 131072 | tf_op jit(solution)/shard_map/all_to_all | solution.py:732
  193.9 1.4 copy-done
  195.3 3.3 %fusion = bf16[2,8,24,3072]{3,2,1,0:T(8,128)(2,1)S(1)} fusion(bf16[2,8,24,3072]{3,2,1,0:T(8,128)(2,1)} %bitcast.169, bf16[2,8,24,3072]{3,2,1,0:T(8,128)(2,1)} %copy-done), kind=kLoop, calls=%fused_computation.1 | loop fusion | flops 4718592 | bytes 7077888 | tf_op jit(solution)/shard_map/convert_element_type | solution.py:674
  199.7 1.7 collective-permute-start.25
  201.4 1.5 fusion.31
  206.2 3.1 %add_convert_fusion = bf16[2,8,96,768]{3,2,1,0:T(8,128)(2,1)S(1)} fusion(bf16[2,8,96,768]{3,2,1,0:T(8,128)(2,1)} %collective-permute-done.18, bf16[2,8,96,768]{3,2,1,0:T(8,128)(2,1)} %get-tuple-element.69), kind=kLoop, calls=%fused_computation.2 | loop fusion | flops 4718592 | bytes 7077888 | tf_op jit(solution)/shard_map/convert_element_type | solution.py:674
  209.3 1.5 collective-permute-start.19
  210.9 17.1 %collective-permute-done.25 = bf16[8,24,3072]{2,1,0:T(8,128)(2,1)S(1)} collective-permute-done((bf16[8,24,3072]{2,1,0:T(8,128)(2,1)}, bf16[8,24,3072]{2,1,0:T(8,128)(2,1)S(1)}, u32[]{:S(2)}, u32[]{:S(2)}) %collective-permute-start.25) | collective-permute-done | bytes 1179680 | tf_op jit(solution)/shard_map/ppermute | solution.py:679
  228.4 1.7 collective-permute-start.26
  230.1 8.1 %collective-permute-done.19 = bf16[2,4,96,768]{3,2,1,0:T(8,128)(2,1)S(1)} collective-permute-done((bf16[2,4,96,768]{3,2,1,0:T(8,128)(2,1)S(1)}, bf16[2,4,96,768]{3,2,1,0:T(8,128)(2,1)S(1)}, u32[]{:S(2)}, u32[]{:S(2)}) %collective-permute-start.19) | collective-permute-done | bytes 1179680 | tf_op jit(solution)/shard_map/ppermute | solution.py:684
  239.0 1.9 add_convert_fusion.1
  241.1 1.8 collective-permute-start.7
  242.9 1.5 collective-permute-start.5
  244.5 6.4 %collective-permute-done.26 = bf16[4,24,3072]{2,1,0:T(8,128)(2,1)S(1)} collective-permute-done((bf16[4,24,3072]{2,1,0:T(8,128)(2,1)S(1)}, bf16[4,24,3072]{2,1,0:T(8,128)(2,1)S(1)}, u32[]{:S(2)}, u32[]{:S(2)}) %collective-permute-start.26) | collective-permute-done | bytes 589856 | tf_op jit(solution)/shard_map/ppermute | solution.py:684
  251.1 1.5 collective-permute-start.27
  252.6 2.4 collective-permute-start.28
  255.0 3.2 %collective-permute-start.29 = (bf16[24,3072]{1,0:T(8,128)(2,1)S(1)}, bf16[24,3072]{1,0:T(8,128)(2,1)S(1)}, u32[]{:S(2)}, u32[]{:S(2)}) collective-permute-start(bf16[24,3072]{1,0:T(8,128)(2,1)S(1)} %get-tuple-element.81), channel_id=1, source_target_pairs={{0,24},{4,28},{8,16},{12,20},{16,8},{20,12},{24,0},{28,4},{1,25},{... | collective-permute-start | bytes 442376 | tf_op jit(solution)/shard_map/ppermute | solution.py:684
  258.4 1.5 collective-permute-done.7
  259.9 1.5 collective-permute-start.21
  262.6 2.4 collective-permute-start.22
  265.1 1.5 collective-permute-start.23
  267.2 1.5 collective-permute-start.6
  269.5 3.1 %collective-permute-done.8 = bf16[4,72,384]{2,1,0:T(8,128)(2,1)S(1)} collective-permute-done((bf16[4,72,384]{2,1,0:T(8,128)(2,1)S(1)}, bf16[4,72,384]{2,1,0:T(8,128)(2,1)S(1)}, u32[]{:S(2)}, u32[]{:S(2)}) %collective-permute-start.8) | collective-permute-done | bytes 221216 | tf_op jit(solution)/shard_map/ppermute | solution.py:679
  273.2 9.8 %collective-permute-start.10 = (bf16[72,768]{1,0:T(8,128)(2,1)S(1)}, bf16[72,768]{1,0:T(8,128)(2,1)S(1)}, u32[]{:S(2)}, u32[]{:S(2)}) collective-permute-start(bf16[72,768]{1,0:T(8,128)(2,1)S(1)} %get-tuple-element.88), channel_id=1, source_target_pairs={{0,16},{4,20},{8,24},{12,28},{16,0},{20,4},{24,8},{28,12},{1,17},{... | collective-permute-start | bytes 331784 | tf_op jit(solution)/shard_map/ppermute | solution.py:684
  283.1 2.7 collective-permute-start.11
  286.6 3.2 %collective-permute-done.11 = bf16[72,768]{1,0:T(8,128)(2,1)S(1)} collective-permute-done((bf16[72,768]{1,0:T(8,128)(2,1)S(1)}, bf16[72,768]{1,0:T(8,128)(2,1)S(1)}, u32[]{:S(2)}, u32[]{:S(2)}) %collective-permute-start.11) | collective-permute-done | bytes 110624 | tf_op jit(solution)/shard_map/ppermute | solution.py:684
  (129 shorter events, 33.5 us)
Async XLA Ops:
  18.7 6.0 %collective-permute-start = (bf16[3,640,384]{2,1,0:T(8,128)(2,1)}, bf16[3,640,384]{2,1,0:T(8,128)(2,1)S(1)}, u32[]{:S(2)}, u32[]{:S(2)}) collective-permute-start(bf16[3,640,384]{2,1,0:T(8,128)(2,1)} %get-tuple-element.45), channel_id=1, source_target_pairs={{0,1},{1,0},{2,3},{3,2},{4,5},{5,4},{6,7},{7,6},{8,9},{9,8},{10,11... | collective-permute-start | bytes 4423688 | tf_op jit(solution)/shard_map/ppermute | solution.py:679
  24.7 1.1 copy-start.12
  25.8 17.1 %copy-start.8 = (bf16[768]{0:T(1024)(128)(2,1)S(1)}, bf16[768]{0:T(1024)(128)(2,1)}, u32[]{:S(2)}) copy-start(bf16[768]{0:T(1024)(128)(2,1)} %param.27) | copy-start | bytes 4612
  25.8 17.7 %copy-start.9 = (bf16[768]{0:T(1024)(128)(2,1)S(1)}, bf16[768]{0:T(1024)(128)(2,1)}, u32[]{:S(2)}) copy-start(bf16[768]{0:T(1024)(128)(2,1)} %param.26) | copy-start | bytes 4612
  25.8 18.3 %copy-start.10 = (bf16[768]{0:T(1024)(128)(2,1)S(1)}, bf16[768]{0:T(1024)(128)(2,1)}, u32[]{:S(2)}) copy-start(bf16[768]{0:T(1024)(128)(2,1)} %param.28) | copy-start | bytes 4612
  25.8 18.8 %copy-start.7 = (bf16[3072]{0:T(1024)(128)(2,1)S(1)}, bf16[3072]{0:T(1024)(128)(2,1)}, u32[]{:S(2)}) copy-start(bf16[3072]{0:T(1024)(128)(2,1)} %param.30) | copy-start | bytes 18436
  42.8 3.8 %collective-permute-start.1 = (bf16[640,384]{1,0:T(8,128)(2,1)}, bf16[640,384]{1,0:T(8,128)(2,1)S(1)}, u32[]{:S(2)}, u32[]{:S(2)}) collective-permute-start(bf16[640,384]{1,0:T(8,128)(2,1)} %get-tuple-element.47.far), channel_id=1, source_target_pairs={{0,1},{1,0},{2,3},{3,2},{4,5},{5,4},{6,7},{7,6},{8,9},{9,8},{10,11... | collective-permute-start | bytes 1474568 | tf_op jit(solution)/shard_map/ppermute | solution.py:679
  46.7 0.8 copy-start.3
  98.9 6.5 %copy-start.13 = (bf16[640,384]{1,0:T(8,128)(2,1)S(1)}, bf16[640,384]{1,0:T(8,128)(2,1)}, u32[]{:S(2)}) copy-start(bf16[640,384]{1,0:T(8,128)(2,1)} %get-tuple-element.55) | copy-start | bytes 1474564
  104.9 2.4 collective-permute-start.12
  105.4 88.4 %collective-permute-start.24 = (bf16[2,8,24,3072]{3,2,1,0:T(8,128)(2,1)}, bf16[2,8,24,3072]{3,2,1,0:T(8,128)(2,1)S(1)}, u32[]{:S(2)}, u32[]{:S(2)}) collective-permute-start(bf16[2,8,24,3072]{3,2,1,0:T(8,128)(2,1)} %bitcast.49), channel_id=1, source_target_pairs={{0,1},{1,0},{2,3},{3,2},{4,5},{5,4},{6,7},{7,6},{8,9},{9,8},{10,11... | collective-permute-start | bytes 7077896 | tf_op jit(solution)/shard_map/ppermute | solution.py:679
  105.4 5.9 %collective-permute-start.2 = (bf16[640,384]{1,0:T(8,128)(2,1)S(1)}, bf16[640,384]{1,0:T(8,128)(2,1)S(1)}, u32[]{:S(2)}, u32[]{:S(2)}) collective-permute-start(bf16[640,384]{1,0:T(8,128)(2,1)S(1)} %copy-done.13), channel_id=1, source_target_pairs={{0,1},{1,0},{2,3},{3,2},{4,5},{5,4},{6,7},{7,6},{8,9},{9,8},{10,11... | collective-permute-start | bytes 1474568 | tf_op jit(solution)/shard_map/ppermute | solution.py:679
  108.5 37.9 %collective-permute-start.13 = (bf16[2,4,24,768]{3,2,1,0:T(8,128)(2,1)S(1)}, bf16[2,4,24,768]{3,2,1,0:T(8,128)(2,1)S(1)}, u32[]{:S(2)}, u32[]{:S(2)}) collective-permute-start(bf16[2,4,24,768]{3,2,1,0:T(8,128)(2,1)S(1)} %slice_bitcast_fusion.12), channel_id=1, source_target_pairs={{0,4},{4,0},{8,12},{12,8},{16,20},{20,16},{24,28},{28,24},{1,5},{5... | collective-permute-start | bytes 884744 | tf_op jit(solution)/shard_map/ppermute | solution.py:684
  111.3 0.8 copy-start.14
  112.1 26.5 %copy-start.11 = (bf16[768]{0:T(1024)(128)(2,1)S(1)}, bf16[768]{0:T(1024)(128)(2,1)}, u32[]{:S(2)}) copy-start(bf16[768]{0:T(1024)(128)(2,1)} %param.32) | copy-start | bytes 4612
  112.1 27.2 %copy-start.5 = (f32[4,768]{1,0:T(4,128)S(1)}, f32[4,768]{1,0:T(4,128)}, u32[]{:S(2)}) copy-start(f32[4,768]{1,0:T(4,128)} %get-tuple-element.62) | copy-start | bytes 36868
  138.1 28.0 %collective-permute-start.3 = (bf16[3,640,384]{2,1,0:T(8,128)(2,1)}, bf16[3,640,384]{2,1,0:T(8,128)(2,1)}, u32[]{:S(2)}, u32[]{:S(2)}) collective-permute-start(bf16[3,640,384]{2,1,0:T(8,128)(2,1)} %get-tuple-element.57), channel_id=1, source_target_pairs={{0,1},{1,0},{2,3},{3,2},{4,5},{5,4},{6,7},{7,6},{8,9},{9,8},{10,11... | collective-permute-start | bytes 4423688 | tf_op jit(solution)/shard_map/ppermute | solution.py:679
  139.2 67.0 %collective-permute-start.18 = (bf16[2,8,96,768]{3,2,1,0:T(8,128)(2,1)}, bf16[2,8,96,768]{3,2,1,0:T(8,128)(2,1)}, u32[]{:S(2)}, u32[]{:S(2)}) collective-permute-start(bf16[2,8,96,768]{3,2,1,0:T(8,128)(2,1)} %get-tuple-element.70), channel_id=1, source_target_pairs={{0,1},{1,0},{2,3},{3,2},{4,5},{5,4},{6,7},{7,6},{8,9},{9,8},{10,11... | collective-permute-start | bytes 7077896 | tf_op jit(solution)/shard_map/ppermute | solution.py:679
  146.4 9.1 %collective-permute-start.14 = (bf16[4,24,768]{2,1,0:T(8,128)(2,1)S(1)}, bf16[4,24,768]{2,1,0:T(8,128)(2,1)S(1)}, u32[]{:S(2)}, u32[]{:S(2)}) collective-permute-start(bf16[4,24,768]{2,1,0:T(8,128)(2,1)S(1)} %slice_bitcast_fusion.26), channel_id=1, source_target_pairs={{0,2},{1,3},{2,0},{3,1},{4,6},{5,7},{6,4},{7,5},{8,10},{9,11},{10,... | collective-permute-start | bytes 442376 | tf_op jit(solution)/shard_map/ppermute | solution.py:679
  155.6 20.2 %copy-start.2 = (bf16[4,24,768]{2,1,0:T(8,128)(2,1)}, bf16[4,24,768]{2,1,0:T(8,128)(2,1)S(1)}, u32[]{:S(2)}) copy-start(bf16[4,24,768]{2,1,0:T(8,128)(2,1)S(1)} %fusion.18) | copy-start | bytes 442372
  156.3 45.1 %collective-permute-start.15 = (bf16[24,768]{1,0:T(8,128)(2,1)}, bf16[24,768]{1,0:T(8,128)(2,1)}, u32[]{:S(2)}, u32[]{:S(2)}) collective-permute-start(bf16[24,768]{1,0:T(8,128)(2,1)} %get-tuple-element.89), channel_id=1, source_target_pairs={{0,8},{4,12},{8,0},{12,4},{16,24},{20,28},{24,16},{28,20},{1,9},{5... | collective-permute-start | bytes 110600 | tf_op jit(solution)/shard_map/ppermute | solution.py:684
  162.1 39.2 %collective-permute-start.16 = (bf16[24,768]{1,0:T(8,128)(2,1)}, bf16[24,768]{1,0:T(8,128)(2,1)}, u32[]{:S(2)}, u32[]{:S(2)}) collective-permute-start(bf16[24,768]{1,0:T(8,128)(2,1)} %get-tuple-element.91), channel_id=1, source_target_pairs={{0,16},{4,20},{8,24},{12,28},{16,0},{20,4},{24,8},{28,12},{1,17},{... | collective-permute-start | bytes 110600 | tf_op jit(solution)/shard_map/ppermute | solution.py:684
  166.2 35.2 %collective-permute-start.17 = (bf16[24,768]{1,0:T(8,128)(2,1)}, bf16[24,768]{1,0:T(8,128)(2,1)}, u32[]{:S(2)}, u32[]{:S(2)}) collective-permute-start(bf16[24,768]{1,0:T(8,128)(2,1)} %get-tuple-element.90), channel_id=1, source_target_pairs={{0,24},{4,28},{8,16},{12,20},{16,8},{20,12},{24,0},{28,4},{1,25},{... | collective-permute-start | bytes 110600 | tf_op jit(solution)/shard_map/ppermute | solution.py:684
  175.8 11.5 %copy-start.6 = (f32[3,768]{1,0:T(4,128)S(1)}, f32[3,768]{1,0:T(4,128)}, u32[]{:S(2)}) copy-start(f32[3,768]{1,0:T(4,128)} %get-tuple-element.61) | copy-start | bytes 27652
  175.9 12.8 %copy-start.4 = (f32[32,96]{1,0:T(8,128)S(1)}, f32[32,96]{1,0:T(8,128)}, u32[]{:S(2)}) copy-start(f32[32,96]{1,0:T(8,128)} %reshape_transpose_reshape.3) | copy-start | bytes 36868
  189.5 13.4 %all-to-all-start = ((f32[32,1,432]{2,1,0:T(1,128)}), f32[32,1,432]{2,1,0:T(1,128)}, u32[]{:S(2)}, u32[]{:S(2)}) async-start(f32[32,1,432]{2,1,0:T(1,128)} %copy.60), calls=%async_computation | async-start | bytes 131072 | tf_op jit(solution)/shard_map/all_to_all | solution.py:732
  193.8 1.4 copy-start
  199.7 28.3 %collective-permute-start.25 = (bf16[8,24,3072]{2,1,0:T(8,128)(2,1)}, bf16[8,24,3072]{2,1,0:T(8,128)(2,1)S(1)}, u32[]{:S(2)}, u32[]{:S(2)}) collective-permute-start(bf16[8,24,3072]{2,1,0:T(8,128)(2,1)} %slice_bitcast_fusion), channel_id=1, source_target_pairs={{0,2},{1,3},{2,0},{3,1},{4,6},{5,7},{6,4},{7,5},{8,10},{9,11},{10,... | collective-permute-start | bytes 3538952 | tf_op jit(solution)/shard_map/ppermute | solution.py:679
  202.8 36.2 %collective-permute-start.4 = (bf16[2,8,72,768]{3,2,1,0:T(8,128)(2,1)}, bf16[2,8,72,768]{3,2,1,0:T(8,128)(2,1)}, u32[]{:S(2)}, u32[]{:S(2)}) collective-permute-start(bf16[2,8,72,768]{3,2,1,0:T(8,128)(2,1)} %get-tuple-element.65), channel_id=1, source_target_pairs={{0,1},{1,0},{2,3},{3,2},{4,5},{5,4},{6,7},{7,6},{8,9},{9,8},{10,11... | collective-permute-start | bytes 5308424 | tf_op jit(solution)/shard_map/ppermute | solution.py:679
  209.3 28.9 %collective-permute-start.19 = (bf16[2,4,96,768]{3,2,1,0:T(8,128)(2,1)S(1)}, bf16[2,4,96,768]{3,2,1,0:T(8,128)(2,1)S(1)}, u32[]{:S(2)}, u32[]{:S(2)}) collective-permute-start(bf16[2,4,96,768]{3,2,1,0:T(8,128)(2,1)S(1)} %slice_bitcast_fusion.2), channel_id=1, source_target_pairs={{0,4},{4,0},{8,12},{12,8},{16,20},{20,16},{24,28},{28,24},{1,5},{5... | collective-permute-start | bytes 3538952 | tf_op jit(solution)/shard_map/ppermute | solution.py:684
  228.4 10.6 %copy-start.1 = (bf16[2,8,72,768]{3,2,1,0:T(8,128)(2,1)S(1)}, bf16[2,8,72,768]{3,2,1,0:T(8,128)(2,1)}, u32[]{:S(2)}) copy-start(bf16[2,8,72,768]{3,2,1,0:T(8,128)(2,1)} %get-tuple-element.64) | copy-start | bytes 5308420
  228.4 22.5 %collective-permute-start.26 = (bf16[4,24,3072]{2,1,0:T(8,128)(2,1)S(1)}, bf16[4,24,3072]{2,1,0:T(8,128)(2,1)S(1)}, u32[]{:S(2)}, u32[]{:S(2)}) collective-permute-start(bf16[4,24,3072]{2,1,0:T(8,128)(2,1)S(1)} %slice_bitcast_fusion.4), channel_id=1, source_target_pairs={{0,4},{4,0},{8,12},{12,8},{16,20},{20,16},{24,28},{28,24},{1,5},{5... | collective-permute-start | bytes 1769480 | tf_op jit(solution)/shard_map/ppermute | solution.py:684
  238.6 16.4 %collective-permute-start.20 = (bf16[4,96,768]{2,1,0:T(8,128)(2,1)S(1)}, bf16[4,96,768]{2,1,0:T(8,128)(2,1)S(1)}, u32[]{:S(2)}, u32[]{:S(2)}) collective-permute-start(bf16[4,96,768]{2,1,0:T(8,128)(2,1)S(1)} %slice_bitcast_fusion.6), channel_id=1, source_target_pairs={{0,2},{1,3},{2,0},{3,1},{4,6},{5,7},{6,4},{7,5},{8,10},{9,11},{10,... | collective-permute-start | bytes 1769480 | tf_op jit(solution)/shard_map/ppermute | solution.py:679
  241.1 18.8 %collective-permute-start.7 = (bf16[2,4,72,384]{3,2,1,0:T(8,128)(2,1)S(1)}, bf16[2,4,72,384]{3,2,1,0:T(8,128)(2,1)S(1)}, u32[]{:S(2)}, u32[]{:S(2)}) collective-permute-start(bf16[2,4,72,384]{3,2,1,0:T(8,128)(2,1)S(1)} %slice_bitcast_fusion.8), channel_id=1, source_target_pairs={{0,4},{4,0},{8,12},{12,8},{16,20},{20,16},{24,28},{28,24},{1,5},{5... | collective-permute-start | bytes 1327112 | tf_op jit(solution)/shard_map/ppermute | solution.py:684
  242.9 19.7 %collective-permute-start.5 = (bf16[8,72,384]{2,1,0:T(8,128)(2,1)S(1)}, bf16[8,72,384]{2,1,0:T(8,128)(2,1)S(1)}, u32[]{:S(2)}, u32[]{:S(2)}) collective-permute-start(bf16[8,72,384]{2,1,0:T(8,128)(2,1)S(1)} %slice_bitcast_fusion.10), channel_id=1, source_target_pairs={{0,2},{1,3},{2,0},{3,1},{4,6},{5,7},{6,4},{7,5},{8,10},{9,11},{10,... | collective-permute-start | bytes 1327112 | tf_op jit(solution)/shard_map/ppermute | solution.py:679
  251.1 14.0 %collective-permute-start.27 = (bf16[24,3072]{1,0:T(8,128)(2,1)S(1)}, bf16[24,3072]{1,0:T(8,128)(2,1)S(1)}, u32[]{:S(2)}, u32[]{:S(2)}) collective-permute-start(bf16[24,3072]{1,0:T(8,128)(2,1)S(1)} %get-tuple-element.80), channel_id=1, source_target_pairs={{0,8},{4,12},{8,0},{12,4},{16,24},{20,28},{24,16},{28,20},{1,9},{5... | collective-permute-start | bytes 442376 | tf_op jit(solution)/shard_map/ppermute | solution.py:684
  252.6 14.0 %collective-permute-start.28 = (bf16[24,3072]{1,0:T(8,128)(2,1)S(1)}, bf16[24,3072]{1,0:T(8,128)(2,1)S(1)}, u32[]{:S(2)}, u32[]{:S(2)}) collective-permute-start(bf16[24,3072]{1,0:T(8,128)(2,1)S(1)} %get-tuple-element.82), channel_id=1, source_target_pairs={{0,16},{4,20},{8,24},{12,28},{16,0},{20,4},{24,8},{28,12},{1,17},{... | collective-permute-start | bytes 442376 | tf_op jit(solution)/shard_map/ppermute | solution.py:684
  255.0 12.2 %collective-permute-start.29 = (bf16[24,3072]{1,0:T(8,128)(2,1)S(1)}, bf16[24,3072]{1,0:T(8,128)(2,1)S(1)}, u32[]{:S(2)}, u32[]{:S(2)}) collective-permute-start(bf16[24,3072]{1,0:T(8,128)(2,1)S(1)} %get-tuple-element.81), channel_id=1, source_target_pairs={{0,24},{4,28},{8,16},{12,20},{16,8},{20,12},{24,0},{28,4},{1,25},{... | collective-permute-start | bytes 442376 | tf_op jit(solution)/shard_map/ppermute | solution.py:684
  259.9 25.9 %collective-permute-start.21 = (bf16[96,768]{1,0:T(8,128)(2,1)S(1)}, bf16[96,768]{1,0:T(8,128)(2,1)S(1)}, u32[]{:S(2)}, u32[]{:S(2)}) collective-permute-start(bf16[96,768]{1,0:T(8,128)(2,1)S(1)} %get-tuple-element.83), channel_id=1, source_target_pairs={{0,8},{4,12},{8,0},{12,4},{16,24},{20,28},{24,16},{28,20},{1,9},{5... | collective-permute-start | bytes 442376 | tf_op jit(solution)/shard_map/ppermute | solution.py:684
  262.6 23.2 %collective-permute-start.22 = (bf16[96,768]{1,0:T(8,128)(2,1)S(1)}, bf16[96,768]{1,0:T(8,128)(2,1)S(1)}, u32[]{:S(2)}, u32[]{:S(2)}) collective-permute-start(bf16[96,768]{1,0:T(8,128)(2,1)S(1)} %get-tuple-element.85), channel_id=1, source_target_pairs={{0,16},{4,20},{8,24},{12,28},{16,0},{20,4},{24,8},{28,12},{1,17},{... | collective-permute-start | bytes 442376 | tf_op jit(solution)/shard_map/ppermute | solution.py:684
  265.1 20.7 %collective-permute-start.23 = (bf16[96,768]{1,0:T(8,128)(2,1)S(1)}, bf16[96,768]{1,0:T(8,128)(2,1)S(1)}, u32[]{:S(2)}, u32[]{:S(2)}) collective-permute-start(bf16[96,768]{1,0:T(8,128)(2,1)S(1)} %get-tuple-element.84), channel_id=1, source_target_pairs={{0,24},{4,28},{8,16},{12,20},{16,8},{20,12},{24,0},{28,4},{1,25},{... | collective-permute-start | bytes 442376 | tf_op jit(solution)/shard_map/ppermute | solution.py:684
  266.6 5.9 %collective-permute-start.8 = (bf16[4,72,384]{2,1,0:T(8,128)(2,1)S(1)}, bf16[4,72,384]{2,1,0:T(8,128)(2,1)S(1)}, u32[]{:S(2)}, u32[]{:S(2)}) collective-permute-start(bf16[4,72,384]{2,1,0:T(8,128)(2,1)S(1)} %slice_bitcast_fusion.14), channel_id=1, source_target_pairs={{0,2},{1,3},{2,0},{3,1},{4,6},{5,7},{6,4},{7,5},{8,10},{9,11},{10,... | collective-permute-start | bytes 663560 | tf_op jit(solution)/shard_map/ppermute | solution.py:679
  267.2 5.9 %collective-permute-start.6 = (bf16[4,72,384]{2,1,0:T(8,128)(2,1)S(1)}, bf16[4,72,384]{2,1,0:T(8,128)(2,1)S(1)}, u32[]{:S(2)}, u32[]{:S(2)}) collective-permute-start(bf16[4,72,384]{2,1,0:T(8,128)(2,1)S(1)} %slice_bitcast_fusion.16), channel_id=1, source_target_pairs={{0,4},{4,0},{8,12},{12,8},{16,20},{20,16},{24,28},{28,24},{1,5},{5... | collective-permute-start | bytes 663560 | tf_op jit(solution)/shard_map/ppermute | solution.py:684
  273.2 13.3 %collective-permute-start.10 = (bf16[72,768]{1,0:T(8,128)(2,1)S(1)}, bf16[72,768]{1,0:T(8,128)(2,1)S(1)}, u32[]{:S(2)}, u32[]{:S(2)}) collective-permute-start(bf16[72,768]{1,0:T(8,128)(2,1)S(1)} %get-tuple-element.88), channel_id=1, source_target_pairs={{0,16},{4,20},{8,24},{12,28},{16,0},{20,4},{24,8},{28,12},{1,17},{... | collective-permute-start | bytes 331784 | tf_op jit(solution)/shard_map/ppermute | solution.py:684
  283.1 6.8 %collective-permute-start.11 = (bf16[72,768]{1,0:T(8,128)(2,1)S(1)}, bf16[72,768]{1,0:T(8,128)(2,1)S(1)}, u32[]{:S(2)}, u32[]{:S(2)}) collective-permute-start(bf16[72,768]{1,0:T(8,128)(2,1)S(1)} %get-tuple-element.87), channel_id=1, source_target_pairs={{0,24},{4,28},{8,16},{12,20},{16,8},{20,12},{24,0},{28,4},{1,25},{... | collective-permute-start | bytes 331784 | tf_op jit(solution)/shard_map/ppermute | solution.py:684
  285.8 5.2 %collective-permute-start.9 = (bf16[72,768]{1,0:T(8,128)(2,1)S(1)}, bf16[72,768]{1,0:T(8,128)(2,1)S(1)}, u32[]{:S(2)}, u32[]{:S(2)}) collective-permute-start(bf16[72,768]{1,0:T(8,128)(2,1)S(1)} %get-tuple-element.86), channel_id=1, source_target_pairs={{0,8},{4,12},{8,0},{12,4},{16,24},{20,28},{24,16},{28,20},{1,9},{5... | collective-permute-start | bytes 331784 | tf_op jit(solution)/shard_map/ppermute | solution.py:684

commit v2 on v1

v2 whole, which is shorter than its diff:
```python
import jax
import jax.numpy as jnp
from jax import lax
from jax.experimental import pallas as pl
from jax.experimental.pallas import tpu as pltpu
from jax.sharding import PartitionSpec as P

HEAD_DIM = 64
SEQ_LEN = 1280
PAIR = 2 * HEAD_DIM
BQ = 256
BK = 128
BLOCKS = 8
SUB = 256
NEG = -1e30
F32 = jnp.float32
BF16 = jnp.bfloat16
VMEM_LIMIT = 56 * 1024 * 1024


def dot(left, right):
    return lax.dot_general(left, right, (((1,), (0,)), ((), ())), preferred_element_type=F32)


def dot_nt(left, right):
    return lax.dot_general(left, right, (((1,), (1,)), ((), ())), preferred_element_type=F32)


def center_and_scale(values):
    center = values - jnp.mean(values, -1, keepdims=True)
    spread = jnp.mean(center * center, -1, keepdims=True)
    scale = lax.rsqrt(spread + 1e-05)
    return center * scale, scale


def dot_tn(left, right):
    return lax.dot_general(left, right, (((0,), (0,)), ((), ())), preferred_element_type=F32)


def pass_rows(ids_ref, passes):
    ids = ids_ref[...]
    row = lax.broadcasted_iota(jnp.int32, (passes, ids.shape[1]), 0)
    return (row == ids).astype(F32).astype(BF16)


def embed_tokens(tok_ref, ids_ref, emb_ref):
    return tok_ref[...].astype(F32) + dot_tn(pass_rows(ids_ref, emb_ref.shape[0]), emb_ref[...])


def wide(item):
    return item[...].astype(F32)


def half_lanes(core, half):
    return pl.ds(pl.multiple_of(core * half, 128), half)


def whole(shape):
    return pl.BlockSpec(shape, lambda *_: (0,) * len(shape))


def carry(operands, outs, carried):
    return {1 + operands + at: outs + at for at in range(len(carried))}


def shapes(items):
    return [jax.ShapeDtypeStruct(item.shape, item.dtype) for item in items]


def params():
    return pltpu.CompilerParams(vmem_limit_bytes=VMEM_LIMIT)


def cost():
    return pl.CostEstimate(flops=1000, transcendentals=0, bytes_accessed=1000)


ANY = pl.BlockSpec(memory_space=pl.ANY)


def third_bias(bias):
    third = pl.program_id(0)
    rows = bias[...].astype(F32)
    return jnp.where(third == 0, rows[0:1], jnp.where(third == 2, rows[1:2], 0.0))


def qkv_send_kernel(pos, tok, ids, emb, gain, shift, weight, bias, normed_out, half_out, out):
    @pl.when(pl.program_id(0) == 0)
    def _():
        scaled, _ = center_and_scale(embed_tokens(tok, ids, emb))
        normed_out[...] = (scaled * wide(gain) + wide(shift)).astype(BF16)
        half_out[...] = normed_out[:, half_lanes(1 - pos[0], half_out.shape[1])]

    out[0] = (dot(normed_out[...], weight[...]) + third_bias(bias)).astype(BF16)


def qkv_keep_kernel(pos, normed, weight, bias, out):
    out[0] = (dot(normed[...], weight[...]) + third_bias(bias)).astype(BF16)


def qkv_send(pos, tok, ids, emb, gain, shift, weight, bias):
    rows, width = tok.shape
    half = width // 2
    return pl.pallas_call(
        qkv_send_kernel,
        grid_spec=pltpu.PrefetchScalarGridSpec(
            num_scalar_prefetch=1,
            grid=(3,),
            in_specs=[
                whole(tok.shape),
                whole(ids.shape),
                whole(emb.shape),
                whole(gain.shape),
                whole(shift.shape),
                pl.BlockSpec((width, half), lambda t, s: (0, 2 * t + 1 - s[0])),
                pl.BlockSpec((2, half), lambda t, s: (0, 1 - s[0])),
            ],
            out_specs=[
                whole(tok.shape),
                whole((rows, half)),
                pl.BlockSpec((1, rows, half), lambda t, s: (t, 0, 0)),
            ],
        ),
        out_shape=[
            jax.ShapeDtypeStruct(tok.shape, BF16),
            jax.ShapeDtypeStruct((rows, half), BF16),
            jax.ShapeDtypeStruct((3, rows, half), BF16),
        ],
        compiler_params=params(),
        cost_estimate=cost(),
        name="qkv_send",
    )(pos, tok, ids, emb, gain, shift, weight, bias)


def qkv_keep(pos, normed, weight, bias):
    rows, width = normed.shape
    half = width // 2
    return pl.pallas_call(
        qkv_keep_kernel,
        grid_spec=pltpu.PrefetchScalarGridSpec(
            num_scalar_prefetch=1,
            grid=(3,),
            in_specs=[
                whole(normed.shape),
                pl.BlockSpec((width, half), lambda t, s: (0, 2 * t + s[0])),
                pl.BlockSpec((2, half), lambda t, s: (0, s[0])),
            ],
            out_specs=pl.BlockSpec((1, rows, half), lambda t, s: (t, 0, 0)),
        ),
        out_shape=jax.ShapeDtypeStruct((3, rows, half), BF16),
        compiler_params=params(),
        cost_estimate=cost(),
        name="qkv_keep",
    )(pos, normed, weight, bias)


def lane_masks():
    lane = lax.broadcasted_iota(jnp.int32, (1, PAIR), 1)
    first = (lane < HEAD_DIM).astype(F32).astype(BF16)
    return first, (1 - first).astype(BF16)


def row_split(values):
    row = lax.broadcasted_iota(jnp.int32, values.shape, 0)
    keep = row < HEAD_DIM
    wide = values.astype(F32)
    return jnp.concatenate(
        [jnp.where(keep, wide, 0.0).astype(BF16), jnp.where(keep, 0.0, wide).astype(BF16)], axis=1
    )


def gather_rows(mine, other, target, sems, core, rows):
    own = pl.ds(pl.multiple_of(core * rows, 128), rows)
    far = pl.ds(pl.multiple_of((1 - core) * rows, 128), rows)
    if len(mine.shape) == 3:
        return (
            pltpu.make_async_copy(mine, target.at[:, own, :], sems.at[0]),
            pltpu.make_async_copy(other, target.at[:, far, :], sems.at[1]),
        )
    return (
        pltpu.make_async_copy(mine, target.at[own, :], sems.at[0]),
        pltpu.make_async_copy(other, target.at[far, :], sems.at[1]),
    )


def segment_firsts(seg_ref, x):
    row = seg_ref[pl.ds(x, 1), :]
    return [jnp.sum((row < number).astype(F32)).astype(jnp.int32) for number in (1, 2, 3)]


def fill_starts(firsts, start):
    at = lax.broadcasted_iota(jnp.int32, start.shape, 1)
    own = jnp.zeros(start.shape, jnp.int32)
    for first in firsts:
        own = jnp.where(at >= first, first, own)
    start[...] = own


def first_block(firsts, q0):
    own = jnp.int32(0)
    for first in firsts:
        own = jnp.where(first <= q0, first, own)
    return own // BK


def valid_keys(start, q0, kb):
    key_at = lax.broadcasted_iota(jnp.int32, (BK, BQ), 0) + kb * BK
    query_at = lax.broadcasted_iota(jnp.int32, (BK, BQ), 1) + q0
    inside = (key_at >= start) & (key_at <= query_at)
    return jnp.concatenate([inside, inside], axis=1)


def attend_kernel(pos, seg, keep, recv, own_out, far_out, lse_out, qkv, qq, vm, sc, acc, joined, start_ref, sems):
    core = pos[0]
    rows = own_out.shape[0]
    pairs = own_out.shape[1] // PAIR
    copies = gather_rows(keep, recv, qkv, sems, core, rows)
    for item in copies:
        item.start()
    firsts = segment_firsts(seg, pos[4])
    fill_starts(firsts, start_ref)
    for item in copies:
        item.wait()
    first, second = lane_masks()

    def prepare(kb, _):
        at = pl.ds(pl.multiple_of(kb * BK, BK), BK)
        for p in range(pairs):
            vm[kb, p] = row_split(qkv[2, at, p * PAIR : (p + 1) * PAIR].T)
        return 0

    lax.fori_loop(0, SEQ_LEN // BK, prepare, 0)

    def one_block(qi, _):
        q0 = pl.multiple_of(qi * BQ, BQ)
        at = pl.ds(q0, BQ)
        start = start_ref[:, at]
        low = first_block(firsts, q0)
        high = (qi + 1) * (BQ // BK)
        for p in range(pairs):
            q = qkv[0, at, p * PAIR : (p + 1) * PAIR] * jnp.asarray(0.125, BF16)
            qq[p, :BQ] = q * first
            qq[p, BQ:] = q * second
            acc[p] = jnp.zeros((PAIR, BQ), F32)

        def scores(kb, tops):
            inside = valid_keys(start, q0, kb)
            rows_at = pl.ds(pl.multiple_of(kb * BK, BK), BK)
            grown = []
            for p in range(pairs):
                s = dot_nt(qkv[1, rows_at, p * PAIR : (p + 1) * PAIR], qq[p])
                s = jnp.where(inside, s, NEG)
                sc[kb - low, p] = s
                grown.append(jnp.maximum(tops[p], jnp.max(s, axis=0, keepdims=True)))
            return tuple(grown)

        tops = lax.fori_loop(
            low, high, scores, tuple(jnp.full((1, 2 * BQ), NEG, F32) for _ in range(pairs))
        )

        def weigh(kb, sums):
            grown = []
            for p in range(pairs):
                raw = jnp.exp(sc[kb - low, p] - tops[p])
                grown.append(sums[p] + jnp.sum(raw, axis=0, keepdims=True))
                raw = raw.astype(BF16)
                acc[p] += dot(vm[kb, p], jnp.concatenate([raw[:, :BQ], raw[:, BQ:]], axis=0))
            return tuple(grown)

        sums = lax.fori_loop(
            low, high, weigh, tuple(jnp.zeros((1, 2 * BQ), F32) for _ in range(pairs))
        )
        for p in range(pairs):
            inv = 1.0 / sums[p]
            out = jnp.concatenate(
                [acc[p, :HEAD_DIM] * inv[:, :BQ], acc[p, HEAD_DIM:] * inv[:, BQ:]], axis=0
            )
            joined[at, p * PAIR : (p + 1) * PAIR] = out.T.astype(BF16)
            lse_out[qi, p] = tops[p] + jnp.log(sums[p])
        return 0

    lax.fori_loop(0, SEQ_LEN // BQ, one_block, 0)
    own_out[...] = joined[pl.ds(pl.multiple_of(core * rows, 128), rows), :]
    far_out[...] = joined[pl.ds(pl.multiple_of((1 - core) * rows, 128), rows), :]


def attend(pos, seg, keep, recv):
    _, rows, half = keep.shape
    pairs = half // PAIR
    window = SEQ_LEN // BK
    return pl.pallas_call(
        attend_kernel,
        grid_spec=pltpu.PrefetchScalarGridSpec(
            num_scalar_prefetch=1,
            grid=(1,),
            in_specs=[whole(seg.shape), ANY, ANY],
            out_specs=[
                whole((rows, half)),
                whole((rows, half)),
                whole((SEQ_LEN // BQ, pairs, 1, 2 * BQ)),
            ],
            scratch_shapes=[
                pltpu.VMEM((3, SEQ_LEN, half), BF16),
                pltpu.VMEM((pairs, 2 * BQ, PAIR), BF16),
                pltpu.VMEM((SEQ_LEN // BK, pairs, PAIR, 2 * BK), BF16),
                pltpu.VMEM((window, pairs, BK, 2 * BQ), F32),
                pltpu.VMEM((pairs, PAIR, BQ), F32),
                pltpu.VMEM((SEQ_LEN, half), BF16),
                pltpu.VMEM((1, SEQ_LEN), jnp.int32),
                pltpu.SemaphoreType.DMA((2,)),
            ],
        ),
        out_shape=[
            jax.ShapeDtypeStruct((rows, half), BF16),
            jax.ShapeDtypeStruct((rows, half), BF16),
            jax.ShapeDtypeStruct((SEQ_LEN // BQ, pairs, 1, 2 * BQ), F32),
        ],
        compiler_params=params(),
        cost_estimate=cost(),
        name="attend",
    )(pos, seg, keep, recv)


def attend_back_kernel(
    pos, seg, lse_ref, keep, recv, own, far, grad_own, grad_far, *rest, ties
):
    keep_out, send_out, qkv, att, dout, qq, dd, km, delta, dq_t, dq, dk, dv, start_ref, sems = rest[ties:]
    core = pos[0]
    rows, half = own.shape
    pairs = half // PAIR
    copies = (
        gather_rows(keep, recv, qkv, sems.at[0], core, rows)
        + gather_rows(own, far, att, sems.at[1], core, rows)
        + gather_rows(grad_own, grad_far, dout, sems.at[2], core, rows)
    )
    for item in copies:
        item.start()
    firsts = segment_firsts(seg, pos[4])
    fill_starts(firsts, start_ref)
    dk[...] = jnp.zeros_like(dk)
    dv[...] = jnp.zeros_like(dv)
    for item in copies:
        item.wait()
    first, second = lane_masks()

    def prepare(kb, _):
        at = pl.ds(pl.multiple_of(kb * BK, BK), BK)
        for p in range(pairs):
            km[kb, p] = row_split(qkv[1, at, p * PAIR : (p + 1) * PAIR].T)
        return 0

    lax.fori_loop(0, SEQ_LEN // BK, prepare, 0)

    def one_block(qi, _):
        q0 = pl.multiple_of(qi * BQ, BQ)
        at = pl.ds(q0, BQ)
        start = start_ref[:, at]
        low = first_block(firsts, q0)
        high = (qi + 1) * (BQ // BK)
        for p in range(pairs):
            lanes = slice(p * PAIR, (p + 1) * PAIR)
            q = qkv[0, at, lanes] * jnp.asarray(0.125, BF16)
            qq[p, :BQ] = q * first
            qq[p, BQ:] = q * second
            g = dout[at, lanes]
            dd[p, :BQ] = g * first
            dd[p, BQ:] = g * second
            both = (g.astype(F32) * att[at, lanes].astype(F32)).T
            delta[p] = jnp.concatenate(
                [
                    jnp.sum(both[:HEAD_DIM], axis=0, keepdims=True),
                    jnp.sum(both[HEAD_DIM:], axis=0, keepdims=True),
                ],
                axis=1,
            )
            dq_t[p] = jnp.zeros((PAIR, BQ), F32)

        def step(kb, _):
            inside = valid_keys(start, q0, kb)
            rows_at = pl.ds(pl.multiple_of(kb * BK, BK), BK)
            for p in range(pairs):
                lanes = slice(p * PAIR, (p + 1) * PAIR)
                s = dot_nt(qkv[1, rows_at, lanes], qq[p])
                prob = jnp.where(inside, jnp.exp(s - lse_ref[qi, p]), 0.0)
                grad_prob = dot_nt(qkv[2, rows_at, lanes], dd[p])
                grad_s = (prob * (grad_prob - delta[p])).astype(BF16)
                dv[rows_at, lanes] += dot(prob.astype(BF16), dd[p])
                dk[rows_at, lanes] += dot(grad_s, qq[p])
                dq_t[p] += dot(km[kb, p], jnp.concatenate([grad_s[:, :BQ], grad_s[:, BQ:]], axis=0))
            return 0

        lax.fori_loop(low, high, step, 0)
        for p in range(pairs):
            dq[p * PAIR : (p + 1) * PAIR, at] = (dq_t[p] * 0.125).astype(BF16)
        return 0

    lax.fori_loop(0, SEQ_LEN // BQ, one_block, 0)
    for target, at in ((keep_out, core), (send_out, 1 - core)):
        tokens = pl.ds(pl.multiple_of(at * rows, 128), rows)
        target[0] = dq[:, tokens]
        target[1] = dk[tokens, :].astype(BF16).T
        target[2] = dv[tokens, :].astype(BF16).T


def attend_back(ties, pos, seg, lse, keep, recv, own, far, grad_own, grad_far):
    _, rows, half = keep.shape
    pairs = half // PAIR
    out = (3, half, rows)

    def kernel(*refs):
        attend_back_kernel(*refs, ties=len(ties))

    return pl.pallas_call(
        kernel,
        grid_spec=pltpu.PrefetchScalarGridSpec(
            num_scalar_prefetch=1,
            grid=(1,),
            in_specs=[whole(seg.shape), whole(lse.shape)] + [ANY] * (6 + len(ties)),
            out_specs=[whole(out), whole(out)],
            scratch_shapes=[
                pltpu.VMEM((3, SEQ_LEN, half), BF16),
                pltpu.VMEM((SEQ_LEN, half), BF16),
                pltpu.VMEM((SEQ_LEN, half), BF16),
                pltpu.VMEM((pairs, 2 * BQ, PAIR), BF16),
                pltpu.VMEM((pairs, 2 * BQ, PAIR), BF16),
                pltpu.VMEM((SEQ_LEN // BK, pairs, PAIR, 2 * BK), BF16),
                pltpu.VMEM((pairs, 1, 2 * BQ), F32),
                pltpu.VMEM((pairs, PAIR, BQ), F32),
                pltpu.VMEM((half, SEQ_LEN), BF16),
                pltpu.VMEM((SEQ_LEN, half), F32),
                pltpu.VMEM((SEQ_LEN, half), F32),
                pltpu.VMEM((1, SEQ_LEN), jnp.int32),
                pltpu.SemaphoreType.DMA((3, 2)),
            ],
        ),
        out_shape=[jax.ShapeDtypeStruct(out, BF16)] * 2,
        compiler_params=params(),
        cost_estimate=cost(),
        name="attend_back",
    )(pos, seg, lse, keep, recv, own, far, grad_own, grad_far, *ties)


def gather_lanes(core, own, far, target):
    half = own.shape[1]
    target[:, half_lanes(core, half)] = own[...]
    target[:, half_lanes(1 - core, half)] = far[...]


def hidden_block(i, core):
    late = i >> 1
    return 2 * (late * core + (1 - late) * (1 - core)) + (i & 1)


def early(i):
    return jnp.minimum(i, 1)


def late(i):
    return jnp.maximum(i - 2, 0)


def ff_first_kernel(
    pos, tok, ids, emb, own, far, weight, bias, gain, shift, cot, up, up_bias, down,
    after_out, normed_out, half_out, act_own, act_send, grad_out, bias_grad, attended, act,
):
    step = pl.program_id(0)

    @pl.when(step == 0)
    def _():
        gather_lanes(pos[0], own, far, attended)
        after = embed_tokens(tok, ids, emb) + dot(attended[...], weight[...]) + wide(bias)
        after_out[...] = after
        scaled, _ = center_and_scale(after)
        normed_out[...] = (scaled * wide(gain) + wide(shift)).astype(BF16)
        half_out[...] = normed_out[:, half_lanes(1 - pos[0], half_out.shape[1])]

    for part in range(up.shape[1] // SUB):
        cols = slice(part * SUB, (part + 1) * SUB)
        u = dot(normed_out[...], up[:, cols]) + up_bias[:, cols].astype(F32)
        grad_act = dot_nt(cot[...], down[cols, :])
        square = u * u
        t = jnp.tanh(0.7978845608028654 * u * (1.0 + 0.044715 * square))
        half = 0.5 * (1.0 + t)
        act[:, cols] = (u * half).astype(BF16)
        slope = half + 0.5 * u * (1.0 - t * t) * (0.7978845608028654 * (1.0 + 0.134145 * square))
        grad = (grad_act * slope).astype(BF16)
        grad_out[:, cols] = grad
        bias_grad[:, cols] = jnp.sum(grad.astype(F32), axis=0, keepdims=True)

    @pl.when(step < 2)
    def _():
        act_send[...] = act[...]

    @pl.when(step >= 2)
    def _():
        act_own[...] = act[...]


def ff_first(pos, tok, ids, emb, own, far, weight, bias, gain, shift, cot, up, up_bias, down):
    rows, width = tok.shape
    hidden = up.shape[1]
    first = (tok, ids, emb, own, far, weight, bias, gain, shift, cot)
    shape = jax.ShapeDtypeStruct
    return pl.pallas_call(
        ff_first_kernel,
        grid_spec=pltpu.PrefetchScalarGridSpec(
            num_scalar_prefetch=1,
            grid=(4,),
            in_specs=[whole(item.shape) for item in first]
            + [
                pl.BlockSpec((width, width), lambda i, s: (0, hidden_block(i, s[0]))),
                pl.BlockSpec((1, width), lambda i, s: (0, hidden_block(i, s[0]))),
                pl.BlockSpec((width, width), lambda i, s: (hidden_block(i, s[0]), 0)),
            ],
            out_specs=[
                whole((rows, width)),
                whole((rows, width)),
                whole((rows, width // 2)),
                pl.BlockSpec((rows, width), lambda i, s: (0, late(i))),
                pl.BlockSpec((rows, width), lambda i, s: (0, early(i))),
                pl.BlockSpec((rows, width), lambda i, s: (0, hidden_block(i, s[0]))),
                pl.BlockSpec((1, width), lambda i, s: (0, hidden_block(i, s[0]))),
            ],
            scratch_shapes=[pltpu.VMEM((rows, width), BF16), pltpu.VMEM((rows, width), BF16)],
        ),
        out_shape=[
            shape((rows, width), F32),
            shape((rows, width), BF16),
            shape((rows, width // 2), BF16),
            shape((rows, hidden // 2), BF16),
            shape((rows, hidden // 2), BF16),
            shape((rows, hidden), BF16),
            shape((1, hidden), F32),
        ],
        compiler_params=params(),
        cost_estimate=cost(),
        name="ff_first",
    )(pos, *first, up, up_bias, down)


def ff_back_kernel(
    pos, grad_pre, up, after, cot, gain, weight,
    grad_after, branch_out, own_out, far_out, sums, total,
):
    step = pl.program_id(0)
    part = dot_nt(grad_pre[...], up[...])

    @pl.when(step == 0)
    def _():
        total[...] = part

    @pl.when(step > 0)
    def _():
        total[...] += part

    @pl.when(step == pl.num_programs(0) - 1)
    def _():
        core = pos[0]
        half = own_out.shape[1]
        scaled, scale = center_and_scale(after[...])
        grad = total[...]
        inner = grad * wide(gain)
        shift = jnp.mean(inner, -1, keepdims=True)
        slope = jnp.mean(inner * scaled, -1, keepdims=True)
        cot_f32 = wide(cot)
        result = cot_f32 + scale * (inner - shift - scaled * slope)
        grad_after[...] = result
        branch_out[...] = result.astype(BF16)
        branch = branch_out[...]
        for target, at in ((far_out, 1 - core), (own_out, core)):
            rows = pl.ds(pl.multiple_of(at * half, 128), half)
            target[...] = dot_nt(branch, weight[rows, :]).astype(BF16)
        sums[0:1] = jnp.sum(grad * scaled, axis=0, keepdims=True)
        sums[1:2] = jnp.sum(grad, axis=0, keepdims=True)
        sums[2:3] = jnp.sum(branch.astype(F32), axis=0, keepdims=True)
        sums[3:4] = jnp.sum(cot_f32, axis=0, keepdims=True)


def ff_back(pos, grad_pre, up, after, cot, gain, weight):
    rows, width = after.shape
    half = width // 2
    last = (after, cot, gain, weight)
    outs = [
        jax.ShapeDtypeStruct((rows, width), F32),
        jax.ShapeDtypeStruct((rows, width), BF16),
        jax.ShapeDtypeStruct((rows, half), BF16),
        jax.ShapeDtypeStruct((rows, half), BF16),
        jax.ShapeDtypeStruct((4, width), F32),
    ]
    return pl.pallas_call(
        ff_back_kernel,
        grid_spec=pltpu.PrefetchScalarGridSpec(
            num_scalar_prefetch=1,
            grid=(grad_pre.shape[1] // width,),
            in_specs=[
                pl.BlockSpec((rows, width), lambda i, s: (0, i)),
                pl.BlockSpec((width, width), lambda i, s: (0, i)),
            ]
            + [whole(item.shape) for item in last],
            out_specs=[whole(item.shape) for item in outs],
            scratch_shapes=[pltpu.VMEM((rows, width), F32)],
        ),
        out_shape=outs,
        compiler_params=params(),
        cost_estimate=cost(),
        name="ff_back",
    )(pos, grad_pre, up, *last)


def z_place(z):
    return (z & 1) * 2 + (z >> 1)


def chips():
    return [(x, y, z) for x in range(2) for y in range(2) for z in range(4)]


def chip_row(pos, x, y, z):
    return ((2 * z_place(z) + y) ^ pos[3]) * 2 + (x ^ pos[2])


def rows_of(values, chip, per, at=0, count=None):
    count = per if count is None else count
    return values[pl.ds(pl.multiple_of(chip * per + at, 8), count), :].astype(BF16)


def middle_weights_kernel(
    pos, act, act_far, grad, grad_far, cot, cot_far, normed, normed_far, *rest, ties
):
    left_keep, left_send, right_keep, right_send, rows_f32 = rest[ties:]
    step = pl.program_id(0)
    half = normed_far.shape[1]
    left, right = (left_keep, left_send), (right_keep, right_send)

    @pl.when(step < 2)
    def _():
        per = rows_f32.shape[0] // 16
        for part in range(2):
            cols = slice(part * half, (part + 1) * half)
            rows_f32[...] = dot_tn(cot[...], act[:, cols]) + dot_tn(cot_far[...], act_far[:, cols])
            for x, y, z in chips():
                left[x][y, z, part * per : (part + 1) * per, :] = rows_of(
                    rows_f32, chip_row(pos, x, y, z), per
                )

    @pl.when(step >= 2)
    def _():
        per = rows_f32.shape[0] // 4
        own = normed[:, half_lanes(pos[0], half)]
        rows_f32[...] = dot_tn(grad[...], own) + dot_tn(grad_far[...], normed_far[...])
        for x in range(2):
            for y in range(2):
                chip = (y ^ (pos[3] & 1)) * 2 + (x ^ pos[2])
                right[y][x, 0, :per, :] = rows_of(rows_f32, chip, per)


def middle_weights(pos, ties, act, act_far, grad, grad_far, cot, cot_far, normed, normed_far):
    rows, width = normed.shape
    half = width // 2
    per = width // 16
    left = jax.ShapeDtypeStruct((2, 4, 4 * per, half), BF16)
    right = jax.ShapeDtypeStruct((2, 4, 5 * per, half), BF16)
    fixed = (cot, cot_far, normed, normed_far)

    def kernel(*refs):
        middle_weights_kernel(*refs, ties=len(ties))

    def left_at(i, s):
        return 0, 0, early(i), 0

    def right_at(i, s):
        return 0, z_place(late(i) ^ (s[3] >> 1)), 0, 0

    return pl.pallas_call(
        kernel,
        grid_spec=pltpu.PrefetchScalarGridSpec(
            num_scalar_prefetch=1,
            grid=(6,),
            in_specs=[pl.BlockSpec((rows, width), lambda i, s: (0, early(i)))] * 2
            + [pl.BlockSpec((rows, width), lambda i, s: (0, late(i)))] * 2
            + [whole(item.shape) for item in fixed]
            + [ANY] * len(ties),
            out_specs=[pl.BlockSpec((2, 4, 2 * per, half), left_at)] * 2
            + [pl.BlockSpec((2, 1, 4 * per, half), right_at)] * 2,
            scratch_shapes=[pltpu.VMEM((width, half), F32)],
        ),
        out_shape=[left, left, right, right],
        compiler_params=params(),
        cost_estimate=cost(),
        name="middle_weights",
    )(pos, act, act_far, grad, grad_far, *fixed, *ties)


def out_weight_kernel(pos, branch, branch_far, own, far, keep_in, send_in, keep_out, send_out, rows_f32):
    per = rows_f32.shape[0] // 16
    rows_f32[...] = dot_tn(branch[...], own[...]) + dot_tn(branch_far[...], far[...])
    for x, y, z in chips():
        (keep_out, send_out)[y][x, z] = rows_of(rows_f32, chip_row(pos, x, y, z), per)


def out_weight_call(pos, branch, branch_far, own, far, keep, send):
    rows, width = branch.shape
    half = width // 2
    block = pl.BlockSpec((2, 4, width // 16, half), lambda i, s: (0, 0, 4, 0))
    return pl.pallas_call(
        out_weight_kernel,
        grid_spec=pltpu.PrefetchScalarGridSpec(
            num_scalar_prefetch=1,
            grid=(1,),
            in_specs=[whole(branch.shape)] * 2 + [whole(own.shape)] * 2 + [ANY, ANY],
            out_specs=[block, block],
            scratch_shapes=[pltpu.VMEM((width, half), F32)],
        ),
        out_shape=[jax.ShapeDtypeStruct(keep.shape, BF16)] * 2,
        input_output_aliases={5: 0, 6: 1},
        compiler_params=params(),
        cost_estimate=cost(),
        name="out_weight",
    )(pos, branch, branch_far, own, far, keep, send)


def pack_sums(tables, long, packed):
    count, _, share = packed.shape
    for device in range(count):
        low = 0
        for table in tables:
            rows = table.shape[0]
            packed[device, low : low + rows, :] = table[:, device * share : (device + 1) * share]
            low += rows
        for part in range(4):
            at = (4 * device + part) * share
            packed[device, low + part : low + part + 1, :] = long[:, at : at + share]


def mixed_kernel(pos, act_send, act_own, down, after, bias, one, two, three, four, *rest, ties, carried):
    out, packed = rest[ties + carried : ties + carried + 2]
    total = rest[-1]
    step = pl.program_id(0)

    @pl.when(step == 0)
    def _():
        total[...] = after[...] + wide(bias)

    @pl.when(step < 2)
    def _():
        total[...] += dot(act_send[...], down[...])

    @pl.when(step >= 2)
    def _():
        total[...] += dot(act_own[...], down[...])

    @pl.when(step == pl.num_programs(0) - 1)
    def _():
        out[...] = total[...].astype(BF16)
        pack_sums((one, two, three), four, packed)


def mixed_call(pos, ties, carried, act_send, act_own, down, after, bias, *sums):
    rows, width = after.shape
    devices = lax.axis_size("batch") * lax.axis_size("head")
    packed = (devices, sum(item.shape[0] for item in sums[:3]) + 4, width // devices)

    def kernel(*refs):
        mixed_kernel(*refs, ties=len(ties), carried=len(carried))

    return pl.pallas_call(
        kernel,
        grid_spec=pltpu.PrefetchScalarGridSpec(
            num_scalar_prefetch=1,
            grid=(4,),
            in_specs=[
                pl.BlockSpec((rows, width), lambda i, s: (0, early(i))),
                pl.BlockSpec((rows, width), lambda i, s: (0, late(i))),
                pl.BlockSpec((width, width), lambda i, s: (hidden_block(i, s[0]), 0)),
                whole(after.shape),
                whole(bias.shape),
            ]
            + [whole(item.shape) for item in sums]
            + [ANY] * (len(ties) + len(carried)),
            out_specs=[whole((rows, width)), whole(packed)] + [ANY] * len(carried),
            scratch_shapes=[pltpu.VMEM((rows, width), F32)],
        ),
        out_shape=[jax.ShapeDtypeStruct((rows, width), BF16), jax.ShapeDtypeStruct(packed, F32)]
        + shapes(carried),
        input_output_aliases=carry(5 + len(sums) + len(ties), 2, carried),
        compiler_params=params(),
        cost_estimate=cost(),
        name="mixed",
    )(pos, act_send, act_own, down, after, bias, *sums, *ties, *carried)


def qkv_weight_kernel(
    pos, mine, mine_far, other, other_far, normed, normed_far, *rest, ties
):
    left_keep, left_send, right_keep, right_send, sums, rows_f32 = rest[ties:]
    core = pos[0]
    half = normed_far.shape[1]
    third = pl.program_id(0)
    own = normed[:, half_lanes(core, half)]
    ones = jnp.ones((8, own.shape[0]), BF16)

    @pl.when(third == 0)
    def _():
        sums[...] = jnp.zeros_like(sums)

    for near, far, at in ((mine, mine_far, core), (other, other_far, 1 - core)):
        rows = pl.ds(pl.multiple_of((2 * third + at) * half, 128), half)
        rows_f32[rows, :] = dot(near[0], own) + dot(far[0], normed_far[...])
    row = (dot_nt(ones, mine[0]) + dot_nt(ones, mine_far[0]))[:1]
    lanes = half_lanes(core, half)
    for t in range(3):
        sums[t : t + 1, lanes] += jnp.where(third == t, row, 0.0)

    @pl.when(third == pl.num_programs(0) - 1)
    def _():
        per = rows_f32.shape[0] // 32
        for x, y, z in chips():
            chip = chip_row(pos, x, y, z)
            (left_keep, left_send)[x][y, z] = rows_of(rows_f32, chip, 2 * per, 0, per)
            (right_keep, right_send)[y][x, z] = rows_of(rows_f32, chip, 2 * per, per, per)


def qkv_weight_call(pos, ties, mine, mine_far, other, other_far, normed, normed_far):
    rows, width = normed.shape
    half = width // 2
    third = pl.BlockSpec((1, half, rows), lambda t, s: (t, 0, 0))
    out = jax.ShapeDtypeStruct((2, 4, 3 * width // 32, half), BF16)

    def kernel(*refs):
        qkv_weight_kernel(*refs, ties=len(ties))

    return pl.pallas_call(
        kernel,
        grid_spec=pltpu.PrefetchScalarGridSpec(
            num_scalar_prefetch=1,
            grid=(3,),
            in_specs=[third] * 4 + [whole(normed.shape), whole(normed_far.shape)] + [ANY] * len(ties),
            out_specs=[whole(out.shape)] * 4 + [whole((3, width))],
            scratch_shapes=[pltpu.VMEM((3 * width, half), F32)],
        ),
        out_shape=[out] * 4 + [jax.ShapeDtypeStruct((3, width), F32)],
        compiler_params=params(),
        cost_estimate=cost(),
        name="qkv_weight",
    )(pos, mine, mine_far, other, other_far, normed, normed_far, *ties)


def input_back_kernel(pos, mine, other, weight, tok, ids, emb, gain, grad_after, *rest, ties, carried):
    out, sums = rest[ties + carried : ties + carried + 2]
    joined, total = rest[-2:]
    core = pos[0]
    step = pl.program_id(0)
    half = mine.shape[1]
    joined[half_lanes(core, half), :] = mine[0]
    joined[half_lanes(1 - core, half), :] = other[0]
    part = lax.dot_general(
        joined[...], weight[...], (((0,), (1,)), ((), ())), preferred_element_type=F32
    )

    @pl.when(step == 0)
    def _():
        total[...] = part

    @pl.when(step > 0)
    def _():
        total[...] += part

    @pl.when(step == pl.num_programs(0) - 1)
    def _():
        grad = total[...]
        scaled, scale = center_and_scale(embed_tokens(tok, ids, emb))
        inner = grad * wide(gain)
        shift = jnp.mean(inner, -1, keepdims=True)
        slope = jnp.mean(inner * scaled, -1, keepdims=True)
        result = grad_after[...] + scale * (inner - shift - scaled * slope)
        out[...] = result
        passes = emb.shape[0]
        chosen = pass_rows(ids, passes)
        high = result.astype(BF16)
        less = result - high.astype(F32)
        middle = less.astype(BF16)
        least = (less - middle.astype(F32)).astype(BF16)
        sums[0:passes] = dot(chosen, high) + (dot(chosen, middle) + dot(chosen, least))
        sums[passes : passes + 1] = jnp.sum(grad * scaled, axis=0, keepdims=True)
        sums[passes + 1 : passes + 2] = jnp.sum(grad, axis=0, keepdims=True)


def input_back(pos, ties, carried, mine, other, weight, tok, ids, emb, gain, grad_after):
    rows, width = tok.shape
    third = pl.BlockSpec((1, width // 2, rows), lambda t, s: (t, 0, 0))
    fixed = (tok, ids, emb, gain, grad_after)
    outs = [
        jax.ShapeDtypeStruct((rows, width), F32),
        jax.ShapeDtypeStruct((emb.shape[0] + 2, width), F32),
    ]

    def kernel(*refs):
        input_back_kernel(*refs, ties=len(ties), carried=len(carried))

    return pl.pallas_call(
        kernel,
        grid_spec=pltpu.PrefetchScalarGridSpec(
            num_scalar_prefetch=1,
            grid=(3,),
            in_specs=[third, third, pl.BlockSpec((width, width), lambda t, s: (0, t))]
            + [whole(item.shape) for item in fixed]
            + [ANY] * (len(ties) + len(carried)),
            out_specs=[whole(item.shape) for item in outs] + [ANY] * len(carried),
            scratch_shapes=[pltpu.VMEM((width, rows), BF16), pltpu.VMEM((rows, width), F32)],
        ),
        out_shape=outs + shapes(carried),
        input_output_aliases=carry(3 + len(fixed) + len(ties), len(outs), carried),
        compiler_params=params(),
        cost_estimate=cost(),
        name="input_back",
    )(pos, mine, other, weight, *fixed, *ties, *carried)


def swap_head(values, bit):
    size = lax.axis_size("head")
    return lax.ppermute(values, "head", [(i, i ^ bit) for i in range(size)])


def swap_batch(values, bit):
    size = lax.axis_size("batch")
    return lax.ppermute(values, "batch", [(i, i ^ bit) for i in range(size)])


class Sum:
    def __init__(self, *parts):
        self.parts = parts

    def __getitem__(self, index):
        return Sum(*[part[index] for part in self.parts])

    def wide(self):
        total = self.parts[0].astype(F32)
        for part in self.parts[1:]:
            total = total + part.astype(F32)
        return total

    def sent(self):
        return self.wide().astype(BF16)


def swap_x(values):
    return swap_head(values, 2)


def swap_y(values):
    return swap_batch(values, 1)


def z_step(left, right):
    cut = left.parts[0].shape[0] // 2
    split = left.parts[0].shape[1]
    sent = jnp.concatenate([left[cut:].sent(), right[cut:].sent()], 1)

    def finish():
        got = swap_batch(sent, 2 if cut == 2 else 4)
        return Sum(*left[:cut].parts, got[:, :split]), Sum(*right[:cut].parts, got[:, split:])

    return sent, finish


def chip_sums(core, *items):
    flat = [jnp.where(core == 0, item[..., 1, :, :], item[..., 0, :, :]) for item in items]
    width = flat[0].shape[-1]
    got = swap_head(jnp.concatenate([item.reshape(-1, width) for item in flat], 0), 1)
    out, at = [], 0
    for item, sent in zip(items, flat):
        count = sent.size // width
        far = got[at : at + count].reshape(sent.shape)
        near = jnp.where(core == 0, item[..., 0, :, :], item[..., 1, :, :])
        out.append((jnp.where(core == 0, near, far), jnp.where(core == 0, far, near)))
        at += count
    return out


def scatter_any(core, values):
    half = values.shape[-1]
    rows = values.reshape(-1, half).astype(F32)
    both = lax.dynamic_update_slice(jnp.zeros((rows.shape[0], 2 * half), F32), rows, (0, core * half))
    return lax.psum_scatter(both, ("batch", "head"), scatter_dimension=0, tiled=True)


def by_chip(values):
    rest = values.shape[3:]
    split = values.reshape((2, 2, 2, 2) + rest)
    order = (3, 2, 1, 0) + tuple(range(4, split.ndim))
    return split.transpose(order).reshape((16,) + rest)


def on_device(
    tokens,
    pass_ids,
    segment_ids,
    pass_embed,
    norm1_gain,
    norm1_shift,
    qkv_weight,
    qv_bias,
    out_weight,
    out_bias,
    norm2_gain,
    norm2_shift,
    up_weight,
    up_bias,
    down_weight,
    down_bias,
    cotangent,
):
    rows, width = tokens.shape
    hidden_units = up_weight.shape[1]
    passes = pass_embed.shape[0]
    pairs = width // 2 // PAIR
    assert 2 * rows == SEQ_LEN and lax.axis_size("head") == 4 and hidden_units == 4 * width
    direct = lax.axis_size("batch") == BLOCKS

    head = lax.axis_index("head").astype(jnp.int32)
    batch = lax.axis_index("batch").astype(jnp.int32)
    core, x_bit = head % 2, head // 2
    zero = jnp.zeros((), jnp.int32)
    place = [core, x_bit, batch] if direct else [zero, zero, zero]
    pos = jnp.stack([core] + place + [x_bit])

    row = lambda item: item.reshape(1, -1)
    ids = row(pass_ids)
    gain_one, gain_two = row(norm1_gain), row(norm2_gain)
    cot_far = swap_head(cotangent, 1)
    normed, normed_send, send = qkv_send(
        pos, tokens, ids, pass_embed, gain_one, row(norm1_shift), qkv_weight, qv_bias
    )
    recv = swap_head(send, 1)
    normed_far = swap_head(normed_send, 1)
    keep = qkv_keep(pos, normed, qkv_weight, qv_bias)
    own, far_send, lse = attend(pos, segment_ids, keep, recv)
    far = swap_head(far_send, 1)
    after, normed_two, normed_two_send, act_own, act_send, grad_pre, up_bias_grad = ff_first(
        pos, tokens, ids, pass_embed, own, far, out_weight, row(out_bias), gain_two, row(norm2_shift),
        cotangent, up_weight, row(up_bias), down_weight,
    )
    act_far = swap_head(act_send, 1)
    grad_pre_far = swap_head(grad_pre, 1)
    normed_two_far = swap_head(normed_two_send, 1)
    grad_after, branch, grad_own, grad_send, sums_two = ff_back(
        pos, grad_pre, up_weight, after, cotangent, gain_two, out_weight
    )
    grad_far = swap_head(grad_send, 1)
    branch_far = swap_head(branch, 1)
    down_keep, down_send, up_keep, up_send = middle_weights(
        pos, (), act_own, act_far, grad_pre, grad_pre_far, cotangent, cot_far, normed_two, normed_two_far
    )
    up_keep, up_send = out_weight_call(pos, branch, branch_far, own, far_send, up_keep, up_send)
    if direct:
        left = Sum(down_keep, swap_x(down_send))
        right = Sum(up_keep, swap_y(up_send))
    mine, mine_send = attend_back(
        (down_send, up_send), pos, segment_ids, lse, keep, recv, own, far_send, grad_own, grad_far
    )
    other = swap_head(mine_send, 1)
    other_far = swap_head(mine, 1)
    ties, carried = (), ()
    if direct:
        left_sent, right_sent = left[1].sent(), right[1].sent()
        ties = (left_sent, right_sent)
    left_keep, left_send, right_keep, right_send, bias_sums = qkv_weight_call(
        pos, ties, mine, mine_send, other, other_far, normed, normed_far
    )
    if direct:
        one_got, two_got = swap_x(left_send), swap_y(right_send)
        left = Sum(*left[0].parts, swap_y(left_sent))
        right = Sum(*right[0].parts, swap_x(right_sent))
        mid_sent, mid_next = z_step(left, right)
        ties, carried = (mid_sent,), (left_keep, right_keep)
    input_grad, sums_one, *carried = input_back(
        pos, ties, carried, mine, other, qkv_weight, tokens, ids, pass_embed, gain_one, grad_after
    )
    if direct:
        one, two = Sum(carried[0], one_got), Sum(carried[1], two_got)
        one_sent, two_sent = one[1].sent(), two[1].sent()
        one_last, two_last = swap_y(one_sent), swap_x(two_sent)
        mid_sent, mid_next = z_step(*mid_next())
        qkv_sent, qkv_next = z_step(Sum(*one[0].parts, one_last), Sum(*two[0].parts, two_last))
        ties = (mid_sent, qkv_sent)
    result, packed, *carried = mixed_call(
        pos, ties, carried, act_send, act_own, down_weight, after, row(down_bias),
        sums_one, bias_sums, sums_two, up_bias_grad,
    )

    per = width // 32
    if direct:
        one, two = qkv_next()
        one = Sum(carried[0][0][:2], *one.parts[1:])
        two = Sum(carried[1][0][:2], *two.parts[1:])
        _, qkv_next = z_step(one, two)
        left, right = [item.wide()[0] for item in mid_next()]
        cut = 8 * per
        down, up, out = chip_sums(
            core,
            left.reshape(4, 2, per, -1),
            right[:cut].reshape(2, 4 * per, -1),
            right[cut:].reshape(2, per, -1),
        )
        (qkv,) = chip_sums(core, jnp.stack([item.wide()[0] for item in qkv_next()]))
        down_grad = jnp.concatenate(down, 0).transpose(0, 2, 1).reshape(hidden_units, -1)
        up_grad, out_grad, qkv_grad = [jnp.concatenate(item, -1) for item in (up, out, qkv)]
    else:
        down = by_chip(jnp.stack([down_keep, down_send])).reshape(16, 4, 2 * per, -1)
        down = down.transpose(0, 2, 1, 3).reshape(16, 2 * per, -1)
        up = by_chip(jnp.stack([up_keep, up_send], 1))
        left = by_chip(jnp.stack([left_keep, left_send]))
        right = by_chip(jnp.stack([right_keep, right_send], 1))
        cut = 8 * per
        down_grad = scatter_any(core, down).T
        up_grad = scatter_any(core, up[:, :cut])
        out_grad = scatter_any(core, up[:, cut:])
        qkv_grad = scatter_any(core, jnp.concatenate([left, right], 1))
    got = lax.all_to_all(packed, ("batch", "head"), split_axis=0, concat_axis=0, tiled=True)
    small = jnp.sum(got, 0)
    bias_at, two_at, up_at = passes + 2, passes + 5, passes + 9
    return (
        result,
        input_grad,
        small[:passes],
        small[passes],
        small[passes + 1],
        qkv_grad.T,
        jnp.stack([small[bias_at], small[bias_at + 2]]),
        out_grad.T,
        small[two_at + 2],
        small[two_at],
        small[two_at + 1],
        up_grad.T,
        small[up_at:].reshape(-1),
        down_grad,
        small[two_at + 3],
    )


def solution(mesh):
    both = ("batch", "head")
    copied = P()
    in_specs = (P(both, None), P(both), P("batch", None)) + (copied,) * 13 + (P(both, None),)
    out_specs = (
        P(both, None),
        P(both, None),
        P(None, both),
        P(both),
        P(both),
        P(None, both),
        P(None, both),
        P(None, both),
        P(both),
        P(both),
        P(both),
        P(None, both),
        P(both),
        P(None, both),
        P(both),
    )
    return jax.shard_map(
        on_device, mesh=mesh, in_specs=in_specs, out_specs=out_specs, check_vma=False
    )
```

time: 292 us -> 225 us (0.77)
  starting transfers between devices: 53.9 us -> 28.6 us
  waiting for transfers between devices: 44.6 us -> 21.4 us
  Pallas kernels: 143 us -> 133 us
  other arithmetic: 25.8 us -> 19.1 us
    ppermute x17 -> x8, starting transfers between devices: 43.2 us -> 14.4 us  [swap_batch(): return lax.ppermute(values, 'batch', [(i, i ^ bit) for i in range(size)])]
    ppermute x17 -> x8, waiting for transfers between devices: 21 us -> 4.7 us  [swap_batch(): return lax.ppermute(values, 'batch', [(i, i ^ bit) for i in range(size)])]
    ppermute x13 -> x17, waiting for transfers between devices: 23.6 us -> 13.6 us  [swap_head(): return lax.ppermute(values, 'head', [(i, i ^ bit) for i in range(size)])]
    pallas_call x8 -> x7, Pallas kernels: 94 us -> 86.3 us  [the longest x1 21.9 us: attend_back(): pl.pallas_call(kernel, grid_spec=pltpu.PrefetchScalarGridSpec(num_scalar_...]
    unnamed x30 -> x54, local copies, waits for them, and re-layouts: 4.13 us -> 9.91 us
    ppermute x13 -> x17, starting transfers between devices: 6.43 us -> 11.1 us  [swap_head(): return lax.ppermute(values, 'head', [(i, i ^ bit) for i in range(size)])]
    all_to_all x1, waiting for transfers between devices: 0.01 us -> 3.04 us  [on_device(): lax.all_to_all(packed, ('batch', 'head'), split_axis=0, concat_axis=0, ti...]
    convert_element_type x16 -> x11, other arithmetic: 13.1 us -> 11.2 us  [sent(): return self.wide().astype(BF16)]
  transfers between devices with their start and end apart: 31 -> 26, of which waited for: 11 -> 9; matrix products, arithmetic and copies ran while one was open for 11% -> 11% of each run, Pallas kernels for 21% -> 39%
where the time goes in v2:
time: 225 us; the launch traced here: 223 us
  Pallas kernels  133 us (59%)
  starting transfers between devices  28.6 us (13%)
  waiting for transfers between devices  21.4 us (10%)
  local copies, waits for them, and re-layouts  20.2 us (9%)
  other arithmetic  19.1 us (8%)
    pallas_call x1, Pallas kernels, attend_back(): pl.pallas_call(kernel, grid_spec=pltpu.PrefetchScalarGridSpec(num_scalar_...  21.9 us
    pallas_call x1, Pallas kernels, ff_first(): pl.pallas_call(ff_first_kernel, grid_spec=pltpu.PrefetchScalarGridSpec(nu...  19.9 us
    pallas_call x1, Pallas kernels, middle_weights(): pl.pallas_call(kernel, grid_spec=pltpu.PrefetchScalarGridSpec(num_scalar_...  16.9 us
    pallas_call x1, Pallas kernels, attend(): pl.pallas_call(attend_kernel, grid_spec=pltpu.PrefetchScalarGridSpec(num_...  14.6 us
    ppermute x8, starting transfers between devices, swap_batch(): return lax.ppermute(values, 'batch', [(i, i ^ bit) for i in range(size)])  14.4 us
    ppermute x17, waiting for transfers between devices, swap_head(): return lax.ppermute(values, 'head', [(i, i ^ bit) for i in range(size)])  13.6 us
    pallas_call x1, Pallas kernels, ff_back(): pl.pallas_call(ff_back_kernel, grid_spec=pltpu.PrefetchScalarGridSpec(num...  13.1 us
    pallas_call x1, Pallas kernels, input_back(): pl.pallas_call(kernel, grid_spec=pltpu.PrefetchScalarGridSpec(num_scalar_...  11.4 us
  transfers between devices with their start and end apart: 26, of which 9 were waited for; matrix products, arithmetic and copies ran while one was open for 11% of the time, Pallas kernels for 39%

profile of v2, /device:TPU:0, one launch (start us, length us, event | category | flops | bytes accessed | tf_op | source)
XLA Modules:
  0.0 223.3 jit_solution(16066408004776889735)
XLA Ops:
  0.7 1.3 reshape.404.ids.refs_5_
  1.9 1.3 reshape.405.gain.refs_7_
  3.2 1.3 reshape.406.shift
  5.1 6.6 %qkv_send.1 = (bf16[640,768]{1,0:T(8,128)(2,1)}, bf16[640,384]{1,0:T(8,128)(2,1)}, bf16[3,640,384]{2,1,0:T(8,128)(2,1)}) custom-call(s32[5]{0:T(128)} %stack.20.pos.refs_0_, bf16[640,768]{1,0:T(8,128)(2,1)} %refs_4_.1, s32[1,640]{1,0:T(1,128)} %reshape.404.ids.refs_5_, bf16[5,768]{1,0:T(8,128)(2,1)} %refs_6_.1, bf16[1,768]{1,0:T(2,128)(2,1)} %reshape.405.gain.refs_7_, ...), custom_call_target="tpu_custom_call" | custom-call | flops 1000 | bytes 1000 | tf_op jit(solution)/shard_map/qkv_send/pallas_call | solution.py:104
  12.1 5.5 %qkv_keep.1.keep.refs_3_ = bf16[3,640,384]{2,1,0:T(8,128)(2,1)} custom-call(s32[5]{0:T(128)} %stack.20.pos.refs_0_, bf16[640,768]{1,0:T(8,128)(2,1)} %get-tuple-element.54.normed.refs_5_, bf16[768,2304]{1,0:T(8,128)(2,1)} %refs_3_.2, bf16[2,768]{1,0:T(2,128)(2,1)} %bias.3), custom_call_target="tpu_custom_call" | custom-call | flops 1000 | bytes 1000 | tf_op jit(solution)/shard_map/qkv_keep/pallas_call | solution.py:138
  17.7 1.1 copy-done.1
  18.8 14.6 %attend.1 = (bf16[640,384]{1,0:T(8,128)(2,1)}, bf16[640,384]{1,0:T(8,128)(2,1)}, f32[5,3,1,512]{3,2,1,0:T(1,128)}) custom-call(s32[5]{0:T(128)} %stack.20.pos.refs_0_, s32[2,1280]{1,0:T(2,128)} %refs_1_.1, bf16[3,640,384]{2,1,0:T(8,128)(2,1)} %qkv_keep.1.keep.refs_3_, bf16[3,640,384]{2,1,0:T(8,128)(2,1)} %copy-done.1), custom_call_target="tpu_custom_call" | custom-call | flops 1000 | bytes 1000 | tf_op jit(solution)/shard_map/attend/pallas_call | solution.py:291
  36.7 19.9 %ff_first.1 = (f32[640,768]{1,0:T(8,128)}, bf16[640,768]{1,0:T(8,128)(2,1)}, bf16[640,384]{1,0:T(8,128)(2,1)}, bf16[640,1536]{1,0:T(8,128)(2,1)}, bf16[640,1536]...) custom-call(s32[5]{0:T(128)} %stack.20.pos.refs_0_, bf16[640,768]{1,0:T(8,128)(2,1)} %refs_4_.1, ...), custom_call_target="tpu_custom_call" | custom-call | flops 1000 | bytes 1000 | tf_op jit(solution)/shard_map/ff_first/pallas_call | solution.py:504
  57.7 13.1 %ff_back.1 = (f32[640,768]{1,0:T(8,128)}, bf16[640,768]{1,0:T(8,128)(2,1)}, bf16[640,384]{1,0:T(8,128)(2,1)}, bf16[640,384]{1,0:T(8,128)(2,1)}, f32[4,768]{1,0:T(4,128)}) custom-call(s32[5]{0:T(128)} %stack.20.pos.refs_0_, bf16[640,3072]{1,0:T(8,128)(2,1)} %get-tuple-element.62.grad_pre.refs_3_, bf16[768,3072]{1,0:T(8,128)(2,1)} %up.3, ...), custom_call_target="tpu_custom_call" | custom-call | flops 1000 | bytes 1000 | tf_op jit(solution)/shard_map/ff_back/pallas_call | solution.py:590
  71.4 3.0 %collective-permute-done.6.refs_8_ = bf16[640,384]{1,0:T(8,128)(2,1)S(1)} collective-permute-done((bf16[640,384]{1,0:T(8,128)(2,1)}, bf16[640,384]{1,0:T(8,128)(2,1)S(1)}, u32[]{:S(2)}, u32[]{:S(2)}) %collective-permute-start.6) | collective-permute-done | bytes 491552 | tf_op jit(solution)/shard_map/ppermute | solution.py:921
  75.8 1.3 copy-done.4
  77.1 16.9 %middle_weights.1 = (bf16[2,4,192,384]{3,2,1,0:T(8,128)(2,1)}, bf16[2,4,192,384]{3,2,1,0:T(8,128)(2,1)}, bf16[2,4,240,384]{3,2,1,0:T(8,128)(2,1)}, bf16[2,4,240,384]{3,2,1,0:T(8,128)(2,1)}) custom-call(s32[5]{0:T(128)} %stack.20.pos.refs_0_, bf16[640,1536]{1,0:T(8,128)(2,1)} %get-tuple-element.59.refs_1_.refs_2_, bf16[640,1536]{1,0:T(8,128)(2,1)} %copy-done.7, ...), custom_call_target="tpu_custom_call" | custom-call | flops 1000 | bytes 1000 | tf_op jit(solution)/shard_map/middle_weights/pallas_call | solution.py:674
  94.0 4.8 %out_weight.1 = (bf16[2,4,240,384]{3,2,1,0:T(8,128)(2,1)}, bf16[2,4,240,384]{3,2,1,0:T(8,128)(2,1)}) custom-call(s32[5]{0:T(128)} %stack.20.pos.refs_0_, bf16[640,768]{1,0:T(8,128)(2,1)} %get-tuple-element.68.branch, bf16[640,768]{1,0:T(8,128)(2,1)} %collective-permute-done.7.branch_far, ...), custom_call_target="tpu_custom_call", output_to_operand_aliasing={{0}: (5, {}), {1}: (6, {})} | custom-call | flops 1000 | bytes 1000 | tf_op jit(solution)/shard_map/out_weight/pallas_call | solution.py:705
  98.8 3.7 %collective-permute-start.11 = (bf16[2,4,240,384]{3,2,1,0:T(8,128)(2,1)}, bf16[2,4,240,384]{3,2,1,0:T(8,128)(2,1)S(1)}, u32[]{:S(2)}, u32[]{:S(2)}) collective-permute-start(bf16[2,4,240,384]{3,2,1,0:T(8,128)(2,1)} %get-tuple-element.71.refs_10_), channel_id=1, source_target_pairs={{0,4},{4,0},{8,12},{12,8},{16,20},{20,16},{24,28},{28,24},{1,5},{5... | collective-permute-start | bytes 4423688 | tf_op jit(solution)/shard_map/ppermute | solution.py:926
  102.5 2.2 collective-permute-start.9
  104.8 1.8 collective-permute-done.2.refs_8_
  107.4 21.9 %attend_back.1 = (bf16[3,384,640]{2,1,0:T(8,128)(2,1)}, bf16[3,384,640]{2,1,0:T(8,128)(2,1)}) custom-call(s32[5]{0:T(128)} %stack.20.pos.refs_0_, s32[2,1280]{1,0:T(2,128)} %refs_1_.1, f32[5,3,1,512]{3,2,1,0:T(1,128)} %get-tuple-element.61.refs_2_, bf16[3,640,384]{2,1,0:T(8,128)(2,1)} %qkv_keep.1.keep.refs_3_, bf16[3,640,384]{2,1,0:T(8,128)(2,1)} %copy-done.1, ...), custom_call_target="tpu_custom_call" | custom-call | flops 1000 | bytes 1000 | tf_op jit(solution)/shard_map/attend_back/pallas_call | solution.py:413
  130.0 1.5 collective-permute-done.9
  131.6 2.4 %collective-permute-start.10 = (bf16[4,192,384]{2,1,0:T(8,128)(2,1)S(1)}, bf16[4,192,384]{2,1,0:T(8,128)(2,1)}, u32[]{:S(2)}, u32[]{:S(2)}) collective-permute-start(bf16[4,192,384]{2,1,0:T(8,128)(2,1)S(1)} %fusion.2.refs_7_), channel_id=1, source_target_pairs={{0,4},{4,0},{8,12},{12,8},{16,20},{20,16},{24,28},{28,24},{1,5},{5... | collective-permute-start | bytes 1769480 | tf_op jit(solution)/shard_map/ppermute | solution.py:926
  134.0 1.8 collective-permute-done.11
  135.8 1.1 copy-done.8
  137.0 1.1 fusion.refs_8_
  138.0 4.2 %collective-permute-start.12 = (bf16[4,240,384]{2,1,0:T(8,128)(2,1)}, bf16[4,240,384]{2,1,0:T(8,128)(2,1)}, u32[]{:S(2)}, u32[]{:S(2)}) collective-permute-start(bf16[4,240,384]{2,1,0:T(8,128)(2,1)} %fusion.refs_8_), channel_id=1, source_target_pairs={{0,2},{1,3},{2,0},{3,1},{4,6},{5,7},{6,4},{7,5},{8,10},{9,11},{10,... | collective-permute-start | bytes 2211848 | tf_op jit(solution)/shard_map/ppermute | solution.py:921
  142.9 1.2 copy-done.2
  144.1 8.8 %qkv_weight.1 = (bf16[2,4,72,384]{3,2,1,0:T(8,128)(2,1)}, bf16[2,4,72,384]{3,2,1,0:T(8,128)(2,1)}, bf16[2,4,72,384]{3,2,1,0:T(8,128)(2,1)}, bf16[2,4,72,384]{3,2,1,0:T(8,128)(2,1)}, f32[3,768]{1,0:T(4,128)}) custom-call(s32[5]{0:T(128)} %stack.20.pos.refs_0_, bf16[3,384,640]{2,1,0:T(8,128)(2,1)} %get-tuple-element.72.refs_1_, ...), custom_call_target="tpu_custom_call" | custom-call | flops 1000 | bytes 1000 | tf_op jit(solution)/shard_map/qkv_weight/pallas_call | solution.py:832
  153.0 1.3 fusion.3
  154.3 5.6 %collective-permute-done.12 = bf16[4,240,384]{2,1,0:T(8,128)(2,1)} collective-permute-done((bf16[4,240,384]{2,1,0:T(8,128)(2,1)}, bf16[4,240,384]{2,1,0:T(8,128)(2,1)}, u32[]{:S(2)}, u32[]{:S(2)}) %collective-permute-start.12) | collective-permute-done | bytes 737312 | tf_op jit(solution)/shard_map/ppermute | solution.py:921
  159.9 1.2 fusion.1
  161.2 1.1 collective-permute-start.15
  162.3 11.4 %input_back.1 = (f32[640,768]{1,0:T(8,128)}, f32[7,768]{1,0:T(8,128)}, bf16[2,4,72,384]{3,2,1,0:T(8,128)(2,1)}, bf16[2,4,72,384]{3,2,1,0:T(8,128)(2,1)}) custom-call(s32[5]{0:T(128)} %stack.20.pos.refs_0_, bf16[3,384,640]{2,1,0:T(8,128)(2,1)} %get-tuple-element.72.refs_1_, ...), custom_call_target="tpu_custom_call", output_to_operand_aliasing={{2}: (10, {}), {3}: (11, {})} | custom-call | flops 1000 | bytes 1000 | tf_op jit(solution)/shard_map/input_back/pallas_call | solution.py:900
  173.8 1.2 fusion.12
  174.9 1.0 collective-permute-start.17
  176.0 1.2 fusion.13
  178.0 2.9 %collective-permute-done.17 = bf16[4,72,384]{2,1,0:T(8,128)(2,1)S(1)} collective-permute-done((bf16[4,72,384]{2,1,0:T(8,128)(2,1)S(1)}, bf16[4,72,384]{2,1,0:T(8,128)(2,1)S(1)}, u32[]{:S(2)}, u32[]{:S(2)}) %collective-permute-start.17) | collective-permute-done | bytes 221216 | tf_op jit(solution)/shard_map/ppermute | solution.py:926
  181.9 1.3 collective-permute-done.19
  183.1 1.0 fusion.14
  185.0 1.1 fusion.7
  186.1 1.1 fusion.11
  187.3 2.5 %collective-permute-start.23 = (bf16[1,432,384]{2,1,0:T(8,128)(2,1)S(1)}, bf16[1,432,384]{2,1,0:T(8,128)(2,1)S(1)}, u32[]{:S(2)}, u32[]{:S(2)}) collective-permute-start(bf16[1,432,384]{2,1,0:T(8,128)(2,1)S(1)} %pad_maximum_fusion.1.refs_10_), channel_id=1, source_target_pairs={{0,16},{4,20},{8,24},{12,28},{16,0},{20,4},{24,8},{28,12},{1,17},{... | collective-permute-start | bytes 995336 | tf_op jit(solution)/shard_map/ppermute | solution.py:926
  189.9 9.3 %mixed.1 = (bf16[640,768]{1,0:T(8,128)(2,1)}, f32[32,18,24]{2,1,0:T(8,128)}, bf16[2,4,72,384]{3,2,1,0:T(8,128)(2,1)}, bf16[2,4,72,384]{3,2,1,0:T(8,128)(2,1)}) custom-call(s32[5]{0:T(128)} %stack.20.pos.refs_0_, bf16[640,1536]{1,0:T(8,128)(2,1)} %get-tuple-element.58.refs_1_, ...), custom_call_target="tpu_custom_call", output_to_operand_aliasing={{2}: (12, {}), {3}: (13, {})} | custom-call | flops 1000 | bytes 1000 | tf_op jit(solution)/shard_map/mixed/pallas_call | solution.py:766
  199.2 2.0 reshape.415
  201.2 3.2 %all-to-all-start = ((f32[32,1,432]{2,1,0:T(1,128)}), f32[32,1,432]{2,1,0:T(1,128)S(1)}, u32[]{:S(2)}, u32[]{:S(2)}) async-start(f32[32,1,432]{2,1,0:T(1,128)} %reshape.415), calls=%async_computation | async-start | bytes 131072 | tf_op jit(solution)/shard_map/all_to_all | solution.py:1119
  204.4 1.0 fusion.21
  206.1 2.7 %collective-permute-start.21 = (bf16[1,144,384]{2,1,0:T(8,128)(2,1)}, bf16[1,144,384]{2,1,0:T(8,128)(2,1)}, u32[]{:S(2)}, u32[]{:S(2)}) collective-permute-start(bf16[1,144,384]{2,1,0:T(8,128)(2,1)} %pad_maximum_fusion.4), channel_id=1, source_target_pairs={{0,16},{4,20},{8,24},{12,28},{16,0},{20,4},{24,8},{28,12},{1,17},{... | collective-permute-start | bytes 331784 | tf_op jit(solution)/shard_map/ppermute | solution.py:926
  208.8 3.0 %all-to-all-done = f32[32,1,432]{2,1,0:T(1,128)S(1)} async-done(((f32[32,1,432]{2,1,0:T(1,128)}), f32[32,1,432]{2,1,0:T(1,128)S(1)}, u32[]{:S(2)}, u32[]{:S(2)}) %all-to-all-start) | async-done | bytes 55328 | tf_op jit(solution)/shard_map/all_to_all | solution.py:1119
  215.7 1.1 select_bitcast_fusion.1
  216.9 1.1 fusion.5
  218.1 1.1 fusion.9
  (117 shorter events, 21.4 us)
Async XLA Ops:
  11.6 6.0 %collective-permute-start = (bf16[3,640,384]{2,1,0:T(8,128)(2,1)}, bf16[3,640,384]{2,1,0:T(8,128)(2,1)S(1)}, u32[]{:S(2)}, u32[]{:S(2)}) collective-permute-start(bf16[3,640,384]{2,1,0:T(8,128)(2,1)} %get-tuple-element.55), channel_id=1, source_target_pairs={{0,1},{1,0},{2,3},{3,2},{4,5},{5,4},{6,7},{7,6},{8,9},{9,8},{10,11... | collective-permute-start | bytes 4423688 | tf_op jit(solution)/shard_map/ppermute | solution.py:921
  17.6 15.9 %copy-start.21 = (bf16[768]{0:T(1024)(128)(2,1)S(1)}, bf16[768]{0:T(1024)(128)(2,1)}, u32[]{:S(2)}) copy-start(bf16[768]{0:T(1024)(128)(2,1)} %param.27) | copy-start | bytes 4612
  17.6 16.5 %copy-start.20 = (bf16[3072]{0:T(1024)(128)(2,1)S(1)}, bf16[3072]{0:T(1024)(128)(2,1)}, u32[]{:S(2)}) copy-start(bf16[3072]{0:T(1024)(128)(2,1)} %param.30) | copy-start | bytes 18436
  17.6 17.1 %copy-start.22 = (bf16[768]{0:T(1024)(128)(2,1)S(1)}, bf16[768]{0:T(1024)(128)(2,1)}, u32[]{:S(2)}) copy-start(bf16[768]{0:T(1024)(128)(2,1)} %param.26) | copy-start | bytes 4612
  17.6 17.7 %copy-start.23 = (bf16[768]{0:T(1024)(128)(2,1)S(1)}, bf16[768]{0:T(1024)(128)(2,1)}, u32[]{:S(2)}) copy-start(bf16[768]{0:T(1024)(128)(2,1)} %param.28) | copy-start | bytes 4612
  17.6 1.1 copy-start.1
  33.4 2.5 %collective-permute-start.1 = (bf16[640,384]{1,0:T(8,128)(2,1)}, bf16[640,384]{1,0:T(8,128)(2,1)S(1)}, u32[]{:S(2)}, u32[]{:S(2)}) collective-permute-start(bf16[640,384]{1,0:T(8,128)(2,1)} %get-tuple-element.57.far.refs_6_), channel_id=1, source_target_pairs={{0,1},{1,0},{2,3},{3,2},{4,5},{5,4},{6,7},{7,6},{8,9},{9,8},{10,11... | collective-permute-start | bytes 1474568 | tf_op jit(solution)/shard_map/ppermute | solution.py:921
  36.7 20.7 %copy-start = (bf16[640,768]{1,0:T(8,128)(2,1)S(1)}, bf16[640,768]{1,0:T(8,128)(2,1)}, u32[]{:S(2)}) copy-start(bf16[640,768]{1,0:T(8,128)(2,1)} %refs_5_.1) | copy-start | bytes 2949124
  56.6 17.8 %collective-permute-start.4 = (bf16[640,3072]{1,0:T(8,128)(2,1)}, bf16[640,3072]{1,0:T(8,128)(2,1)S(1)}, u32[]{:S(2)}, u32[]{:S(2)}) collective-permute-start(bf16[640,3072]{1,0:T(8,128)(2,1)} %get-tuple-element.62.grad_pre.refs_3_), channel_id=1, source_target_pairs={{0,1},{1,0},{2,3},{3,2},{4,5},{5,4},{6,7},{7,6},{8,9},{9,8},{10,11... | collective-permute-start | bytes 11796488 | tf_op jit(solution)/shard_map/ppermute | solution.py:921
  57.2 17.1 %collective-permute-start.3 = (bf16[640,1536]{1,0:T(8,128)(2,1)}, bf16[640,1536]{1,0:T(8,128)(2,1)S(1)}, u32[]{:S(2)}, u32[]{:S(2)}) collective-permute-start(bf16[640,1536]{1,0:T(8,128)(2,1)} %get-tuple-element.58.refs_1_), channel_id=1, source_target_pairs={{0,1},{1,0},{2,3},{3,2},{4,5},{5,4},{6,7},{7,6},{8,9},{9,8},{10,11... | collective-permute-start | bytes 5898248 | tf_op jit(solution)/shard_map/ppermute | solution.py:921
  57.3 14.1 %collective-permute-start.5 = (bf16[640,768]{1,0:T(8,128)(2,1)S(1)}, bf16[640,768]{1,0:T(8,128)(2,1)S(1)}, u32[]{:S(2)}, u32[]{:S(2)}) collective-permute-start(bf16[640,768]{1,0:T(8,128)(2,1)S(1)} %copy-done), channel_id=1, source_target_pairs={{0,1},{1,0},{2,3},{3,2},{4,5},{5,4},{6,7},{7,6},{8,9},{9,8},{10,11... | collective-permute-start | bytes 2949128 | tf_op jit(solution)/shard_map/ppermute | solution.py:921
  70.9 23.1 %collective-permute-start.7 = (bf16[640,768]{1,0:T(8,128)(2,1)}, bf16[640,768]{1,0:T(8,128)(2,1)}, u32[]{:S(2)}, u32[]{:S(2)}) collective-permute-start(bf16[640,768]{1,0:T(8,128)(2,1)} %get-tuple-element.68.branch), channel_id=1, source_target_pairs={{0,1},{1,0},{2,3},{3,2},{4,5},{5,4},{6,7},{7,6},{8,9},{9,8},{10,11... | collective-permute-start | bytes 2949128 | tf_op jit(solution)/shard_map/ppermute | solution.py:921
  70.9 3.4 %collective-permute-start.6 = (bf16[640,384]{1,0:T(8,128)(2,1)}, bf16[640,384]{1,0:T(8,128)(2,1)S(1)}, u32[]{:S(2)}, u32[]{:S(2)}) collective-permute-start(bf16[640,384]{1,0:T(8,128)(2,1)} %get-tuple-element.66), channel_id=1, source_target_pairs={{0,1},{1,0},{2,3},{3,2},{4,5},{5,4},{6,7},{7,6},{8,9},{9,8},{10,11... | collective-permute-start | bytes 1474568 | tf_op jit(solution)/shard_map/ppermute | solution.py:921
  71.4 3.8 %copy-start.12 = (bf16[640,768]{1,0:T(8,128)(2,1)}, bf16[640,768]{1,0:T(8,128)(2,1)S(1)}, u32[]{:S(2)}) copy-start(bf16[640,768]{1,0:T(8,128)(2,1)S(1)} %collective-permute-done.5.refs_6_) | copy-start | bytes 2949124
  74.3 1.4 copy-start.7
  75.1 2.0 copy-start.4
  94.0 10.7 %copy-start.25 = (bf16[640,384]{1,0:T(8,128)(2,1)S(1)}, bf16[640,384]{1,0:T(8,128)(2,1)}, u32[]{:S(2)}) copy-start(bf16[640,384]{1,0:T(8,128)(2,1)} %get-tuple-element.64) | copy-start | bytes 1474564
  98.8 37.0 %collective-permute-start.11 = (bf16[2,4,240,384]{3,2,1,0:T(8,128)(2,1)}, bf16[2,4,240,384]{3,2,1,0:T(8,128)(2,1)S(1)}, u32[]{:S(2)}, u32[]{:S(2)}) collective-permute-start(bf16[2,4,240,384]{3,2,1,0:T(8,128)(2,1)} %get-tuple-element.71.refs_10_), channel_id=1, source_target_pairs={{0,4},{4,0},{8,12},{12,8},{16,20},{20,16},{24,28},{28,24},{1,5},{5... | collective-permute-start | bytes 4423688 | tf_op jit(solution)/shard_map/ppermute | solution.py:926
  102.5 28.9 %collective-permute-start.9 = (bf16[2,4,192,384]{3,2,1,0:T(8,128)(2,1)}, bf16[2,4,192,384]{3,2,1,0:T(8,128)(2,1)S(1)}, u32[]{:S(2)}, u32[]{:S(2)}) collective-permute-start(bf16[2,4,192,384]{3,2,1,0:T(8,128)(2,1)} %get-tuple-element.67.refs_9_), channel_id=1, source_target_pairs={{0,2},{1,3},{2,0},{3,1},{4,6},{5,7},{6,4},{7,5},{8,10},{9,11},{10,... | collective-permute-start | bytes 3538952 | tf_op jit(solution)/shard_map/ppermute | solution.py:921
  104.7 1.9 collective-permute-start.2
  107.4 24.1 %copy-start.10 = (bf16[2,4,192,384]{3,2,1,0:T(8,128)(2,1)S(1)}, bf16[2,4,192,384]{3,2,1,0:T(8,128)(2,1)}, u32[]{:S(2)}) copy-start(bf16[2,4,192,384]{3,2,1,0:T(8,128)(2,1)} %get-tuple-element.75) | copy-start | bytes 3538948
  129.2 7.7 %copy-start.3 = (bf16[2,4,240,384]{3,2,1,0:T(8,128)(2,1)S(1)}, bf16[2,4,240,384]{3,2,1,0:T(8,128)(2,1)}, u32[]{:S(2)}) copy-start(bf16[2,4,240,384]{3,2,1,0:T(8,128)(2,1)} %get-tuple-element.76) | copy-start | bytes 4423684
  129.2 13.6 %collective-permute-start.13 = (bf16[3,384,640]{2,1,0:T(8,128)(2,1)}, bf16[3,384,640]{2,1,0:T(8,128)(2,1)}, u32[]{:S(2)}, u32[]{:S(2)}) collective-permute-start(bf16[3,384,640]{2,1,0:T(8,128)(2,1)} %get-tuple-element.72.refs_1_), channel_id=1, source_target_pairs={{0,1},{1,0},{2,3},{3,2},{4,5},{5,4},{6,7},{7,6},{8,9},{9,8},{10,11... | collective-permute-start | bytes 4423688 | tf_op jit(solution)/shard_map/ppermute | solution.py:921
  129.4 13.4 %collective-permute-start.8 = (bf16[3,384,640]{2,1,0:T(8,128)(2,1)}, bf16[3,384,640]{2,1,0:T(8,128)(2,1)S(1)}, u32[]{:S(2)}, u32[]{:S(2)}) collective-permute-start(bf16[3,384,640]{2,1,0:T(8,128)(2,1)} %get-tuple-element.73.refs_2_), channel_id=1, source_target_pairs={{0,1},{1,0},{2,3},{3,2},{4,5},{5,4},{6,7},{7,6},{8,9},{9,8},{10,11... | collective-permute-start | bytes 4423688 | tf_op jit(solution)/shard_map/ppermute | solution.py:921
  129.8 13.0 %collective-permute-start.14 = (bf16[640,384]{1,0:T(8,128)(2,1)}, bf16[640,384]{1,0:T(8,128)(2,1)}, u32[]{:S(2)}, u32[]{:S(2)}) collective-permute-start(bf16[640,384]{1,0:T(8,128)(2,1)} %get-tuple-element.77), channel_id=1, source_target_pairs={{0,1},{1,0},{2,3},{3,2},{4,5},{5,4},{6,7},{7,6},{8,9},{9,8},{10,11... | collective-permute-start | bytes 1474568 | tf_op jit(solution)/shard_map/ppermute | solution.py:921
  131.4 6.6 %copy-start.11 = (bf16[2,4,192,384]{3,2,1,0:T(8,128)(2,1)}, bf16[2,4,192,384]{3,2,1,0:T(8,128)(2,1)S(1)}, u32[]{:S(2)}) copy-start(bf16[2,4,192,384]{3,2,1,0:T(8,128)(2,1)S(1)} %collective-permute-done.9) | copy-start | bytes 3538948
  131.6 11.3 %copy-start.6 = (bf16[4,192,384]{2,1,0:T(8,128)(2,1)}, bf16[4,192,384]{2,1,0:T(8,128)(2,1)S(1)}, u32[]{:S(2)}) copy-start(bf16[4,192,384]{2,1,0:T(8,128)(2,1)S(1)} %fusion.2.refs_7_) | copy-start | bytes 1769476
  131.6 10.7 %copy-start.24 = (bf16[768]{0:T(1024)(128)(2,1)S(1)}, bf16[768]{0:T(1024)(128)(2,1)}, u32[]{:S(2)}) copy-start(bf16[768]{0:T(1024)(128)(2,1)} %param.32) | copy-start | bytes 4612
  131.6 21.4 %collective-permute-start.10 = (bf16[4,192,384]{2,1,0:T(8,128)(2,1)S(1)}, bf16[4,192,384]{2,1,0:T(8,128)(2,1)}, u32[]{:S(2)}, u32[]{:S(2)}) collective-permute-start(bf16[4,192,384]{2,1,0:T(8,128)(2,1)S(1)} %fusion.2.refs_7_), channel_id=1, source_target_pairs={{0,4},{4,0},{8,12},{12,8},{16,20},{20,16},{24,28},{28,24},{1,5},{5... | collective-permute-start | bytes 1769480 | tf_op jit(solution)/shard_map/ppermute | solution.py:926
  135.8 1.1 copy-start.8
  138.0 21.9 %collective-permute-start.12 = (bf16[4,240,384]{2,1,0:T(8,128)(2,1)}, bf16[4,240,384]{2,1,0:T(8,128)(2,1)}, u32[]{:S(2)}, u32[]{:S(2)}) collective-permute-start(bf16[4,240,384]{2,1,0:T(8,128)(2,1)} %fusion.refs_8_), channel_id=1, source_target_pairs={{0,2},{1,3},{2,0},{3,1},{4,6},{5,7},{6,4},{7,5},{8,10},{9,11},{10,... | collective-permute-start | bytes 2211848 | tf_op jit(solution)/shard_map/ppermute | solution.py:921
  142.9 1.2 copy-start.2
  152.9 20.8 %collective-permute-start.16 = (bf16[2,4,72,384]{3,2,1,0:T(8,128)(2,1)}, bf16[2,4,72,384]{3,2,1,0:T(8,128)(2,1)S(1)}, u32[]{:S(2)}, u32[]{:S(2)}) collective-permute-start(bf16[2,4,72,384]{3,2,1,0:T(8,128)(2,1)} %get-tuple-element.85), channel_id=1, source_target_pairs={{0,2},{1,3},{2,0},{3,1},{4,6},{5,7},{6,4},{7,5},{8,10},{9,11},{10,... | collective-permute-start | bytes 1327112 | tf_op jit(solution)/shard_map/ppermute | solution.py:921
  152.9 23.0 %collective-permute-start.18 = (bf16[2,4,72,384]{3,2,1,0:T(8,128)(2,1)}, bf16[2,4,72,384]{3,2,1,0:T(8,128)(2,1)S(1)}, u32[]{:S(2)}, u32[]{:S(2)}) collective-permute-start(bf16[2,4,72,384]{3,2,1,0:T(8,128)(2,1)} %get-tuple-element.87), channel_id=1, source_target_pairs={{0,4},{4,0},{8,12},{12,8},{16,20},{20,16},{24,28},{28,24},{1,5},{5... | collective-permute-start | bytes 1327112 | tf_op jit(solution)/shard_map/ppermute | solution.py:926
  161.2 23.8 %collective-permute-start.15 = (bf16[2,432,384]{2,1,0:T(8,128)(2,1)S(1)}, bf16[2,432,384]{2,1,0:T(8,128)(2,1)S(1)}, u32[]{:S(2)}, u32[]{:S(2)}) collective-permute-start(bf16[2,432,384]{2,1,0:T(8,128)(2,1)S(1)} %pad_maximum_fusion.refs_9_), channel_id=1, source_target_pairs={{0,8},{4,12},{8,0},{12,4},{16,24},{20,28},{24,16},{28,20},{1,9},{5... | collective-permute-start | bytes 1990664 | tf_op jit(solution)/shard_map/ppermute | solution.py:926
  173.7 12.4 %copy-start.17 = (bf16[2,4,72,384]{3,2,1,0:T(8,128)(2,1)}, bf16[2,4,72,384]{3,2,1,0:T(8,128)(2,1)S(1)}, u32[]{:S(2)}) copy-start(bf16[2,4,72,384]{3,2,1,0:T(8,128)(2,1)S(1)} %collective-permute-done.16) | copy-start | bytes 1327108
  174.9 6.0 %collective-permute-start.17 = (bf16[4,72,384]{2,1,0:T(8,128)(2,1)S(1)}, bf16[4,72,384]{2,1,0:T(8,128)(2,1)S(1)}, u32[]{:S(2)}, u32[]{:S(2)}) collective-permute-start(bf16[4,72,384]{2,1,0:T(8,128)(2,1)S(1)} %fusion.12), channel_id=1, source_target_pairs={{0,4},{4,0},{8,12},{12,8},{16,20},{20,16},{24,28},{28,24},{1,5},{5... | collective-permute-start | bytes 663560 | tf_op jit(solution)/shard_map/ppermute | solution.py:926
  176.0 11.3 %copy-start.18 = (bf16[2,4,72,384]{3,2,1,0:T(8,128)(2,1)}, bf16[2,4,72,384]{3,2,1,0:T(8,128)(2,1)S(1)}, u32[]{:S(2)}) copy-start(bf16[2,4,72,384]{3,2,1,0:T(8,128)(2,1)S(1)} %collective-permute-done.18) | copy-start | bytes 1327108
  177.1 6.0 %collective-permute-start.19 = (bf16[4,72,384]{2,1,0:T(8,128)(2,1)S(1)}, bf16[4,72,384]{2,1,0:T(8,128)(2,1)S(1)}, u32[]{:S(2)}, u32[]{:S(2)}) collective-permute-start(bf16[4,72,384]{2,1,0:T(8,128)(2,1)S(1)} %fusion.13), channel_id=1, source_target_pairs={{0,2},{1,3},{2,0},{3,1},{4,6},{5,7},{6,4},{7,5},{8,10},{9,11},{10,... | collective-permute-start | bytes 663560 | tf_op jit(solution)/shard_map/ppermute | solution.py:921
  183.1 21.3 %copy-start.19 = (bf16[4,72,384]{2,1,0:T(8,128)(2,1)}, bf16[4,72,384]{2,1,0:T(8,128)(2,1)S(1)}, u32[]{:S(2)}) copy-start(bf16[4,72,384]{2,1,0:T(8,128)(2,1)S(1)} %collective-permute-done.19) | copy-start | bytes 663556
  184.2 5.7 %copy-start.13 = (bf16[2,144,384]{2,1,0:T(8,128)(2,1)}, bf16[2,144,384]{2,1,0:T(8,128)(2,1)S(1)}, u32[]{:S(2)}) copy-start(bf16[2,144,384]{2,1,0:T(8,128)(2,1)S(1)} %pad_maximum_fusion.3.refs_11_) | copy-start | bytes 663556
  184.2 20.2 %collective-permute-start.20 = (bf16[2,144,384]{2,1,0:T(8,128)(2,1)S(1)}, bf16[2,144,384]{2,1,0:T(8,128)(2,1)}, u32[]{:S(2)}, u32[]{:S(2)}) collective-permute-start(bf16[2,144,384]{2,1,0:T(8,128)(2,1)S(1)} %pad_maximum_fusion.3.refs_11_), channel_id=1, source_target_pairs={{0,8},{4,12},{8,0},{12,4},{16,24},{20,28},{24,16},{28,20},{1,9},{5... | collective-permute-start | bytes 663560 | tf_op jit(solution)/shard_map/ppermute | solution.py:926
  187.3 2.6 %copy-start.9 = (bf16[1,432,384]{2,1,0:T(8,128)(2,1)}, bf16[1,432,384]{2,1,0:T(8,128)(2,1)S(1)}, u32[]{:S(2)}) copy-start(bf16[1,432,384]{2,1,0:T(8,128)(2,1)S(1)} %pad_maximum_fusion.1.refs_10_) | copy-start | bytes 995332
  187.3 29.6 %collective-permute-start.23 = (bf16[1,432,384]{2,1,0:T(8,128)(2,1)S(1)}, bf16[1,432,384]{2,1,0:T(8,128)(2,1)S(1)}, u32[]{:S(2)}, u32[]{:S(2)}) collective-permute-start(bf16[1,432,384]{2,1,0:T(8,128)(2,1)S(1)} %pad_maximum_fusion.1.refs_10_), channel_id=1, source_target_pairs={{0,16},{4,20},{8,24},{12,28},{16,0},{20,4},{24,8},{28,12},{1,17},{... | collective-permute-start | bytes 995336 | tf_op jit(solution)/shard_map/ppermute | solution.py:926
  201.2 10.6 %all-to-all-start = ((f32[32,1,432]{2,1,0:T(1,128)}), f32[32,1,432]{2,1,0:T(1,128)S(1)}, u32[]{:S(2)}, u32[]{:S(2)}) async-start(f32[32,1,432]{2,1,0:T(1,128)} %reshape.415), calls=%async_computation | async-start | bytes 131072 | tf_op jit(solution)/shard_map/all_to_all | solution.py:1119
  206.1 9.5 %collective-permute-start.21 = (bf16[1,144,384]{2,1,0:T(8,128)(2,1)}, bf16[1,144,384]{2,1,0:T(8,128)(2,1)}, u32[]{:S(2)}, u32[]{:S(2)}) collective-permute-start(bf16[1,144,384]{2,1,0:T(8,128)(2,1)} %pad_maximum_fusion.4), channel_id=1, source_target_pairs={{0,16},{4,20},{8,24},{12,28},{16,0},{20,4},{24,8},{28,12},{1,17},{... | collective-permute-start | bytes 331784 | tf_op jit(solution)/shard_map/ppermute | solution.py:926
  216.8 3.0 %collective-permute-start.22 = (f32[72,384]{1,0:T(8,128)S(1)}, f32[72,384]{1,0:T(8,128)S(1)}, u32[]{:S(2)}, u32[]{:S(2)}) collective-permute-start(f32[72,384]{1,0:T(8,128)S(1)} %get-tuple-element.93), channel_id=1, source_target_pairs={{0,1},{1,0},{2,3},{3,2},{4,5},{5,4},{6,7},{7,6},{8,9},{9,8},{10,11... | collective-permute-start | bytes 331784 | tf_op jit(solution)/shard_map/ppermute | solution.py:921
  219.3 1.7 collective-permute-start.24
  (4 other events, 3.4 us)

commit v3 on v2

--- a/solution.py
+++ b/solution.py
@@ -15,7 +15,7 @@
 NEG = -1e30
 F32 = jnp.float32
 BF16 = jnp.bfloat16
-VMEM_LIMIT = 56 * 1024 * 1024
+VMEM_LIMIT = 24 * 1024 * 1024
 
 
 def dot(left, right):
@@ -38,7 +38,7 @@
 
 
 def pass_rows(ids_ref, passes):
-    ids = ids_ref[...]
+    ids = ids_ref[...].reshape(1, -1)
     row = lax.broadcasted_iota(jnp.int32, (passes, ids.shape[1]), 0)
     return (row == ids).astype(F32).astype(BF16)
 
@@ -48,7 +48,8 @@
 
 
 def wide(item):
-    return item[...].astype(F32)
+    values = item[...].astype(F32)
+    return values if values.ndim == 2 else values.reshape(1, -1)
 
 
 def half_lanes(core, half):
@@ -210,7 +211,8 @@
     return jnp.concatenate([inside, inside], axis=1)
 
 
-def attend_kernel(pos, seg, keep, recv, own_out, far_out, lse_out, qkv, qq, vm, sc, acc, joined, start_ref, sems):
+def attend_kernel(pos, seg, keep, recv, *rest, ties):
+    own_out, far_out, lse_out, qkv, qq, vm, sc, acc, joined, start_ref, sems = rest[ties:]
     core = pos[0]
     rows = own_out.shape[0]
     pairs = own_out.shape[1] // PAIR
@@ -284,16 +286,20 @@
     far_out[...] = joined[pl.ds(pl.multiple_of((1 - core) * rows, 128), rows), :]
 
 
-def attend(pos, seg, keep, recv):
+def attend(pos, ties, seg, keep, recv):
     _, rows, half = keep.shape
     pairs = half // PAIR
     window = SEQ_LEN // BK
+
+    def kernel(*refs):
+        attend_kernel(*refs, ties=len(ties))
+
     return pl.pallas_call(
-        attend_kernel,
+        kernel,
         grid_spec=pltpu.PrefetchScalarGridSpec(
             num_scalar_prefetch=1,
             grid=(1,),
-            in_specs=[whole(seg.shape), ANY, ANY],
+            in_specs=[whole(seg.shape)] + [ANY] * (2 + len(ties)),
             out_specs=[
                 whole((rows, half)),
                 whole((rows, half)),
@@ -318,7 +324,7 @@
         compiler_params=params(),
         cost_estimate=cost(),
         name="attend",
-    )(pos, seg, keep, recv)
+    )(pos, seg, keep, recv, *ties)
 
 
 def attend_back_kernel(
@@ -691,14 +697,14 @@
     )(pos, act, act_far, grad, grad_far, *fixed, *ties)
 
 
-def out_weight_kernel(pos, branch, branch_far, own, far, keep_in, send_in, keep_out, send_out, rows_f32):
+def out_weight_kernel(pos, branch, branch_far, own, far, keep_in, send_in, tie, keep_out, send_out, rows_f32):
     per = rows_f32.shape[0] // 16
     rows_f32[...] = dot_tn(branch[...], own[...]) + dot_tn(branch_far[...], far[...])
     for x, y, z in chips():
         (keep_out, send_out)[y][x, z] = rows_of(rows_f32, chip_row(pos, x, y, z), per)
 
 
-def out_weight_call(pos, branch, branch_far, own, far, keep, send):
+def out_weight_call(pos, tie, branch, branch_far, own, far, keep, send):
     rows, width = branch.shape
     half = width // 2
     block = pl.BlockSpec((2, 4, width // 16, half), lambda i, s: (0, 0, 4, 0))
@@ -707,7 +713,7 @@
         grid_spec=pltpu.PrefetchScalarGridSpec(
             num_scalar_prefetch=1,
             grid=(1,),
-            in_specs=[whole(branch.shape)] * 2 + [whole(own.shape)] * 2 + [ANY, ANY],
+            in_specs=[whole(branch.shape)] * 2 + [whole(own.shape)] * 2 + [ANY] * 3,
             out_specs=[block, block],
             scratch_shapes=[pltpu.VMEM((width, half), F32)],
         ),
@@ -716,7 +722,7 @@
         compiler_params=params(),
         cost_estimate=cost(),
         name="out_weight",
-    )(pos, branch, branch_far, own, far, keep, send)
+    )(pos, branch, branch_far, own, far, keep, send, tie)
 
 
 def pack_sums(tables, long, packed):
@@ -1024,7 +1030,7 @@
     place = [core, x_bit, batch] if direct else [zero, zero, zero]
     pos = jnp.stack([core] + place + [x_bit])
 
-    row = lambda item: item.reshape(1, -1)
+    row = lambda item: item
     ids = row(pass_ids)
     gain_one, gain_two = row(norm1_gain), row(norm2_gain)
     cot_far = swap_head(cotangent, 1)
@@ -1034,11 +1040,11 @@
     recv = swap_head(send, 1)
     normed_far = swap_head(normed_send, 1)
     keep = qkv_keep(pos, normed, qkv_weight, qv_bias)
-    own, far_send, lse = attend(pos, segment_ids, keep, recv)
+    own, far_send, lse = attend(pos, (cot_far, normed_far), segment_ids, keep, recv)
     far = swap_head(far_send, 1)
     after, normed_two, normed_two_send, act_own, act_send, grad_pre, up_bias_grad = ff_first(
         pos, tokens, ids, pass_embed, own, far, out_weight, row(out_bias), gain_two, row(norm2_shift),
-        cotangent, up_weight, row(up_bias), down_weight,
+        cotangent, up_weight, up_bias.reshape(1, -1), down_weight,
     )
     act_far = swap_head(act_send, 1)
     grad_pre_far = swap_head(grad_pre, 1)
@@ -1051,7 +1057,7 @@
     down_keep, down_send, up_keep, up_send = middle_weights(
         pos, (), act_own, act_far, grad_pre, grad_pre_far, cotangent, cot_far, normed_two, normed_two_far
     )
-    up_keep, up_send = out_weight_call(pos, branch, branch_far, own, far_send, up_keep, up_send)
+    up_keep, up_send = out_weight_call(pos, grad_far, branch, branch_far, own, far_send, up_keep, up_send)
     if direct:
         left = Sum(down_keep, swap_x(down_send))
         right = Sum(up_keep, swap_y(up_send))

time: 225 us -> 193 us (0.86)
  Pallas kernels: 133 us -> 106 us
  other arithmetic: 19.1 us -> 16 us
  waiting for transfers between devices: 21.4 us -> 23.8 us
    reshape x8 -> x1, local copies, waits for them, and re-layouts: 6.75 us -> 0.01 us  [on_device(): up_bias.reshape(1, -1)]
    pallas_call x1, Pallas kernels: 19.9 us -> 14.4 us  [ff_first(): pl.pallas_call(ff_first_kernel, grid_spec=pltpu.PrefetchScalarGridSpec(nu...]
    unnamed x54 -> x106, local copies, waits for them, and re-layouts: 9.91 us -> 14.9 us
    pallas_call x1, Pallas kernels: 13.1 us -> 8.23 us  [ff_back(): pl.pallas_call(ff_back_kernel, grid_spec=pltpu.PrefetchScalarGridSpec(num...]
    pallas_call x1, Pallas kernels: 16.9 us -> 13.2 us  [middle_weights(): pl.pallas_call(kernel, grid_spec=pltpu.PrefetchScalarGridSpec(num_scalar_...]
    pallas_call x1, Pallas kernels: 9.34 us -> 6.18 us  [mixed_call(): pl.pallas_call(kernel, grid_spec=pltpu.PrefetchScalarGridSpec(num_scalar_...]
    pallas_call x1, Pallas kernels: 21.9 us -> 24.8 us  [attend_back(): pl.pallas_call(kernel, grid_spec=pltpu.PrefetchScalarGridSpec(num_scalar_...]
    pallas_call x1, Pallas kernels: 4.8 us -> 1.99 us  [out_weight_call(): pl.pallas_call(out_weight_kernel, grid_spec=pltpu.PrefetchScalarGridSpec(...]
  transfers between devices with their start and end apart: 26 -> 26, of which waited for: 9 -> 10; matrix products, arithmetic and copies ran while one was open for 11% -> 9% of each run, Pallas kernels for 39% -> 37%
where the time goes in v3:
time: 193 us; the launch traced here: 192 us
  Pallas kernels  106 us (55%)
  starting transfers between devices  26.4 us (14%)
  waiting for transfers between devices  23.8 us (12%)
  local copies, waits for them, and re-layouts  18 us (9%)
  other arithmetic  16 us (8%)
    pallas_call x1, Pallas kernels, attend_back(): pl.pallas_call(kernel, grid_spec=pltpu.PrefetchScalarGridSpec(num_scalar_...  24.8 us
    unnamed x106, local copies, waits for them, and re-layouts  14.9 us
    pallas_call x1, Pallas kernels, ff_first(): pl.pallas_call(ff_first_kernel, grid_spec=pltpu.PrefetchScalarGridSpec(nu...  14.4 us
    pallas_call x1, Pallas kernels, attend(): pl.pallas_call(kernel, grid_spec=pltpu.PrefetchScalarGridSpec(num_scalar_...  14.1 us
    ppermute x17, waiting for transfers between devices, swap_head(): return lax.ppermute(values, 'head', [(i, i ^ bit) for i in range(size)])  13.6 us
    pallas_call x1, Pallas kernels, middle_weights(): pl.pallas_call(kernel, grid_spec=pltpu.PrefetchScalarGridSpec(num_scalar_...  13.2 us
    ppermute x8, starting transfers between devices, swap_batch(): return lax.ppermute(values, 'batch', [(i, i ^ bit) for i in range(size)])  12.5 us
    ppermute x17, starting transfers between devices, swap_head(): return lax.ppermute(values, 'head', [(i, i ^ bit) for i in range(size)])  11.2 us
  transfers between devices with their start and end apart: 26, of which 10 were waited for; matrix products, arithmetic and copies ran while one was open for 9% of the time, Pallas kernels for 37%

profile of v3, /device:TPU:0, one launch (start us, length us, event | category | flops | bytes accessed | tf_op | source)
XLA Modules:
  0.0 191.6 jit_solution(3506226929146961749)
XLA Ops:
  0.8 2.0 %copy-done = bf16[768,2304]{1,0:T(8,128)(2,1)S(1)} copy-done((bf16[768,2304]{1,0:T(8,128)(2,1)S(1)}, bf16[768,2304]{1,0:T(8,128)(2,1)}, u32[]{:S(2)}) %copy-start) | copy-done | bytes 3538968
  2.8 1.2 copy-done.4
  7.4 3.9 %qkv_send.1 = (bf16[640,768]{1,0:T(8,128)(2,1)S(1)}, bf16[640,384]{1,0:T(8,128)(2,1)S(1)}, bf16[3,640,384]{2,1,0:T(8,128)(2,1)S(1)}) custom-call(s32[5]{0:T(128)S(1)} %stack.20.pos.refs_0_, bf16[640,768]{1,0:T(8,128)(2,1)S(1)} %copy-done.4, s32[640]{0:T(1024)S(1)} %copy-done.26, bf16[5,768]{1,0:T(8,128)(2,1)S(1)} %copy-done.23, ...), custom_call_target="tpu_custom_call" | custom-call | flops 1000 | bytes 1000 | tf_op jit(solution)/shard_map/qkv_send/pallas_call | solution.py:105
  12.4 2.8 %qkv_keep.1.refs_2_.refs_3_ = bf16[3,640,384]{2,1,0:T(8,128)(2,1)S(1)} custom-call(s32[5]{0:T(128)S(1)} %stack.20.pos.refs_0_, bf16[640,768]{1,0:T(8,128)(2,1)S(1)} %get-tuple-element.54.normed.refs_5_, bf16[768,2304]{1,0:T(8,128)(2,1)S(1)} %copy-done.1, bf16[2,768]{1,0:T(2,128)(2,1)S(1)} %copy-done.33), custom_call_target="tpu_custom_call" | custom-call | flops 1000 | bytes 1000 | tf_op jit(solution)/shard_map/qkv_keep/pallas_call | solution.py:139
  15.3 1.6 collective-permute-done.2.refs_5_.refs_6_
  16.9 14.1 %attend.1 = (bf16[640,384]{1,0:T(8,128)(2,1)S(1)}, bf16[640,384]{1,0:T(8,128)(2,1)S(1)}, f32[5,3,1,512]{3,2,1,0:T(1,128)S(1)}) custom-call(s32[5]{0:T(128)S(1)} %stack.20.pos.refs_0_, s32[2,1280]{1,0:T(2,128)S(1)} %copy-done.25, bf16[3,640,384]{2,1,0:T(8,128)(2,1)S(1)} %qkv_keep.1.refs_2_.refs_3_, ...), custom_call_target="tpu_custom_call" | custom-call | flops 1000 | bytes 1000 | tf_op jit(solution)/shard_map/attend/pallas_call | solution.py:297
  31.5 1.5 collective-permute-done.3.far
  33.1 1.3 copy-done.11
  34.3 14.4 %ff_first.1 = (f32[640,768]{1,0:T(8,128)S(1)}, bf16[640,768]{1,0:T(8,128)(2,1)S(1)}, bf16[640,384]{1,0:T(8,128)(2,1)S(1)}, bf16[640,1536]{1,0:T(8,128)(2,1)S(1)}...) custom-call(s32[5]{0:T(128)S(1)} %stack.20.pos.refs_0_, ...), custom_call_target="tpu_custom_call" | custom-call | flops 1000 | bytes 1000 | tf_op jit(solution)/shard_map/ff_first/pallas_call | solution.py:510
  49.8 8.2 %ff_back.1 = (f32[640,768]{1,0:T(8,128)S(1)}, bf16[640,768]{1,0:T(8,128)(2,1)S(1)}, bf16[640,384]{1,0:T(8,128)(2,1)S(1)}, bf16[640,384]{1,0:T(8,128)(2,1)S(1)}, f32[4,768]{1,0:T(4,128)S(1)}) custom-call(s32[5]{0:T(128)S(1)} %stack.20.pos.refs_0_, bf16[640,3072]{1,0:T(8,128)(2,1)S(1)} %get-tuple-element.63.grad_pre.refs_3_, bf16[768,3072]{1,0:T(8,128)(2,1)S(1)} %bitcast.121, ...), custom_call_target="tpu_custom_call" | custom-call | flops 1000 | bytes 1000 | tf_op jit(solution)/shard_map/ff_back/pallas_call | solution.py:596
  58.1 1.3 copy-done.18
  60.3 2.4 %collective-permute-done.7.refs_8_ = bf16[640,384]{1,0:T(8,128)(2,1)S(1)} collective-permute-done((bf16[640,384]{1,0:T(8,128)(2,1)S(1)}, bf16[640,384]{1,0:T(8,128)(2,1)S(1)}, u32[]{:S(2)}, u32[]{:S(2)}) %collective-permute-start.7) | collective-permute-done | bytes 491552 | tf_op jit(solution)/shard_map/ppermute | solution.py:927
  62.7 13.2 %middle_weights.1 = (bf16[2,4,192,384]{3,2,1,0:T(8,128)(2,1)S(1)}, bf16[2,4,192,384]{3,2,1,0:T(8,128)(2,1)S(1)}, bf16[2,4,240,384]{3,2,1,0:T(8,128)(2,1)S(1)}, bf16[2,4,240,384]{3,2,1,0:T(8,128)(2,1)S(1)}) custom-call(s32[5]{0:T(128)S(1)} %stack.20.pos.refs_0_, bf16[640,1536]{1,0:T(8,128)(2,1)S(1)} %get-tuple-element.60.refs_1_.refs_2_, ...), custom_call_target="tpu_custom_call" | custom-call | flops 1000 | bytes 1000 | tf_op jit(solution)/shard_map/middle_weights/pallas_call | solution.py:680
  75.9 2.0 %out_weight.1 = (bf16[2,4,240,384]{3,2,1,0:T(8,128)(2,1)S(1)}, bf16[2,4,240,384]{3,2,1,0:T(8,128)(2,1)S(1)}) custom-call(s32[5]{0:T(128)S(1)} %stack.20.pos.refs_0_, bf16[640,768]{1,0:T(8,128)(2,1)S(1)} %get-tuple-element.69.branch, bf16[640,768]{1,0:T(8,128)(2,1)S(1)} %collective-permute-done.8.branch_far, ...), custom_call_target="tpu_custom_call", output_to_operand_aliasing={{0}: (5, {}), {1}: (6, {})} | custom-call | flops 1000 | bytes 1000 | tf_op jit(solution)/shard_map/out_weight/pallas_call | solution.py:711
  77.9 1.3 collective-permute-start.12
  79.2 2.0 %collective-permute-start.10 = (bf16[2,4,192,384]{3,2,1,0:T(8,128)(2,1)S(1)}, bf16[2,4,192,384]{3,2,1,0:T(8,128)(2,1)S(1)}, u32[]{:S(2)}, u32[]{:S(2)}) collective-permute-start(bf16[2,4,192,384]{3,2,1,0:T(8,128)(2,1)S(1)} %get-tuple-element.68.refs_9_), channel_id=1, source_target_pairs={{0,2},{1,3},{2,0},{3,1},{4,6},{5,7},{6,4},{7,5},{8,10},{9,11},{10,... | collective-permute-start | bytes 3538952 | tf_op jit(solution)/shard_map/ppermute | solution.py:927
  81.2 24.8 %attend_back.1 = (bf16[3,384,640]{2,1,0:T(8,128)(2,1)}, bf16[3,384,640]{2,1,0:T(8,128)(2,1)}) custom-call(s32[5]{0:T(128)S(1)} %stack.20.pos.refs_0_, s32[2,1280]{1,0:T(2,128)S(1)} %copy-done.25, f32[5,3,1,512]{3,2,1,0:T(1,128)S(1)} %get-tuple-element.62.refs_2_, bf16[3,640,384]{2,1,0:T(8,128)(2,1)S(1)} %qkv_keep.1.refs_2_.refs_3_, ...), custom_call_target="tpu_custom_call" | custom-call | flops 1000 | bytes 1000 | tf_op jit(solution)/shard_map/attend_back/pallas_call | solution.py:419
  107.2 1.1 fusion.2.refs_7_
  108.4 1.6 collective-permute-start.11
  110.0 3.1 %collective-permute-done.12 = bf16[2,4,240,384]{3,2,1,0:T(8,128)(2,1)S(1)} collective-permute-done((bf16[2,4,240,384]{3,2,1,0:T(8,128)(2,1)S(1)}, bf16[2,4,240,384]{3,2,1,0:T(8,128)(2,1)S(1)}, u32[]{:S(2)}, u32[]{:S(2)}) %collective-permute-start.12) | collective-permute-done | bytes 1474592 | tf_op jit(solution)/shard_map/ppermute | solution.py:932
  113.1 1.2 fusion.refs_8_
  114.5 2.8 %collective-permute-start.13 = (bf16[4,240,384]{2,1,0:T(8,128)(2,1)}, bf16[4,240,384]{2,1,0:T(8,128)(2,1)}, u32[]{:S(2)}, u32[]{:S(2)}) collective-permute-start(bf16[4,240,384]{2,1,0:T(8,128)(2,1)} %fusion.refs_8_), channel_id=1, source_target_pairs={{0,2},{1,3},{2,0},{3,1},{4,6},{5,7},{6,4},{7,5},{8,10},{9,11},{10,... | collective-permute-start | bytes 2211848 | tf_op jit(solution)/shard_map/ppermute | solution.py:927
  117.3 1.2 copy-done.15
  118.5 1.0 copy-done.21
  119.6 6.9 %qkv_weight.1 = (bf16[2,4,72,384]{3,2,1,0:T(8,128)(2,1)S(1)}, bf16[2,4,72,384]{3,2,1,0:T(8,128)(2,1)S(1)}, bf16[2,4,72,384]{3,2,1,0:T(8,128)(2,1)S(1)}, bf16[2,4,72,384]{3,2,1,0:T(8,128)(2,1)S(1)}, f32[3,768]{1,0:T(4,128)S(1)}) custom-call(s32[5]{0:T(128)S(1)} %stack.20.pos.refs_0_, bf16[3,384,640]{2,1,0:T(8,128)(2,1)} %get-tuple-element.73.refs_1_, ...), custom_call_target="tpu_custom_call" | custom-call | flops 1000 | bytes 1000 | tf_op jit(solution)/shard_map/qkv_weight/pallas_call | solution.py:838
  127.1 1.4 fusion.3
  128.5 6.5 %collective-permute-done.13 = bf16[4,240,384]{2,1,0:T(8,128)(2,1)} collective-permute-done((bf16[4,240,384]{2,1,0:T(8,128)(2,1)}, bf16[4,240,384]{2,1,0:T(8,128)(2,1)}, u32[]{:S(2)}, u32[]{:S(2)}) %collective-permute-start.13) | collective-permute-done | bytes 737312 | tf_op jit(solution)/shard_map/ppermute | solution.py:927
  135.0 1.3 fusion.1
  136.4 2.2 %collective-permute-start.15 = (bf16[2,432,384]{2,1,0:T(8,128)(2,1)S(1)}, bf16[2,432,384]{2,1,0:T(8,128)(2,1)S(1)}, u32[]{:S(2)}, u32[]{:S(2)}) collective-permute-start(bf16[2,432,384]{2,1,0:T(8,128)(2,1)S(1)} %pad_maximum_fusion.refs_9_), channel_id=1, source_target_pairs={{0,8},{4,12},{8,0},{12,4},{16,24},{20,28},{24,16},{28,20},{1,9},{5... | collective-permute-start | bytes 1990664 | tf_op jit(solution)/shard_map/ppermute | solution.py:932
  138.6 9.5 %input_back.1 = (f32[640,768]{1,0:T(8,128)}, f32[7,768]{1,0:T(8,128)S(1)}, bf16[2,4,72,384]{3,2,1,0:T(8,128)(2,1)S(1)}, bf16[2,4,72,384]{3,2,1,0:T(8,128)(2,1)S(1)}) custom-call(s32[5]{0:T(128)S(1)} %stack.20.pos.refs_0_, bf16[3,384,640]{2,1,0:T(8,128)(2,1)} %get-tuple-element.73.refs_1_, ...), custom_call_target="tpu_custom_call", output_to_operand_aliasing={{2}: (10, {}), {3}: (11, {})} | custom-call | flops 1000 | bytes 1000 | tf_op jit(solution)/shard_map/input_back/pallas_call | solution.py:906
  148.8 2.1 %collective-permute-start.19 = (bf16[4,72,384]{2,1,0:T(8,128)(2,1)S(1)}, bf16[4,72,384]{2,1,0:T(8,128)(2,1)S(1)}, u32[]{:S(2)}, u32[]{:S(2)}) collective-permute-start(bf16[4,72,384]{2,1,0:T(8,128)(2,1)S(1)} %fusion.13), channel_id=1, source_target_pairs={{0,2},{1,3},{2,0},{3,1},{4,6},{5,7},{6,4},{7,5},{8,10},{9,11},{10,... | collective-permute-start | bytes 663560 | tf_op jit(solution)/shard_map/ppermute | solution.py:927
  150.9 3.4 %collective-permute-done.17 = bf16[4,72,384]{2,1,0:T(8,128)(2,1)S(1)} collective-permute-done((bf16[4,72,384]{2,1,0:T(8,128)(2,1)S(1)}, bf16[4,72,384]{2,1,0:T(8,128)(2,1)S(1)}, u32[]{:S(2)}, u32[]{:S(2)}) %collective-permute-start.17) | collective-permute-done | bytes 221216 | tf_op jit(solution)/shard_map/ppermute | solution.py:932
  155.5 1.4 fusion.7
  157.0 1.1 fusion.11
  158.1 3.2 %collective-permute-start.23 = (bf16[1,432,384]{2,1,0:T(8,128)(2,1)S(1)}, bf16[1,432,384]{2,1,0:T(8,128)(2,1)S(1)}, u32[]{:S(2)}, u32[]{:S(2)}) collective-permute-start(bf16[1,432,384]{2,1,0:T(8,128)(2,1)S(1)} %pad_maximum_fusion.1.refs_10_), channel_id=1, source_target_pairs={{0,16},{4,20},{8,24},{12,28},{16,0},{20,4},{24,8},{28,12},{1,17},{... | collective-permute-start | bytes 995336 | tf_op jit(solution)/shard_map/ppermute | solution.py:932
  161.4 6.2 %mixed.1 = (bf16[640,768]{1,0:T(8,128)(2,1)}, f32[32,18,24]{2,1,0:T(8,128)S(1)}, bf16[2,4,72,384]{3,2,1,0:T(8,128)(2,1)S(1)}, bf16[2,4,72,384]{3,2,1,0:T(8,128)(2,1)S(1)}) custom-call(s32[5]{0:T(128)S(1)} %stack.20.pos.refs_0_, bf16[640,1536]{1,0:T(8,128)(2,1)S(1)} %copy-done.17, ...), custom_call_target="tpu_custom_call", output_to_operand_aliasing={{2}: (12, {}), {3}: (13, {})} | custom-call | flops 1000 | bytes 1000 | tf_op jit(solution)/shard_map/mixed/pallas_call | solution.py:772
  167.6 0.8 copy-done.12
  168.3 0.8 copy-done.13
  169.1 1.0 reshape.387
  170.1 2.7 %all-to-all-start = ((f32[32,1,432]{2,1,0:T(1,128)}), f32[32,1,432]{2,1,0:T(1,128)S(1)}, u32[]{:S(2)}, u32[]{:S(2)}) async-start(f32[32,1,432]{2,1,0:T(1,128)} %reshape.387), calls=%async_computation | async-start | bytes 131072 | tf_op jit(solution)/shard_map/all_to_all | solution.py:1125
  172.8 1.0 fusion.21
  173.8 2.7 %collective-permute-start.21 = (bf16[1,144,384]{2,1,0:T(8,128)(2,1)S(1)}, bf16[1,144,384]{2,1,0:T(8,128)(2,1)S(1)}, u32[]{:S(2)}, u32[]{:S(2)}) collective-permute-start(bf16[1,144,384]{2,1,0:T(8,128)(2,1)S(1)} %pad_maximum_fusion.4), channel_id=1, source_target_pairs={{0,16},{4,20},{8,24},{12,28},{16,0},{20,4},{24,8},{28,12},{1,17},{... | collective-permute-start | bytes 331784 | tf_op jit(solution)/shard_map/ppermute | solution.py:932
  176.5 3.7 %all-to-all-done = f32[32,1,432]{2,1,0:T(1,128)S(1)} async-done(((f32[32,1,432]{2,1,0:T(1,128)}), f32[32,1,432]{2,1,0:T(1,128)S(1)}, u32[]{:S(2)}, u32[]{:S(2)}) %all-to-all-start) | async-done | bytes 55328 | tf_op jit(solution)/shard_map/all_to_all | solution.py:1125
  180.7 0.8 reduce
  184.0 1.0 select_bitcast_fusion.1
  185.2 1.2 fusion.5
  186.5 1.2 fusion.9
  189.5 0.7 copy.39
  (164 shorter events, 17.5 us)
Async XLA Ops:
  11.3 5.6 %collective-permute-start = (bf16[3,640,384]{2,1,0:T(8,128)(2,1)S(1)}, bf16[3,640,384]{2,1,0:T(8,128)(2,1)S(1)}, u32[]{:S(2)}, u32[]{:S(2)}) collective-permute-start(bf16[3,640,384]{2,1,0:T(8,128)(2,1)S(1)} %get-tuple-element.55), channel_id=1, source_target_pairs={{0,1},{1,0},{2,3},{3,2},{4,5},{5,4},{6,7},{7,6},{8,9},{9,8},{10,11... | collective-permute-start | bytes 4423688 | tf_op jit(solution)/shard_map/ppermute | solution.py:927
  11.9 5.0 %collective-permute-start.1 = (bf16[640,768]{1,0:T(8,128)(2,1)S(1)}, bf16[640,768]{1,0:T(8,128)(2,1)S(1)}, u32[]{:S(2)}, u32[]{:S(2)}) collective-permute-start(bf16[640,768]{1,0:T(8,128)(2,1)S(1)} %copy-done.3), channel_id=1, source_target_pairs={{0,1},{1,0},{2,3},{3,2},{4,5},{5,4},{6,7},{7,6},{8,9},{9,8},{10,11... | collective-permute-start | bytes 2949128 | tf_op jit(solution)/shard_map/ppermute | solution.py:927
  12.0 4.9 %collective-permute-start.2 = (bf16[640,384]{1,0:T(8,128)(2,1)S(1)}, bf16[640,384]{1,0:T(8,128)(2,1)S(1)}, u32[]{:S(2)}, u32[]{:S(2)}) collective-permute-start(bf16[640,384]{1,0:T(8,128)(2,1)S(1)} %get-tuple-element.56), channel_id=1, source_target_pairs={{0,1},{1,0},{2,3},{3,2},{4,5},{5,4},{6,7},{7,6},{8,9},{9,8},{10,11... | collective-permute-start | bytes 1474568 | tf_op jit(solution)/shard_map/ppermute | solution.py:927
  12.4 20.6 %slice-start = ((s8[4718592]{0:T(1024)(128)(4,1)}), s8[4194304]{0:T(1024)(128)(4,1)S(1)}, s32[]{:S(2)}) async-start(s8[4718592]{0:T(1024)(128)(4,1)} %bitcast.120), calls=%async_computation.1 | async-start | bytes 8388608
  12.4 20.6 %slice-start.1 = ((s8[4718592]{0:T(1024)(128)(4,1)}), s8[524288]{0:T(1024)(128)(4,1)S(1)}, s32[]{:S(2)}) async-start(s8[4718592]{0:T(1024)(128)(4,1)} %bitcast.120), calls=%async_computation.2 | async-start | bytes 1048576
  12.4 20.6 %copy-start.2 = (bf16[3072,768]{1,0:T(8,128)(2,1)S(1)}, bf16[3072,768]{1,0:T(8,128)(2,1)}, u32[]{:S(2)}) copy-start(bf16[3072,768]{1,0:T(8,128)(2,1)} %refs_3_.3) | copy-start | bytes 14155780
  15.2 16.3 %copy-start.47 = (bf16[3072]{0:T(1024)(128)(2,1)S(1)}, bf16[3072]{0:T(1024)(128)(2,1)}, u32[]{:S(2)}) copy-start(bf16[3072]{0:T(1024)(128)(2,1)} %param.30) | copy-start | bytes 18436
  15.3 17.7 %copy-start.24 = (bf16[5,768]{1,0:T(8,128)(2,1)S(1)}, bf16[5,768]{1,0:T(8,128)(2,1)}, u32[]{:S(2)}) copy-start(bf16[5,768]{1,0:T(8,128)(2,1)} %refs_6_.1) | copy-start | bytes 23044
  15.3 17.7 %copy-start.27 = (s32[640]{0:T(1024)S(1)}, s32[640]{0:T(1024)}, u32[]{:S(2)}) copy-start(s32[640]{0:T(1024)} %refs_5_.4) | copy-start | bytes 7684
  15.3 17.7 %copy-start.34 = (bf16[768]{0:T(1024)(128)(2,1)S(1)}, bf16[768]{0:T(1024)(128)(2,1)}, u32[]{:S(2)}) copy-start(bf16[768]{0:T(1024)(128)(2,1)} %gain.5) | copy-start | bytes 4612
  15.3 17.7 %copy-start.38 = (bf16[768]{0:T(1024)(128)(2,1)S(1)}, bf16[768]{0:T(1024)(128)(2,1)}, u32[]{:S(2)}) copy-start(bf16[768]{0:T(1024)(128)(2,1)} %bias.5) | copy-start | bytes 4612
  15.3 17.7 %copy-start.39 = (bf16[768]{0:T(1024)(128)(2,1)S(1)}, bf16[768]{0:T(1024)(128)(2,1)}, u32[]{:S(2)}) copy-start(bf16[768]{0:T(1024)(128)(2,1)} %shift.3) | copy-start | bytes 4612
  16.9 14.2 %copy-start.20 = (bf16[640,384]{1,0:T(8,128)(2,1)}, bf16[640,384]{1,0:T(8,128)(2,1)S(1)}, u32[]{:S(2)}) copy-start(bf16[640,384]{1,0:T(8,128)(2,1)S(1)} %collective-permute-done.2.refs_5_.refs_6_) | copy-start | bytes 1474564
  31.1 1.9 %collective-permute-start.3 = (bf16[640,384]{1,0:T(8,128)(2,1)S(1)}, bf16[640,384]{1,0:T(8,128)(2,1)S(1)}, u32[]{:S(2)}, u32[]{:S(2)}) collective-permute-start(bf16[640,384]{1,0:T(8,128)(2,1)S(1)} %get-tuple-element.58.far.refs_6_), channel_id=1, source_target_pairs={{0,1},{1,0},{2,3},{3,2},{4,5},{5,4},{6,7},{7,6},{8,9},{9,8},{10,11... | collective-permute-start | bytes 1474568 | tf_op jit(solution)/shard_map/ppermute | solution.py:927
  49.3 13.3 %copy-start.8 = (bf16[640,1536]{1,0:T(8,128)(2,1)}, bf16[640,1536]{1,0:T(8,128)(2,1)S(1)}, u32[]{:S(2)}) copy-start(bf16[640,1536]{1,0:T(8,128)(2,1)S(1)} %get-tuple-element.60.refs_1_.refs_2_) | copy-start | bytes 5898244
  49.3 13.3 %collective-permute-start.6 = (bf16[640,3072]{1,0:T(8,128)(2,1)S(1)}, bf16[640,3072]{1,0:T(8,128)(2,1)S(1)}, u32[]{:S(2)}, u32[]{:S(2)}) collective-permute-start(bf16[640,3072]{1,0:T(8,128)(2,1)S(1)} %get-tuple-element.63.grad_pre.refs_3_), channel_id=1, source_target_pairs={{0,1},{1,0},{2,3},{3,2},{4,5},{5,4},{6,7},{7,6},{8,9},{9,8},{10,11... | collective-permute-start | bytes 11796488 | tf_op jit(solution)/shard_map/ppermute | solution.py:927
  49.7 12.9 %collective-permute-start.5 = (bf16[640,1536]{1,0:T(8,128)(2,1)S(1)}, bf16[640,1536]{1,0:T(8,128)(2,1)S(1)}, u32[]{:S(2)}, u32[]{:S(2)}) collective-permute-start(bf16[640,1536]{1,0:T(8,128)(2,1)S(1)} %get-tuple-element.59.refs_1_), channel_id=1, source_target_pairs={{0,1},{1,0},{2,3},{3,2},{4,5},{5,4},{6,7},{7,6},{8,9},{9,8},{10,11... | collective-permute-start | bytes 5898248 | tf_op jit(solution)/shard_map/ppermute | solution.py:927
  59.4 16.5 %copy-start.31 = (f32[4,768]{1,0:T(4,128)}, f32[4,768]{1,0:T(4,128)S(1)}, u32[]{:S(2)}) copy-start(f32[4,768]{1,0:T(4,128)S(1)} %get-tuple-element.82.refs_8_) | copy-start | bytes 36868
  59.4 16.5 %collective-permute-start.8 = (bf16[640,768]{1,0:T(8,128)(2,1)S(1)}, bf16[640,768]{1,0:T(8,128)(2,1)S(1)}, u32[]{:S(2)}, u32[]{:S(2)}) collective-permute-start(bf16[640,768]{1,0:T(8,128)(2,1)S(1)} %get-tuple-element.69.branch), channel_id=1, source_target_pairs={{0,1},{1,0},{2,3},{3,2},{4,5},{5,4},{6,7},{7,6},{8,9},{9,8},{10,11... | collective-permute-start | bytes 2949128 | tf_op jit(solution)/shard_map/ppermute | solution.py:927
  59.7 2.9 %collective-permute-start.7 = (bf16[640,384]{1,0:T(8,128)(2,1)S(1)}, bf16[640,384]{1,0:T(8,128)(2,1)S(1)}, u32[]{:S(2)}, u32[]{:S(2)}) collective-permute-start(bf16[640,384]{1,0:T(8,128)(2,1)S(1)} %get-tuple-element.67), channel_id=1, source_target_pairs={{0,1},{1,0},{2,3},{3,2},{4,5},{5,4},{6,7},{7,6},{8,9},{9,8},{10,11... | collective-permute-start | bytes 1474568 | tf_op jit(solution)/shard_map/ppermute | solution.py:927
  59.9 16.0 %collective-permute-start.4 = (bf16[640,384]{1,0:T(8,128)(2,1)S(1)}, bf16[640,384]{1,0:T(8,128)(2,1)S(1)}, u32[]{:S(2)}, u32[]{:S(2)}) collective-permute-start(bf16[640,384]{1,0:T(8,128)(2,1)S(1)} %get-tuple-element.65), channel_id=1, source_target_pairs={{0,1},{1,0},{2,3},{3,2},{4,5},{5,4},{6,7},{7,6},{8,9},{9,8},{10,11... | collective-permute-start | bytes 1474568 | tf_op jit(solution)/shard_map/ppermute | solution.py:927
  75.8 31.4 %copy-start.22 = (bf16[2,4,192,384]{3,2,1,0:T(8,128)(2,1)}, bf16[2,4,192,384]{3,2,1,0:T(8,128)(2,1)S(1)}, u32[]{:S(2)}) copy-start(bf16[2,4,192,384]{3,2,1,0:T(8,128)(2,1)S(1)} %get-tuple-element.76) | copy-start | bytes 3538948
  77.9 35.2 %copy-start.10 = (bf16[2,4,240,384]{3,2,1,0:T(8,128)(2,1)}, bf16[2,4,240,384]{3,2,1,0:T(8,128)(2,1)S(1)}, u32[]{:S(2)}) copy-start(bf16[2,4,240,384]{3,2,1,0:T(8,128)(2,1)S(1)} %get-tuple-element.77) | copy-start | bytes 4423684
  77.9 35.2 %collective-permute-start.12 = (bf16[2,4,240,384]{3,2,1,0:T(8,128)(2,1)S(1)}, bf16[2,4,240,384]{3,2,1,0:T(8,128)(2,1)S(1)}, u32[]{:S(2)}, u32[]{:S(2)}) collective-permute-start(bf16[2,4,240,384]{3,2,1,0:T(8,128)(2,1)S(1)} %get-tuple-element.72.refs_10_), channel_id=1, source_target_pairs={{0,4},{4,0},{8,12},{12,8},{16,20},{20,16},{24,28},{28,24},{1,5},{5... | collective-permute-start | bytes 4423688 | tf_op jit(solution)/shard_map/ppermute | solution.py:932
  79.2 28.0 %collective-permute-start.10 = (bf16[2,4,192,384]{3,2,1,0:T(8,128)(2,1)S(1)}, bf16[2,4,192,384]{3,2,1,0:T(8,128)(2,1)S(1)}, u32[]{:S(2)}, u32[]{:S(2)}) collective-permute-start(bf16[2,4,192,384]{3,2,1,0:T(8,128)(2,1)S(1)} %get-tuple-element.68.refs_9_), channel_id=1, source_target_pairs={{0,2},{1,3},{2,0},{3,1},{4,6},{5,7},{6,4},{7,5},{8,10},{9,11},{10,... | collective-permute-start | bytes 3538952 | tf_op jit(solution)/shard_map/ppermute | solution.py:927
  106.0 11.4 %collective-permute-start.14 = (bf16[3,384,640]{2,1,0:T(8,128)(2,1)}, bf16[3,384,640]{2,1,0:T(8,128)(2,1)}, u32[]{:S(2)}, u32[]{:S(2)}) collective-permute-start(bf16[3,384,640]{2,1,0:T(8,128)(2,1)} %get-tuple-element.73.refs_1_), channel_id=1, source_target_pairs={{0,1},{1,0},{2,3},{3,2},{4,5},{5,4},{6,7},{7,6},{8,9},{9,8},{10,11... | collective-permute-start | bytes 4423688 | tf_op jit(solution)/shard_map/ppermute | solution.py:927
  106.1 11.3 %collective-permute-start.9 = (bf16[3,384,640]{2,1,0:T(8,128)(2,1)}, bf16[3,384,640]{2,1,0:T(8,128)(2,1)}, u32[]{:S(2)}, u32[]{:S(2)}) collective-permute-start(bf16[3,384,640]{2,1,0:T(8,128)(2,1)} %get-tuple-element.74.refs_2_), channel_id=1, source_target_pairs={{0,1},{1,0},{2,3},{3,2},{4,5},{5,4},{6,7},{7,6},{8,9},{9,8},{10,11... | collective-permute-start | bytes 4423688 | tf_op jit(solution)/shard_map/ppermute | solution.py:927
  108.4 18.7 %collective-permute-start.11 = (bf16[4,192,384]{2,1,0:T(8,128)(2,1)}, bf16[4,192,384]{2,1,0:T(8,128)(2,1)}, u32[]{:S(2)}, u32[]{:S(2)}) collective-permute-start(bf16[4,192,384]{2,1,0:T(8,128)(2,1)} %fusion.2.refs_7_), channel_id=1, source_target_pairs={{0,4},{4,0},{8,12},{12,8},{16,20},{20,16},{24,28},{28,24},{1,5},{5... | collective-permute-start | bytes 1769480 | tf_op jit(solution)/shard_map/ppermute | solution.py:932
  114.5 20.5 %collective-permute-start.13 = (bf16[4,240,384]{2,1,0:T(8,128)(2,1)}, bf16[4,240,384]{2,1,0:T(8,128)(2,1)}, u32[]{:S(2)}, u32[]{:S(2)}) collective-permute-start(bf16[4,240,384]{2,1,0:T(8,128)(2,1)} %fusion.refs_8_), channel_id=1, source_target_pairs={{0,2},{1,3},{2,0},{3,1},{4,6},{5,7},{6,4},{7,5},{8,10},{9,11},{10,... | collective-permute-start | bytes 2211848 | tf_op jit(solution)/shard_map/ppermute | solution.py:927
  126.5 21.7 %collective-permute-start.16 = (bf16[2,4,72,384]{3,2,1,0:T(8,128)(2,1)S(1)}, bf16[2,4,72,384]{3,2,1,0:T(8,128)(2,1)S(1)}, u32[]{:S(2)}, u32[]{:S(2)}) collective-permute-start(bf16[2,4,72,384]{3,2,1,0:T(8,128)(2,1)S(1)} %get-tuple-element.85), channel_id=1, source_target_pairs={{0,2},{1,3},{2,0},{3,1},{4,6},{5,7},{6,4},{7,5},{8,10},{9,11},{10,... | collective-permute-start | bytes 1327112 | tf_op jit(solution)/shard_map/ppermute | solution.py:927
  126.6 22.1 %collective-permute-start.18 = (bf16[2,4,72,384]{3,2,1,0:T(8,128)(2,1)S(1)}, bf16[2,4,72,384]{3,2,1,0:T(8,128)(2,1)S(1)}, u32[]{:S(2)}, u32[]{:S(2)}) collective-permute-start(bf16[2,4,72,384]{3,2,1,0:T(8,128)(2,1)S(1)} %get-tuple-element.87), channel_id=1, source_target_pairs={{0,4},{4,0},{8,12},{12,8},{16,20},{20,16},{24,28},{28,24},{1,5},{5... | collective-permute-start | bytes 1327112 | tf_op jit(solution)/shard_map/ppermute | solution.py:932
  127.1 11.5 %copy-start.19 = (f32[640,768]{1,0:T(8,128)S(1)}, f32[640,768]{1,0:T(8,128)}, u32[]{:S(2)}) copy-start(f32[640,768]{1,0:T(8,128)} %copy-done.18) | copy-start | bytes 5898244
  128.5 10.1 %copy-start.5 = (bf16[640,768]{1,0:T(8,128)(2,1)S(1)}, bf16[640,768]{1,0:T(8,128)(2,1)}, u32[]{:S(2)}) copy-start(bf16[640,768]{1,0:T(8,128)(2,1)} %refs_4_.1) | copy-start | bytes 2949124
  136.3 25.0 %slice-start.2 = ((s8[4718592]{0:T(1024)(128)(4,1)}), s8[4194304]{0:T(1024)(128)(4,1)S(1)}, s32[]{:S(2)}) async-start(s8[4718592]{0:T(1024)(128)(4,1)} %bitcast.122), calls=%async_computation.3 | async-start | bytes 8388608
  136.4 19.1 %collective-permute-start.15 = (bf16[2,432,384]{2,1,0:T(8,128)(2,1)S(1)}, bf16[2,432,384]{2,1,0:T(8,128)(2,1)S(1)}, u32[]{:S(2)}, u32[]{:S(2)}) collective-permute-start(bf16[2,432,384]{2,1,0:T(8,128)(2,1)S(1)} %pad_maximum_fusion.refs_9_), channel_id=1, source_target_pairs={{0,8},{4,12},{8,0},{12,4},{16,24},{20,28},{24,16},{28,20},{1,9},{5... | collective-permute-start | bytes 1990664 | tf_op jit(solution)/shard_map/ppermute | solution.py:932
  138.6 22.7 %slice-start.3 = ((s8[4718592]{0:T(1024)(128)(4,1)}), s8[524288]{0:T(1024)(128)(4,1)S(1)}, s32[]{:S(2)}) async-start(s8[4718592]{0:T(1024)(128)(4,1)} %bitcast.122), calls=%async_computation.4 | async-start | bytes 1048576
  138.6 22.7 %copy-start.17 = (bf16[640,1536]{1,0:T(8,128)(2,1)S(1)}, bf16[640,1536]{1,0:T(8,128)(2,1)}, u32[]{:S(2)}) copy-start(bf16[640,1536]{1,0:T(8,128)(2,1)} %copy-done.16) | copy-start | bytes 5898244
  148.3 6.0 %collective-permute-start.17 = (bf16[4,72,384]{2,1,0:T(8,128)(2,1)S(1)}, bf16[4,72,384]{2,1,0:T(8,128)(2,1)S(1)}, u32[]{:S(2)}, u32[]{:S(2)}) collective-permute-start(bf16[4,72,384]{2,1,0:T(8,128)(2,1)S(1)} %fusion.12), channel_id=1, source_target_pairs={{0,4},{4,0},{8,12},{12,8},{16,20},{20,16},{24,28},{28,24},{1,5},{5... | collective-permute-start | bytes 663560 | tf_op jit(solution)/shard_map/ppermute | solution.py:932
  148.7 12.6 %copy-start.9 = (bf16[640,1536]{1,0:T(8,128)(2,1)S(1)}, bf16[640,1536]{1,0:T(8,128)(2,1)}, u32[]{:S(2)}) copy-start(bf16[640,1536]{1,0:T(8,128)(2,1)} %copy-done.8) | copy-start | bytes 5898244
  148.8 6.0 %collective-permute-start.19 = (bf16[4,72,384]{2,1,0:T(8,128)(2,1)S(1)}, bf16[4,72,384]{2,1,0:T(8,128)(2,1)S(1)}, u32[]{:S(2)}, u32[]{:S(2)}) collective-permute-start(bf16[4,72,384]{2,1,0:T(8,128)(2,1)S(1)} %fusion.13), channel_id=1, source_target_pairs={{0,2},{1,3},{2,0},{3,1},{4,6},{5,7},{6,4},{7,5},{8,10},{9,11},{10,... | collective-permute-start | bytes 663560 | tf_op jit(solution)/shard_map/ppermute | solution.py:927
  154.9 17.9 %collective-permute-start.20 = (bf16[2,144,384]{2,1,0:T(8,128)(2,1)S(1)}, bf16[2,144,384]{2,1,0:T(8,128)(2,1)S(1)}, u32[]{:S(2)}, u32[]{:S(2)}) collective-permute-start(bf16[2,144,384]{2,1,0:T(8,128)(2,1)S(1)} %pad_maximum_fusion.3.refs_11_), channel_id=1, source_target_pairs={{0,8},{4,12},{8,0},{12,4},{16,24},{20,28},{24,16},{28,20},{1,9},{5... | collective-permute-start | bytes 663560 | tf_op jit(solution)/shard_map/ppermute | solution.py:932
  155.5 12.1 %copy-start.43 = (bf16[2,432,384]{2,1,0:T(8,128)(2,1)}, bf16[2,432,384]{2,1,0:T(8,128)(2,1)S(1)}, u32[]{:S(2)}) copy-start(bf16[2,432,384]{2,1,0:T(8,128)(2,1)S(1)} %collective-permute-done.15) | copy-start | bytes 1990660
  158.1 27.0 %collective-permute-start.23 = (bf16[1,432,384]{2,1,0:T(8,128)(2,1)S(1)}, bf16[1,432,384]{2,1,0:T(8,128)(2,1)S(1)}, u32[]{:S(2)}, u32[]{:S(2)}) collective-permute-start(bf16[1,432,384]{2,1,0:T(8,128)(2,1)S(1)} %pad_maximum_fusion.1.refs_10_), channel_id=1, source_target_pairs={{0,16},{4,20},{8,24},{12,28},{16,0},{20,4},{24,8},{28,12},{1,17},{... | collective-permute-start | bytes 995336 | tf_op jit(solution)/shard_map/ppermute | solution.py:932
  170.1 15.1 %copy-start.44 = (bf16[2,432,384]{2,1,0:T(8,128)(2,1)S(1)}, bf16[2,432,384]{2,1,0:T(8,128)(2,1)}, u32[]{:S(2)}) copy-start(bf16[2,432,384]{2,1,0:T(8,128)(2,1)} %copy-done.43) | copy-start | bytes 1990660
  170.1 10.1 %all-to-all-start = ((f32[32,1,432]{2,1,0:T(1,128)}), f32[32,1,432]{2,1,0:T(1,128)S(1)}, u32[]{:S(2)}, u32[]{:S(2)}) async-start(f32[32,1,432]{2,1,0:T(1,128)} %reshape.387), calls=%async_computation | async-start | bytes 131072 | tf_op jit(solution)/shard_map/all_to_all | solution.py:1125
  173.8 10.2 %collective-permute-start.21 = (bf16[1,144,384]{2,1,0:T(8,128)(2,1)S(1)}, bf16[1,144,384]{2,1,0:T(8,128)(2,1)S(1)}, u32[]{:S(2)}, u32[]{:S(2)}) collective-permute-start(bf16[1,144,384]{2,1,0:T(8,128)(2,1)S(1)} %pad_maximum_fusion.4), channel_id=1, source_target_pairs={{0,16},{4,20},{8,24},{12,28},{16,0},{20,4},{24,8},{28,12},{1,17},{... | collective-permute-start | bytes 331784 | tf_op jit(solution)/shard_map/ppermute | solution.py:932
  185.0 3.1 %collective-permute-start.22 = (f32[72,384]{1,0:T(8,128)S(1)}, f32[72,384]{1,0:T(8,128)S(1)}, u32[]{:S(2)}, u32[]{:S(2)}) collective-permute-start(f32[72,384]{1,0:T(8,128)S(1)} %get-tuple-element.93), channel_id=1, source_target_pairs={{0,1},{1,0},{2,3},{3,2},{4,5},{5,4},{6,7},{7,6},{8,9},{9,8},{10,11... | collective-permute-start | bytes 331784 | tf_op jit(solution)/shard_map/ppermute | solution.py:927
  187.7 1.7 collective-permute-start.24
  (30 other events, 126.9 us)

commit v4 on v3

--- a/solution.py
+++ b/solution.py
@@ -9,7 +9,7 @@
 SEQ_LEN = 1280
 PAIR = 2 * HEAD_DIM
 BQ = 256
-BK = 128
+BK = 256
 BLOCKS = 8
 SUB = 256
 NEG = -1e30
@@ -68,8 +68,8 @@
     return [jax.ShapeDtypeStruct(item.shape, item.dtype) for item in items]
 
 
-def params():
-    return pltpu.CompilerParams(vmem_limit_bytes=VMEM_LIMIT)
+def params(limit=VMEM_LIMIT):
+    return pltpu.CompilerParams(vmem_limit_bytes=limit)
 
 
 def cost():
@@ -127,7 +127,7 @@
             jax.ShapeDtypeStruct((rows, half), BF16),
             jax.ShapeDtypeStruct((3, rows, half), BF16),
         ],
-        compiler_params=params(),
+        compiler_params=params(58 * 1024 * 1024),
         cost_estimate=cost(),
         name="qkv_send",
     )(pos, tok, ids, emb, gain, shift, weight, bias)
@@ -630,71 +630,79 @@
     return values[pl.ds(pl.multiple_of(chip * per + at, 8), count), :].astype(BF16)
 
 
-def middle_weights_kernel(
-    pos, act, act_far, grad, grad_far, cot, cot_far, normed, normed_far, *rest, ties
-):
-    left_keep, left_send, right_keep, right_send, rows_f32 = rest[ties:]
-    step = pl.program_id(0)
-    half = normed_far.shape[1]
-    left, right = (left_keep, left_send), (right_keep, right_send)
-
-    @pl.when(step < 2)
-    def _():
-        per = rows_f32.shape[0] // 16
-        for part in range(2):
-            cols = slice(part * half, (part + 1) * half)
-            rows_f32[...] = dot_tn(cot[...], act[:, cols]) + dot_tn(cot_far[...], act_far[:, cols])
-            for x, y, z in chips():
-                left[x][y, z, part * per : (part + 1) * per, :] = rows_of(
-                    rows_f32, chip_row(pos, x, y, z), per
-                )
-
-    @pl.when(step >= 2)
-    def _():
-        per = rows_f32.shape[0] // 4
-        own = normed[:, half_lanes(pos[0], half)]
-        rows_f32[...] = dot_tn(grad[...], own) + dot_tn(grad_far[...], normed_far[...])
-        for x in range(2):
-            for y in range(2):
-                chip = (y ^ (pos[3] & 1)) * 2 + (x ^ pos[2])
-                right[y][x, 0, :per, :] = rows_of(rows_f32, chip, per)
-
-
-def middle_weights(pos, ties, act, act_far, grad, grad_far, cot, cot_far, normed, normed_far):
-    rows, width = normed.shape
+def down_weight_kernel(pos, act, act_far, cot, cot_far, *rest, ties):
+    keep, send, rows_f32 = rest[ties:]
+    per = rows_f32.shape[0] // 16
+    half = rows_f32.shape[1] // 2
+    rows_f32[...] = dot_tn(cot[...], act[...]) + dot_tn(cot_far[...], act_far[...])
+    for x, y, z in chips():
+        rows = rows_of(rows_f32, chip_row(pos, x, y, z), per)
+        (keep, send)[x][y, z, :per, :] = rows[:, :half]
+        (keep, send)[x][y, z, per:, :] = rows[:, half:]
+
+
+def down_weight_call(pos, ties, act, act_far, cot, cot_far):
+    rows, width = cot.shape
     half = width // 2
     per = width // 16
-    left = jax.ShapeDtypeStruct((2, 4, 4 * per, half), BF16)
-    right = jax.ShapeDtypeStruct((2, 4, 5 * per, half), BF16)
-    fixed = (cot, cot_far, normed, normed_far)
+    out = jax.ShapeDtypeStruct((2, 4, 4 * per, half), BF16)
 
     def kernel(*refs):
-        middle_weights_kernel(*refs, ties=len(ties))
-
-    def left_at(i, s):
-        return 0, 0, early(i), 0
-
-    def right_at(i, s):
-        return 0, z_place(late(i) ^ (s[3] >> 1)), 0, 0
+        down_weight_kernel(*refs, ties=len(ties))
 
     return pl.pallas_call(
         kernel,
         grid_spec=pltpu.PrefetchScalarGridSpec(
             num_scalar_prefetch=1,
-            grid=(6,),
-            in_specs=[pl.BlockSpec((rows, width), lambda i, s: (0, early(i)))] * 2
-            + [pl.BlockSpec((rows, width), lambda i, s: (0, late(i)))] * 2
-            + [whole(item.shape) for item in fixed]
+            grid=(2,),
+            in_specs=[pl.BlockSpec((rows, width), lambda i, s: (0, i))] * 2
+            + [whole(cot.shape)] * 2
             + [ANY] * len(ties),
-            out_specs=[pl.BlockSpec((2, 4, 2 * per, half), left_at)] * 2
-            + [pl.BlockSpec((2, 1, 4 * per, half), right_at)] * 2,
+            out_specs=[pl.BlockSpec((2, 4, 2 * per, half), lambda i, s: (0, 0, i, 0))] * 2,
+            scratch_shapes=[pltpu.VMEM((width, width), F32)],
+        ),
+        out_shape=[out, out],
+        compiler_params=params(),
+        cost_estimate=cost(),
+        name="down_weight",
+    )(pos, act, act_far, cot, cot_far, *ties)
+
+
+def up_weight_kernel(pos, grad, grad_far, normed, normed_far, keep, send, rows_f32):
+    per = rows_f32.shape[0] // 4
+    own = normed[:, half_lanes(pos[0], rows_f32.shape[1])]
+    far = normed_far[:, half_lanes(pos[0], rows_f32.shape[1])]
+    rows_f32[...] = dot_tn(grad[...], own) + dot_tn(grad_far[...], far)
+    for x in range(2):
+        for y in range(2):
+            chip = (y ^ (pos[3] & 1)) * 2 + (x ^ pos[2])
+            (keep, send)[y][x, 0, :per, :] = rows_of(rows_f32, chip, per)
+
+
+def up_weight_call(pos, grad, grad_far, normed, normed_far):
+    rows, width = normed.shape
+    half = width // 2
+    per = width // 16
+    out = jax.ShapeDtypeStruct((2, 4, 5 * per, half), BF16)
+
+    def at(i, s):
+        return 0, z_place(i ^ (s[3] >> 1)), 0, 0
+
+    return pl.pallas_call(
+        up_weight_kernel,
+        grid_spec=pltpu.PrefetchScalarGridSpec(
+            num_scalar_prefetch=1,
+            grid=(4,),
+            in_specs=[pl.BlockSpec((rows, width), lambda i, s: (0, i))] * 2
+            + [whole(normed.shape), whole(normed_far.shape)],
+            out_specs=[pl.BlockSpec((2, 1, 4 * per, half), at)] * 2,
             scratch_shapes=[pltpu.VMEM((width, half), F32)],
         ),
-        out_shape=[left, left, right, right],
+        out_shape=[out, out],
         compiler_params=params(),
         cost_estimate=cost(),
-        name="middle_weights",
-    )(pos, act, act_far, grad, grad_far, *fixed, *ties)
+        name="up_weight",
+    )(pos, grad, grad_far, normed, normed_far)
 
 
 def out_weight_kernel(pos, branch, branch_far, own, far, keep_in, send_in, tie, keep_out, send_out, rows_f32):
@@ -1048,16 +1056,15 @@
     )
     act_far = swap_head(act_send, 1)
     grad_pre_far = swap_head(grad_pre, 1)
-    normed_two_far = swap_head(normed_two_send, 1)
+    normed_two_far = swap_head(normed_two, 1)
     grad_after, branch, grad_own, grad_send, sums_two = ff_back(
         pos, grad_pre, up_weight, after, cotangent, gain_two, out_weight
     )
     grad_far = swap_head(grad_send, 1)
     branch_far = swap_head(branch, 1)
-    down_keep, down_send, up_keep, up_send = middle_weights(
-        pos, (), act_own, act_far, grad_pre, grad_pre_far, cotangent, cot_far, normed_two, normed_two_far
-    )
+    up_keep, up_send = up_weight_call(pos, grad_pre, grad_pre_far, normed_two, normed_two_far)
     up_keep, up_send = out_weight_call(pos, grad_far, branch, branch_far, own, far_send, up_keep, up_send)
+    down_keep, down_send = down_weight_call(pos, (up_send,), act_own, act_far, cotangent, cot_far)
     if direct:
         left = Sum(down_keep, swap_x(down_send))
         right = Sum(up_keep, swap_y(up_send))

time: 193 us -> 182 us (0.943)
  local copies, waits for them, and re-layouts: 18 us -> 12 us
  Pallas kernels: 106 us -> 102 us
    unnamed x106 -> x98, local copies, waits for them, and re-layouts: 14.9 us -> 8.46 us
    pallas_call x1, Pallas kernels: 24.8 us -> 19.5 us  [attend_back(): pl.pallas_call(kernel, grid_spec=pltpu.PrefetchScalarGridSpec(num_scalar_...]
    ppermute x8, waiting for transfers between devices: 6.53 us -> 1.35 us  [swap_batch(): return lax.ppermute(values, 'batch', [(i, i ^ bit) for i in range(size)])]
    ppermute x17, waiting for transfers between devices: 13.6 us -> 18.2 us  [swap_head(): return lax.ppermute(values, 'head', [(i, i ^ bit) for i in range(size)])]
    pallas_call x1, Pallas kernels: 3.89 us -> 7.13 us  [qkv_send(): pl.pallas_call(qkv_send_kernel, grid_spec=pltpu.PrefetchScalarGridSpec(nu...]
    ppermute x8, starting transfers between devices: 12.5 us -> 15.7 us  [swap_batch(): return lax.ppermute(values, 'batch', [(i, i ^ bit) for i in range(size)])]
    pallas_call x1, Pallas kernels: 14.1 us -> 11.7 us  [attend(): pl.pallas_call(kernel, grid_spec=pltpu.PrefetchScalarGridSpec(num_scalar_...]
    ppermute x17, starting transfers between devices: 11.2 us -> 8.75 us  [swap_head(): return lax.ppermute(values, 'head', [(i, i ^ bit) for i in range(size)])]
  transfers between devices with their start and end apart: 26 -> 26, of which waited for: 10 -> 10; matrix products, arithmetic and copies ran while one was open for 9% -> 10% of each run, Pallas kernels for 37% -> 37%
where the time goes in v4:
time: 182 us; the launch traced here: 181 us
  Pallas kernels  102 us (56%)
  starting transfers between devices  27.1 us (15%)
  waiting for transfers between devices  23.2 us (13%)
  other arithmetic  16 us (9%)
  local copies, waits for them, and re-layouts  12 us (7%)
    pallas_call x1, Pallas kernels, attend_back(): pl.pallas_call(kernel, grid_spec=pltpu.PrefetchScalarGridSpec(num_scalar_...  19.5 us
    ppermute x17, waiting for transfers between devices, swap_head(): return lax.ppermute(values, 'head', [(i, i ^ bit) for i in range(size)])  18.2 us
    ppermute x8, starting transfers between devices, swap_batch(): return lax.ppermute(values, 'batch', [(i, i ^ bit) for i in range(size)])  15.7 us
    pallas_call x1, Pallas kernels, ff_first(): pl.pallas_call(ff_first_kernel, grid_spec=pltpu.PrefetchScalarGridSpec(nu...  14.8 us
    pallas_call x1, Pallas kernels, attend(): pl.pallas_call(kernel, grid_spec=pltpu.PrefetchScalarGridSpec(num_scalar_...  11.7 us
    pallas_call x1, Pallas kernels, input_back(): pl.pallas_call(kernel, grid_spec=pltpu.PrefetchScalarGridSpec(num_scalar_...  9.55 us
    convert_element_type x11, other arithmetic, sent(): return self.wide().astype(BF16)  8.82 us
    ppermute x17, starting transfers between devices, swap_head(): return lax.ppermute(values, 'head', [(i, i ^ bit) for i in range(size)])  8.75 us
  transfers between devices with their start and end apart: 26, of which 10 were waited for; matrix products, arithmetic and copies ran while one was open for 10% of the time, Pallas kernels for 37%

profile of v4, /device:TPU:0, one launch (start us, length us, event | category | flops | bytes accessed | tf_op | source)
XLA Modules:
  0.0 181.3 jit_solution(14391283526636226186)
XLA Ops:
  1.3 7.1 %qkv_send.1 = (bf16[640,768]{1,0:T(8,128)(2,1)}, bf16[640,384]{1,0:T(8,128)(2,1)}, bf16[3,640,384]{2,1,0:T(8,128)(2,1)}) custom-call(s32[5]{0:T(128)} %stack.20.pos.refs_0_, bf16[640,768]{1,0:T(8,128)(2,1)} %refs_4_.1, s32[640]{0:T(1024)} %refs_5_.2, bf16[5,768]{1,0:T(8,128)(2,1)} %refs_6_.1, bf16[768]{0:T(1024)(128)(2,1)} %refs_7_.1, bf16[768]{0:T(1024)(128)(2,1)} %shift.2, ...), custom_call_target="tpu_custom_call" | custom-call | flops 1000 | bytes 1000 | tf_op jit(solution)/shard_map/qkv_send/pallas_call | solution.py:105
  9.4 1.3 copy-done.13
  10.8 2.8 %qkv_keep.1.refs_2_.refs_3_ = bf16[3,640,384]{2,1,0:T(8,128)(2,1)S(1)} custom-call(s32[5]{0:T(128)S(1)} %copy-done.23, bf16[640,768]{1,0:T(8,128)(2,1)S(1)} %copy-done.13, bf16[768,2304]{1,0:T(8,128)(2,1)S(1)} %copy-done, bf16[2,768]{1,0:T(2,128)(2,1)S(1)} %copy-done.31), custom_call_target="tpu_custom_call" | custom-call | flops 1000 | bytes 1000 | tf_op jit(solution)/shard_map/qkv_keep/pallas_call | solution.py:139
  14.1 11.7 %attend.1 = (bf16[640,384]{1,0:T(8,128)(2,1)S(1)}, bf16[640,384]{1,0:T(8,128)(2,1)S(1)}, f32[5,3,1,512]{3,2,1,0:T(1,128)S(1)}) custom-call(s32[5]{0:T(128)S(1)} %copy-done.23, s32[2,1280]{1,0:T(2,128)S(1)} %copy-done.24, bf16[3,640,384]{2,1,0:T(8,128)(2,1)S(1)} %qkv_keep.1.refs_2_.refs_3_, bf16[3,640,384]{2,1,0:T(8,128)(2,1)S(1)} %collective-permute-done.refs_3_.refs_4_, ...), custom_call_target="tpu_custom_call" | custom-call | flops 1000 | bytes 1000 | tf_op jit(solution)/shard_map/attend/pallas_call | solution.py:297
  26.3 1.5 collective-permute-done.3.far
  27.9 1.3 copy-done.10
  29.2 14.8 %ff_first.1 = (f32[640,768]{1,0:T(8,128)S(1)}, bf16[640,768]{1,0:T(8,128)(2,1)S(1)}, bf16[640,384]{1,0:T(8,128)(2,1)}, bf16[640,1536]{1,0:T(8,128)(2,1)S(1)}, bf...) custom-call(s32[5]{0:T(128)S(1)} %copy-done.23, bf16[640,768]{1,0:T(8,128)(2,1)S(1)} %copy-done.2, ...), custom_call_target="tpu_custom_call" | custom-call | flops 1000 | bytes 1000 | tf_op jit(solution)/shard_map/ff_first/pallas_call | solution.py:510
  45.5 8.2 %ff_back.1 = (f32[640,768]{1,0:T(8,128)S(1)}, bf16[640,768]{1,0:T(8,128)(2,1)S(1)}, bf16[640,384]{1,0:T(8,128)(2,1)S(1)}, bf16[640,384]{1,0:T(8,128)(2,1)S(1)}, f32[4,768]{1,0:T(4,128)S(1)}) custom-call(s32[5]{0:T(128)S(1)} %copy-done.23, bf16[640,3072]{1,0:T(8,128)(2,1)S(1)} %get-tuple-element.62.grad_pre.grad, bf16[768,3072]{1,0:T(8,128)(2,1)S(1)} %bitcast.121, ...), custom_call_target="tpu_custom_call" | custom-call | flops 1000 | bytes 1000 | tf_op jit(solution)/shard_map/ff_back/pallas_call | solution.py:596
  54.3 1.3 collective-permute-done.8.normed_far
  55.6 7.2 %up_weight.1 = (bf16[2,4,240,384]{3,2,1,0:T(8,128)(2,1)S(1)}, bf16[2,4,240,384]{3,2,1,0:T(8,128)(2,1)S(1)}) custom-call(s32[5]{0:T(128)S(1)} %copy-done.23, bf16[640,3072]{1,0:T(8,128)(2,1)S(1)} %get-tuple-element.62.grad_pre.grad, bf16[640,3072]{1,0:T(8,128)(2,1)S(1)} %collective-permute-done.7.grad_far, bf16[640,768]{1,0:T(8,128)(2,1)S(1)} %get-tuple-element.66.normed, ...), custom_call_target="tpu_custom_call" | custom-call | flops 1000 | bytes 1000 | tf_op jit(solution)/shard_map/up_weight/pallas_call | solution.py:691
  62.9 2.0 %out_weight.1 = (bf16[2,4,240,384]{3,2,1,0:T(8,128)(2,1)S(1)}, bf16[2,4,240,384]{3,2,1,0:T(8,128)(2,1)S(1)}) custom-call(s32[5]{0:T(128)S(1)} %copy-done.23, bf16[640,768]{1,0:T(8,128)(2,1)S(1)} %get-tuple-element.65.branch, bf16[640,768]{1,0:T(8,128)(2,1)S(1)} %collective-permute-done.6.branch_far, ...), custom_call_target="tpu_custom_call", output_to_operand_aliasing={{0}: (5, {}), {1}: (6, {})} | custom-call | flops 1000 | bytes 1000 | tf_op jit(solution)/shard_map/out_weight/pallas_call | solution.py:719
  64.9 2.9 %collective-permute-start.12 = (bf16[2,4,240,384]{3,2,1,0:T(8,128)(2,1)S(1)}, bf16[2,4,240,384]{3,2,1,0:T(8,128)(2,1)S(1)}, u32[]{:S(2)}, u32[]{:S(2)}) collective-permute-start(bf16[2,4,240,384]{3,2,1,0:T(8,128)(2,1)S(1)} %get-tuple-element.69.refs_5_.refs_10_), channel_id=1, source_target_pairs={{0,4},{4,0},{8,12},{12,8},{16,20},{20,16},{24,28},{28,24},{1,5},{5... | collective-permute-start | bytes 4423688 | tf_op jit(solution)/shard_map/ppermute | solution.py:940
  67.8 5.4 %down_weight.1 = (bf16[2,4,192,384]{3,2,1,0:T(8,128)(2,1)S(1)}, bf16[2,4,192,384]{3,2,1,0:T(8,128)(2,1)S(1)}) custom-call(s32[5]{0:T(128)S(1)} %copy-done.23, bf16[640,1536]{1,0:T(8,128)(2,1)S(1)} %get-tuple-element.59.refs_1_.refs_2_, bf16[640,1536]{1,0:T(8,128)(2,1)S(1)} %collective-permute-done.5.refs_2_, bf16[640,768]{1,0:T(8,128)(2,1)S(1)} %copy-done.4, ...), custom_call_target="tpu_custom_call" | custom-call | flops 1000 | bytes 1000 | tf_op jit(solution)/shard_map/down_weight/pallas_call | solution.py:653
  73.3 1.6 collective-permute-start.10
  74.8 19.5 %attend_back.1 = (bf16[3,384,640]{2,1,0:T(8,128)(2,1)}, bf16[3,384,640]{2,1,0:T(8,128)(2,1)}) custom-call(s32[5]{0:T(128)S(1)} %copy-done.23, s32[2,1280]{1,0:T(2,128)S(1)} %copy-done.24, f32[5,3,1,512]{3,2,1,0:T(1,128)S(1)} %get-tuple-element.61.refs_2_, bf16[3,640,384]{2,1,0:T(8,128)(2,1)S(1)} %qkv_keep.1.refs_2_.refs_3_, ...), custom_call_target="tpu_custom_call" | custom-call | flops 1000 | bytes 1000 | tf_op jit(solution)/shard_map/attend_back/pallas_call | solution.py:419
  94.9 6.2 %collective-permute-done.10 = bf16[2,4,192,384]{3,2,1,0:T(8,128)(2,1)S(1)} collective-permute-done((bf16[2,4,192,384]{3,2,1,0:T(8,128)(2,1)S(1)}, bf16[2,4,192,384]{3,2,1,0:T(8,128)(2,1)S(1)}, u32[]{:S(2)}, u32[]{:S(2)}) %collective-permute-start.10) | collective-permute-done | bytes 1179680 | tf_op jit(solution)/shard_map/ppermute | solution.py:935
  101.1 1.1 fusion.2.refs_7_
  102.5 1.2 fusion.refs_8_
  103.9 1.7 collective-permute-start.13
  105.6 1.2 copy-done.14
  106.8 1.0 copy-done.20
  107.8 6.9 %qkv_weight.1 = (bf16[2,4,72,384]{3,2,1,0:T(8,128)(2,1)S(1)}, bf16[2,4,72,384]{3,2,1,0:T(8,128)(2,1)S(1)}, bf16[2,4,72,384]{3,2,1,0:T(8,128)(2,1)S(1)}, bf16[2,4,72,384]{3,2,1,0:T(8,128)(2,1)S(1)}, f32[3,768]{1,0:T(4,128)S(1)}) custom-call(s32[5]{0:T(128)S(1)} %copy-done.23, bf16[3,384,640]{2,1,0:T(8,128)(2,1)} %get-tuple-element.71.refs_1_, ...), custom_call_target="tpu_custom_call" | custom-call | flops 1000 | bytes 1000 | tf_op jit(solution)/shard_map/qkv_weight/pallas_call | solution.py:846
  115.2 1.7 collective-permute-start.18
  117.2 1.4 fusion.3
  118.7 4.9 %collective-permute-done.13 = bf16[4,240,384]{2,1,0:T(8,128)(2,1)} collective-permute-done((bf16[4,240,384]{2,1,0:T(8,128)(2,1)}, bf16[4,240,384]{2,1,0:T(8,128)(2,1)}, u32[]{:S(2)}, u32[]{:S(2)}) %collective-permute-start.13) | collective-permute-done | bytes 737312 | tf_op jit(solution)/shard_map/ppermute | solution.py:935
  123.6 1.3 fusion.1
  125.0 1.8 %collective-permute-start.15 = (bf16[2,432,384]{2,1,0:T(8,128)(2,1)S(1)}, bf16[2,432,384]{2,1,0:T(8,128)(2,1)S(1)}, u32[]{:S(2)}, u32[]{:S(2)}) collective-permute-start(bf16[2,432,384]{2,1,0:T(8,128)(2,1)S(1)} %pad_maximum_fusion.refs_9_), channel_id=1, source_target_pairs={{0,8},{4,12},{8,0},{12,4},{16,24},{20,28},{24,16},{28,20},{1,9},{5... | collective-permute-start | bytes 1990664 | tf_op jit(solution)/shard_map/ppermute | solution.py:940
  126.9 9.5 %input_back.1 = (f32[640,768]{1,0:T(8,128)}, f32[7,768]{1,0:T(8,128)S(1)}, bf16[2,4,72,384]{3,2,1,0:T(8,128)(2,1)S(1)}, bf16[2,4,72,384]{3,2,1,0:T(8,128)(2,1)S(1)}) custom-call(s32[5]{0:T(128)S(1)} %copy-done.23, bf16[3,384,640]{2,1,0:T(8,128)(2,1)} %get-tuple-element.71.refs_1_, ...), custom_call_target="tpu_custom_call", output_to_operand_aliasing={{2}: (10, {}), {3}: (11, {})} | custom-call | flops 1000 | bytes 1000 | tf_op jit(solution)/shard_map/input_back/pallas_call | solution.py:914
  136.5 1.0 collective-permute-start.19
  137.6 1.6 collective-permute-start.17
  139.2 3.4 %collective-permute-done.19 = bf16[4,72,384]{2,1,0:T(8,128)(2,1)S(1)} collective-permute-done((bf16[4,72,384]{2,1,0:T(8,128)(2,1)S(1)}, bf16[4,72,384]{2,1,0:T(8,128)(2,1)S(1)}, u32[]{:S(2)}, u32[]{:S(2)}) %collective-permute-start.19) | collective-permute-done | bytes 221216 | tf_op jit(solution)/shard_map/ppermute | solution.py:935
  142.6 1.0 collective-permute-done.17
  143.7 1.1 collective-permute-start.20
  144.8 1.4 fusion.7
  146.2 1.1 fusion.11
  147.4 3.5 %collective-permute-start.23 = (bf16[1,432,384]{2,1,0:T(8,128)(2,1)S(1)}, bf16[1,432,384]{2,1,0:T(8,128)(2,1)S(1)}, u32[]{:S(2)}, u32[]{:S(2)}) collective-permute-start(bf16[1,432,384]{2,1,0:T(8,128)(2,1)S(1)} %pad_maximum_fusion.1.refs_10_), channel_id=1, source_target_pairs={{0,16},{4,20},{8,24},{12,28},{16,0},{20,4},{24,8},{28,12},{1,17},{... | collective-permute-start | bytes 995336 | tf_op jit(solution)/shard_map/ppermute | solution.py:940
  151.0 6.2 %mixed.1 = (bf16[640,768]{1,0:T(8,128)(2,1)}, f32[32,18,24]{2,1,0:T(8,128)S(1)}, bf16[2,4,72,384]{3,2,1,0:T(8,128)(2,1)S(1)}, bf16[2,4,72,384]{3,2,1,0:T(8,128)(2,1)S(1)}) custom-call(s32[5]{0:T(128)S(1)} %copy-done.23, bf16[640,1536]{1,0:T(8,128)(2,1)S(1)} %copy-done.16, ...), custom_call_target="tpu_custom_call", output_to_operand_aliasing={{2}: (12, {}), {3}: (13, {})} | custom-call | flops 1000 | bytes 1000 | tf_op jit(solution)/shard_map/mixed/pallas_call | solution.py:780
  157.2 0.8 copy-done.11
  157.9 0.8 copy-done.12
  158.7 1.0 reshape.387
  159.7 2.7 %all-to-all-start = ((f32[32,1,432]{2,1,0:T(1,128)}), f32[32,1,432]{2,1,0:T(1,128)S(1)}, u32[]{:S(2)}, u32[]{:S(2)}) async-start(f32[32,1,432]{2,1,0:T(1,128)} %reshape.387), calls=%async_computation | async-start | bytes 131072 | tf_op jit(solution)/shard_map/all_to_all | solution.py:1132
  162.4 1.0 fusion.21
  163.4 2.7 %collective-permute-start.21 = (bf16[1,144,384]{2,1,0:T(8,128)(2,1)S(1)}, bf16[1,144,384]{2,1,0:T(8,128)(2,1)S(1)}, u32[]{:S(2)}, u32[]{:S(2)}) collective-permute-start(bf16[1,144,384]{2,1,0:T(8,128)(2,1)S(1)} %pad_maximum_fusion.4), channel_id=1, source_target_pairs={{0,16},{4,20},{8,24},{12,28},{16,0},{20,4},{24,8},{28,12},{1,17},{... | collective-permute-start | bytes 331784 | tf_op jit(solution)/shard_map/ppermute | solution.py:940
  166.1 3.7 %all-to-all-done = f32[32,1,432]{2,1,0:T(1,128)S(1)} async-done(((f32[32,1,432]{2,1,0:T(1,128)}), f32[32,1,432]{2,1,0:T(1,128)S(1)}, u32[]{:S(2)}, u32[]{:S(2)}) %all-to-all-start) | async-done | bytes 55328 | tf_op jit(solution)/shard_map/all_to_all | solution.py:1132
  170.3 0.8 reduce
  173.6 1.0 select_bitcast_fusion.1
  174.8 1.2 fusion.5
  176.1 1.2 fusion.9
  (157 shorter events, 14.1 us)
Async XLA Ops:
  1.3 12.9 %copy-start.24 = (s32[2,1280]{1,0:T(2,128)S(1)}, s32[2,1280]{1,0:T(2,128)}, u32[]{:S(2)}) copy-start(s32[2,1280]{1,0:T(2,128)} %refs_1_.3) | copy-start | bytes 30724
  8.4 5.7 %collective-permute-start = (bf16[3,640,384]{2,1,0:T(8,128)(2,1)}, bf16[3,640,384]{2,1,0:T(8,128)(2,1)S(1)}, u32[]{:S(2)}, u32[]{:S(2)}) collective-permute-start(bf16[3,640,384]{2,1,0:T(8,128)(2,1)} %get-tuple-element.54), channel_id=1, source_target_pairs={{0,1},{1,0},{2,3},{3,2},{4,5},{5,4},{6,7},{7,6},{8,9},{9,8},{10,11... | collective-permute-start | bytes 4423688 | tf_op jit(solution)/shard_map/ppermute | solution.py:935
  8.9 5.2 %collective-permute-start.1 = (bf16[640,768]{1,0:T(8,128)(2,1)S(1)}, bf16[640,768]{1,0:T(8,128)(2,1)S(1)}, u32[]{:S(2)}, u32[]{:S(2)}) collective-permute-start(bf16[640,768]{1,0:T(8,128)(2,1)S(1)} %copy-done.4), channel_id=1, source_target_pairs={{0,1},{1,0},{2,3},{3,2},{4,5},{5,4},{6,7},{7,6},{8,9},{9,8},{10,11... | collective-permute-start | bytes 2949128 | tf_op jit(solution)/shard_map/ppermute | solution.py:935
  9.0 5.1 %collective-permute-start.2 = (bf16[640,384]{1,0:T(8,128)(2,1)}, bf16[640,384]{1,0:T(8,128)(2,1)S(1)}, u32[]{:S(2)}, u32[]{:S(2)}) collective-permute-start(bf16[640,384]{1,0:T(8,128)(2,1)} %get-tuple-element.55), channel_id=1, source_target_pairs={{0,1},{1,0},{2,3},{3,2},{4,5},{5,4},{6,7},{7,6},{8,9},{9,8},{10,11... | collective-permute-start | bytes 1474568 | tf_op jit(solution)/shard_map/ppermute | solution.py:935
  9.4 18.4 %slice-start = ((s8[4718592]{0:T(1024)(128)(4,1)}), s8[4194304]{0:T(1024)(128)(4,1)S(1)}, s32[]{:S(2)}) async-start(s8[4718592]{0:T(1024)(128)(4,1)} %bitcast.120), calls=%async_computation.1 | async-start | bytes 8388608
  10.8 15.5 %copy-start.43 = (bf16[3072]{0:T(1024)(128)(2,1)S(1)}, bf16[3072]{0:T(1024)(128)(2,1)}, u32[]{:S(2)}) copy-start(bf16[3072]{0:T(1024)(128)(2,1)} %param.30) | copy-start | bytes 18436
  10.8 17.0 %slice-start.1 = ((s8[4718592]{0:T(1024)(128)(4,1)}), s8[524288]{0:T(1024)(128)(4,1)S(1)}, s32[]{:S(2)}) async-start(s8[4718592]{0:T(1024)(128)(4,1)} %bitcast.120), calls=%async_computation.2 | async-start | bytes 1048576
  10.8 17.0 %copy-start.1 = (bf16[3072,768]{1,0:T(8,128)(2,1)S(1)}, bf16[3072,768]{1,0:T(8,128)(2,1)}, u32[]{:S(2)}) copy-start(bf16[3072,768]{1,0:T(8,128)(2,1)} %refs_3_.5) | copy-start | bytes 14155780
  13.6 14.2 %copy-start.2 = (bf16[640,768]{1,0:T(8,128)(2,1)S(1)}, bf16[640,768]{1,0:T(8,128)(2,1)}, u32[]{:S(2)}) copy-start(bf16[640,768]{1,0:T(8,128)(2,1)} %refs_4_.1) | copy-start | bytes 2949124
  13.6 14.2 %copy-start.22 = (bf16[5,768]{1,0:T(8,128)(2,1)S(1)}, bf16[5,768]{1,0:T(8,128)(2,1)}, u32[]{:S(2)}) copy-start(bf16[5,768]{1,0:T(8,128)(2,1)} %refs_6_.1) | copy-start | bytes 23044
  13.7 14.2 %copy-start.25 = (s32[640]{0:T(1024)S(1)}, s32[640]{0:T(1024)}, u32[]{:S(2)}) copy-start(s32[640]{0:T(1024)} %refs_5_.2) | copy-start | bytes 7684
  13.7 14.2 %copy-start.32 = (bf16[768]{0:T(1024)(128)(2,1)S(1)}, bf16[768]{0:T(1024)(128)(2,1)}, u32[]{:S(2)}) copy-start(bf16[768]{0:T(1024)(128)(2,1)} %gain.5) | copy-start | bytes 4612
  13.7 14.2 %copy-start.34 = (bf16[768]{0:T(1024)(128)(2,1)S(1)}, bf16[768]{0:T(1024)(128)(2,1)}, u32[]{:S(2)}) copy-start(bf16[768]{0:T(1024)(128)(2,1)} %bias.5) | copy-start | bytes 4612
  13.7 14.2 %copy-start.35 = (bf16[768]{0:T(1024)(128)(2,1)S(1)}, bf16[768]{0:T(1024)(128)(2,1)}, u32[]{:S(2)}) copy-start(bf16[768]{0:T(1024)(128)(2,1)} %shift.3) | copy-start | bytes 4612
  14.1 11.7 %copy-start.19 = (bf16[640,384]{1,0:T(8,128)(2,1)}, bf16[640,384]{1,0:T(8,128)(2,1)S(1)}, u32[]{:S(2)}) copy-start(bf16[640,384]{1,0:T(8,128)(2,1)S(1)} %collective-permute-done.2.refs_5_.refs_6_) | copy-start | bytes 1474564
  25.9 1.9 %collective-permute-start.3 = (bf16[640,384]{1,0:T(8,128)(2,1)S(1)}, bf16[640,384]{1,0:T(8,128)(2,1)S(1)}, u32[]{:S(2)}, u32[]{:S(2)}) collective-permute-start(bf16[640,384]{1,0:T(8,128)(2,1)S(1)} %get-tuple-element.57.far.refs_6_), channel_id=1, source_target_pairs={{0,1},{1,0},{2,3},{3,2},{4,5},{5,4},{6,7},{7,6},{8,9},{9,8},{10,11... | collective-permute-start | bytes 1474568 | tf_op jit(solution)/shard_map/ppermute | solution.py:935
  44.6 23.2 %copy-start.7 = (bf16[640,1536]{1,0:T(8,128)(2,1)}, bf16[640,1536]{1,0:T(8,128)(2,1)S(1)}, u32[]{:S(2)}) copy-start(bf16[640,1536]{1,0:T(8,128)(2,1)S(1)} %get-tuple-element.59.refs_1_.refs_2_) | copy-start | bytes 5898244
  44.6 11.0 %collective-permute-start.7 = (bf16[640,3072]{1,0:T(8,128)(2,1)S(1)}, bf16[640,3072]{1,0:T(8,128)(2,1)S(1)}, u32[]{:S(2)}, u32[]{:S(2)}) collective-permute-start(bf16[640,3072]{1,0:T(8,128)(2,1)S(1)} %get-tuple-element.62.grad_pre.grad), channel_id=1, source_target_pairs={{0,1},{1,0},{2,3},{3,2},{4,5},{5,4},{6,7},{7,6},{8,9},{9,8},{10,11... | collective-permute-start | bytes 11796488 | tf_op jit(solution)/shard_map/ppermute | solution.py:935
  45.0 22.9 %collective-permute-start.5 = (bf16[640,1536]{1,0:T(8,128)(2,1)S(1)}, bf16[640,1536]{1,0:T(8,128)(2,1)S(1)}, u32[]{:S(2)}, u32[]{:S(2)}) collective-permute-start(bf16[640,1536]{1,0:T(8,128)(2,1)S(1)} %get-tuple-element.58.refs_1_), channel_id=1, source_target_pairs={{0,1},{1,0},{2,3},{3,2},{4,5},{5,4},{6,7},{7,6},{8,9},{9,8},{10,11... | collective-permute-start | bytes 5898248 | tf_op jit(solution)/shard_map/ppermute | solution.py:935
  45.1 10.5 %collective-permute-start.8 = (bf16[640,768]{1,0:T(8,128)(2,1)S(1)}, bf16[640,768]{1,0:T(8,128)(2,1)S(1)}, u32[]{:S(2)}, u32[]{:S(2)}) collective-permute-start(bf16[640,768]{1,0:T(8,128)(2,1)S(1)} %get-tuple-element.66.normed), channel_id=1, source_target_pairs={{0,1},{1,0},{2,3},{3,2},{4,5},{5,4},{6,7},{7,6},{8,9},{9,8},{10,11... | collective-permute-start | bytes 2949128 | tf_op jit(solution)/shard_map/ppermute | solution.py:935
  53.7 9.1 %collective-permute-start.6 = (bf16[640,768]{1,0:T(8,128)(2,1)S(1)}, bf16[640,768]{1,0:T(8,128)(2,1)S(1)}, u32[]{:S(2)}, u32[]{:S(2)}) collective-permute-start(bf16[640,768]{1,0:T(8,128)(2,1)S(1)} %get-tuple-element.65.branch), channel_id=1, source_target_pairs={{0,1},{1,0},{2,3},{3,2},{4,5},{5,4},{6,7},{7,6},{8,9},{9,8},{10,11... | collective-permute-start | bytes 2949128 | tf_op jit(solution)/shard_map/ppermute | solution.py:935
  53.9 8.9 %collective-permute-start.4 = (bf16[640,384]{1,0:T(8,128)(2,1)S(1)}, bf16[640,384]{1,0:T(8,128)(2,1)S(1)}, u32[]{:S(2)}, u32[]{:S(2)}) collective-permute-start(bf16[640,384]{1,0:T(8,128)(2,1)S(1)} %get-tuple-element.64), channel_id=1, source_target_pairs={{0,1},{1,0},{2,3},{3,2},{4,5},{5,4},{6,7},{7,6},{8,9},{9,8},{10,11... | collective-permute-start | bytes 1474568 | tf_op jit(solution)/shard_map/ppermute | solution.py:935
  64.8 37.7 %copy-start.9 = (bf16[2,4,240,384]{3,2,1,0:T(8,128)(2,1)}, bf16[2,4,240,384]{3,2,1,0:T(8,128)(2,1)S(1)}, u32[]{:S(2)}) copy-start(bf16[2,4,240,384]{3,2,1,0:T(8,128)(2,1)S(1)} %get-tuple-element.75) | copy-start | bytes 4423684
  64.9 37.7 %collective-permute-start.12 = (bf16[2,4,240,384]{3,2,1,0:T(8,128)(2,1)S(1)}, bf16[2,4,240,384]{3,2,1,0:T(8,128)(2,1)S(1)}, u32[]{:S(2)}, u32[]{:S(2)}) collective-permute-start(bf16[2,4,240,384]{3,2,1,0:T(8,128)(2,1)S(1)} %get-tuple-element.69.refs_5_.refs_10_), channel_id=1, source_target_pairs={{0,4},{4,0},{8,12},{12,8},{16,20},{20,16},{24,28},{28,24},{1,5},{5... | collective-permute-start | bytes 4423688 | tf_op jit(solution)/shard_map/ppermute | solution.py:940
  73.2 27.9 %copy-start.21 = (bf16[2,4,192,384]{3,2,1,0:T(8,128)(2,1)}, bf16[2,4,192,384]{3,2,1,0:T(8,128)(2,1)S(1)}, u32[]{:S(2)}) copy-start(bf16[2,4,192,384]{3,2,1,0:T(8,128)(2,1)S(1)} %get-tuple-element.74) | copy-start | bytes 3538948
  73.3 27.8 %collective-permute-start.10 = (bf16[2,4,192,384]{3,2,1,0:T(8,128)(2,1)S(1)}, bf16[2,4,192,384]{3,2,1,0:T(8,128)(2,1)S(1)}, u32[]{:S(2)}, u32[]{:S(2)}) collective-permute-start(bf16[2,4,192,384]{3,2,1,0:T(8,128)(2,1)S(1)} %get-tuple-element.70.refs_9_), channel_id=1, source_target_pairs={{0,2},{1,3},{2,0},{3,1},{4,6},{5,7},{6,4},{7,5},{8,10},{9,11},{10,... | collective-permute-start | bytes 3538952 | tf_op jit(solution)/shard_map/ppermute | solution.py:935
  94.3 11.3 %collective-permute-start.9 = (bf16[3,384,640]{2,1,0:T(8,128)(2,1)}, bf16[3,384,640]{2,1,0:T(8,128)(2,1)}, u32[]{:S(2)}, u32[]{:S(2)}) collective-permute-start(bf16[3,384,640]{2,1,0:T(8,128)(2,1)} %get-tuple-element.72.refs_2_), channel_id=1, source_target_pairs={{0,1},{1,0},{2,3},{3,2},{4,5},{5,4},{6,7},{7,6},{8,9},{9,8},{10,11... | collective-permute-start | bytes 4423688 | tf_op jit(solution)/shard_map/ppermute | solution.py:935
  94.4 11.2 %collective-permute-start.14 = (bf16[3,384,640]{2,1,0:T(8,128)(2,1)}, bf16[3,384,640]{2,1,0:T(8,128)(2,1)}, u32[]{:S(2)}, u32[]{:S(2)}) collective-permute-start(bf16[3,384,640]{2,1,0:T(8,128)(2,1)} %get-tuple-element.71.refs_1_), channel_id=1, source_target_pairs={{0,1},{1,0},{2,3},{3,2},{4,5},{5,4},{6,7},{7,6},{8,9},{9,8},{10,11... | collective-permute-start | bytes 4423688 | tf_op jit(solution)/shard_map/ppermute | solution.py:935
  102.2 15.0 %collective-permute-start.11 = (bf16[4,192,384]{2,1,0:T(8,128)(2,1)}, bf16[4,192,384]{2,1,0:T(8,128)(2,1)}, u32[]{:S(2)}, u32[]{:S(2)}) collective-permute-start(bf16[4,192,384]{2,1,0:T(8,128)(2,1)} %fusion.2.refs_7_), channel_id=1, source_target_pairs={{0,4},{4,0},{8,12},{12,8},{16,20},{20,16},{24,28},{28,24},{1,5},{5... | collective-permute-start | bytes 1769480 | tf_op jit(solution)/shard_map/ppermute | solution.py:940
  103.9 19.7 %collective-permute-start.13 = (bf16[4,240,384]{2,1,0:T(8,128)(2,1)}, bf16[4,240,384]{2,1,0:T(8,128)(2,1)}, u32[]{:S(2)}, u32[]{:S(2)}) collective-permute-start(bf16[4,240,384]{2,1,0:T(8,128)(2,1)} %fusion.refs_8_), channel_id=1, source_target_pairs={{0,2},{1,3},{2,0},{3,1},{4,6},{5,7},{6,4},{7,5},{8,10},{9,11},{10,... | collective-permute-start | bytes 2211848 | tf_op jit(solution)/shard_map/ppermute | solution.py:935
  114.8 22.7 %collective-permute-start.16 = (bf16[2,4,72,384]{3,2,1,0:T(8,128)(2,1)S(1)}, bf16[2,4,72,384]{3,2,1,0:T(8,128)(2,1)S(1)}, u32[]{:S(2)}, u32[]{:S(2)}) collective-permute-start(bf16[2,4,72,384]{3,2,1,0:T(8,128)(2,1)S(1)} %get-tuple-element.83), channel_id=1, source_target_pairs={{0,2},{1,3},{2,0},{3,1},{4,6},{5,7},{6,4},{7,5},{8,10},{9,11},{10,... | collective-permute-start | bytes 1327112 | tf_op jit(solution)/shard_map/ppermute | solution.py:935
  115.2 21.3 %collective-permute-start.18 = (bf16[2,4,72,384]{3,2,1,0:T(8,128)(2,1)S(1)}, bf16[2,4,72,384]{3,2,1,0:T(8,128)(2,1)S(1)}, u32[]{:S(2)}, u32[]{:S(2)}) collective-permute-start(bf16[2,4,72,384]{3,2,1,0:T(8,128)(2,1)S(1)} %get-tuple-element.85), channel_id=1, source_target_pairs={{0,4},{4,0},{8,12},{12,8},{16,20},{20,16},{24,28},{28,24},{1,5},{5... | collective-permute-start | bytes 1327112 | tf_op jit(solution)/shard_map/ppermute | solution.py:940
  124.9 26.0 %slice-start.2 = ((s8[4718592]{0:T(1024)(128)(4,1)}), s8[4194304]{0:T(1024)(128)(4,1)S(1)}, s32[]{:S(2)}) async-start(s8[4718592]{0:T(1024)(128)(4,1)} %bitcast.122), calls=%async_computation.3 | async-start | bytes 8388608
  125.0 19.8 %collective-permute-start.15 = (bf16[2,432,384]{2,1,0:T(8,128)(2,1)S(1)}, bf16[2,432,384]{2,1,0:T(8,128)(2,1)S(1)}, u32[]{:S(2)}, u32[]{:S(2)}) collective-permute-start(bf16[2,432,384]{2,1,0:T(8,128)(2,1)S(1)} %pad_maximum_fusion.refs_9_), channel_id=1, source_target_pairs={{0,8},{4,12},{8,0},{12,4},{16,24},{20,28},{24,16},{28,20},{1,9},{5... | collective-permute-start | bytes 1990664 | tf_op jit(solution)/shard_map/ppermute | solution.py:940
  126.9 24.0 %slice-start.3 = ((s8[4718592]{0:T(1024)(128)(4,1)}), s8[524288]{0:T(1024)(128)(4,1)S(1)}, s32[]{:S(2)}) async-start(s8[4718592]{0:T(1024)(128)(4,1)} %bitcast.122), calls=%async_computation.4 | async-start | bytes 1048576
  126.9 24.0 %copy-start.16 = (bf16[640,1536]{1,0:T(8,128)(2,1)S(1)}, bf16[640,1536]{1,0:T(8,128)(2,1)}, u32[]{:S(2)}) copy-start(bf16[640,1536]{1,0:T(8,128)(2,1)} %copy-done.15) | copy-start | bytes 5898244
  136.5 6.0 %collective-permute-start.19 = (bf16[4,72,384]{2,1,0:T(8,128)(2,1)S(1)}, bf16[4,72,384]{2,1,0:T(8,128)(2,1)S(1)}, u32[]{:S(2)}, u32[]{:S(2)}) collective-permute-start(bf16[4,72,384]{2,1,0:T(8,128)(2,1)S(1)} %fusion.13), channel_id=1, source_target_pairs={{0,2},{1,3},{2,0},{3,1},{4,6},{5,7},{6,4},{7,5},{8,10},{9,11},{10,... | collective-permute-start | bytes 663560 | tf_op jit(solution)/shard_map/ppermute | solution.py:935
  137.5 9.9 %copy-start.41 = (bf16[2,4,72,384]{3,2,1,0:T(8,128)(2,1)}, bf16[2,4,72,384]{3,2,1,0:T(8,128)(2,1)S(1)}, u32[]{:S(2)}) copy-start(bf16[2,4,72,384]{3,2,1,0:T(8,128)(2,1)S(1)} %collective-permute-done.16) | copy-start | bytes 1327108
  137.5 13.4 %copy-start.8 = (bf16[640,1536]{1,0:T(8,128)(2,1)S(1)}, bf16[640,1536]{1,0:T(8,128)(2,1)}, u32[]{:S(2)}) copy-start(bf16[640,1536]{1,0:T(8,128)(2,1)} %copy-done.7) | copy-start | bytes 5898244
  137.6 6.0 %collective-permute-start.17 = (bf16[4,72,384]{2,1,0:T(8,128)(2,1)S(1)}, bf16[4,72,384]{2,1,0:T(8,128)(2,1)S(1)}, u32[]{:S(2)}, u32[]{:S(2)}) collective-permute-start(bf16[4,72,384]{2,1,0:T(8,128)(2,1)S(1)} %fusion.12), channel_id=1, source_target_pairs={{0,4},{4,0},{8,12},{12,8},{16,20},{20,16},{24,28},{28,24},{1,5},{5... | collective-permute-start | bytes 663560 | tf_op jit(solution)/shard_map/ppermute | solution.py:940
  143.7 18.7 %collective-permute-start.20 = (bf16[2,144,384]{2,1,0:T(8,128)(2,1)S(1)}, bf16[2,144,384]{2,1,0:T(8,128)(2,1)S(1)}, u32[]{:S(2)}, u32[]{:S(2)}) collective-permute-start(bf16[2,144,384]{2,1,0:T(8,128)(2,1)S(1)} %pad_maximum_fusion.3.refs_11_), channel_id=1, source_target_pairs={{0,8},{4,12},{8,0},{12,4},{16,24},{20,28},{24,16},{28,20},{1,9},{5... | collective-permute-start | bytes 663560 | tf_op jit(solution)/shard_map/ppermute | solution.py:940
  144.8 12.4 %copy-start.39 = (bf16[2,432,384]{2,1,0:T(8,128)(2,1)}, bf16[2,432,384]{2,1,0:T(8,128)(2,1)S(1)}, u32[]{:S(2)}) copy-start(bf16[2,432,384]{2,1,0:T(8,128)(2,1)S(1)} %collective-permute-done.15) | copy-start | bytes 1990660
  147.4 27.4 %collective-permute-start.23 = (bf16[1,432,384]{2,1,0:T(8,128)(2,1)S(1)}, bf16[1,432,384]{2,1,0:T(8,128)(2,1)S(1)}, u32[]{:S(2)}, u32[]{:S(2)}) collective-permute-start(bf16[1,432,384]{2,1,0:T(8,128)(2,1)S(1)} %pad_maximum_fusion.1.refs_10_), channel_id=1, source_target_pairs={{0,16},{4,20},{8,24},{12,28},{16,0},{20,4},{24,8},{28,12},{1,17},{... | collective-permute-start | bytes 995336 | tf_op jit(solution)/shard_map/ppermute | solution.py:940
  159.7 15.1 %copy-start.40 = (bf16[2,432,384]{2,1,0:T(8,128)(2,1)S(1)}, bf16[2,432,384]{2,1,0:T(8,128)(2,1)}, u32[]{:S(2)}) copy-start(bf16[2,432,384]{2,1,0:T(8,128)(2,1)} %copy-done.39) | copy-start | bytes 1990660
  159.7 10.1 %all-to-all-start = ((f32[32,1,432]{2,1,0:T(1,128)}), f32[32,1,432]{2,1,0:T(1,128)S(1)}, u32[]{:S(2)}, u32[]{:S(2)}) async-start(f32[32,1,432]{2,1,0:T(1,128)} %reshape.387), calls=%async_computation | async-start | bytes 131072 | tf_op jit(solution)/shard_map/all_to_all | solution.py:1132
  163.4 10.2 %collective-permute-start.21 = (bf16[1,144,384]{2,1,0:T(8,128)(2,1)S(1)}, bf16[1,144,384]{2,1,0:T(8,128)(2,1)S(1)}, u32[]{:S(2)}, u32[]{:S(2)}) collective-permute-start(bf16[1,144,384]{2,1,0:T(8,128)(2,1)S(1)} %pad_maximum_fusion.4), channel_id=1, source_target_pairs={{0,16},{4,20},{8,24},{12,28},{16,0},{20,4},{24,8},{28,12},{1,17},{... | collective-permute-start | bytes 331784 | tf_op jit(solution)/shard_map/ppermute | solution.py:940
  174.6 3.1 %collective-permute-start.22 = (f32[72,384]{1,0:T(8,128)S(1)}, f32[72,384]{1,0:T(8,128)S(1)}, u32[]{:S(2)}, u32[]{:S(2)}) collective-permute-start(f32[72,384]{1,0:T(8,128)S(1)} %get-tuple-element.91), channel_id=1, source_target_pairs={{0,1},{1,0},{2,3},{3,2},{4,5},{5,4},{6,7},{7,6},{8,9},{9,8},{10,11... | collective-permute-start | bytes 331784 | tf_op jit(solution)/shard_map/ppermute | solution.py:935
  177.3 1.7 collective-permute-start.24
  (26 other events, 153.0 us)

commit v5 on v4

--- a/solution.py
+++ b/solution.py
@@ -11,7 +11,7 @@
 BQ = 256
 BK = 256
 BLOCKS = 8
-SUB = 256
+SUB = 768
 NEG = -1e30
 F32 = jnp.float32
 BF16 = jnp.bfloat16
@@ -467,7 +467,7 @@
 
 def ff_first_kernel(
     pos, tok, ids, emb, own, far, weight, bias, gain, shift, cot, up, up_bias, down,
-    after_out, normed_out, half_out, act_own, act_send, grad_out, bias_grad, attended, act,
+    after_out, normed_out, act_own, act_send, grad_out, bias_grad, attended, act,
 ):
     step = pl.program_id(0)
 
@@ -478,7 +478,6 @@
         after_out[...] = after
         scaled, _ = center_and_scale(after)
         normed_out[...] = (scaled * wide(gain) + wide(shift)).astype(BF16)
-        half_out[...] = normed_out[:, half_lanes(1 - pos[0], half_out.shape[1])]
 
     for part in range(up.shape[1] // SUB):
         cols = slice(part * SUB, (part + 1) * SUB)
@@ -521,7 +520,6 @@
             out_specs=[
                 whole((rows, width)),
                 whole((rows, width)),
-                whole((rows, width // 2)),
                 pl.BlockSpec((rows, width), lambda i, s: (0, late(i))),
                 pl.BlockSpec((rows, width), lambda i, s: (0, early(i))),
                 pl.BlockSpec((rows, width), lambda i, s: (0, hidden_block(i, s[0]))),
@@ -532,7 +530,6 @@
         out_shape=[
             shape((rows, width), F32),
             shape((rows, width), BF16),
-            shape((rows, width // 2), BF16),
             shape((rows, hidden // 2), BF16),
             shape((rows, hidden // 2), BF16),
             shape((rows, hidden), BF16),
@@ -1050,7 +1047,7 @@
     keep = qkv_keep(pos, normed, qkv_weight, qv_bias)
     own, far_send, lse = attend(pos, (cot_far, normed_far), segment_ids, keep, recv)
     far = swap_head(far_send, 1)
-    after, normed_two, normed_two_send, act_own, act_send, grad_pre, up_bias_grad = ff_first(
+    after, normed_two, act_own, act_send, grad_pre, up_bias_grad = ff_first(
         pos, tokens, ids, pass_embed, own, far, out_weight, row(out_bias), gain_two, row(norm2_shift),
         cotangent, up_weight, up_bias.reshape(1, -1), down_weight,
     )

time: 182 us -> 179 us (0.984)
  Pallas kernels: 102 us -> 96.7 us
  waiting for transfers between devices: 23.2 us -> 26.4 us
    pallas_call x1, Pallas kernels: 14.8 us -> 12 us  [ff_first(): pl.pallas_call(ff_first_kernel, grid_spec=pltpu.PrefetchScalarGridSpec(nu...]
    ppermute x17, waiting for transfers between devices: 18.2 us -> 20.7 us  [swap_head(): return lax.ppermute(values, 'head', [(i, i ^ bit) for i in range(size)])]
    ppermute x8, starting transfers between devices: 15.7 us -> 13.5 us  [swap_batch(): return lax.ppermute(values, 'batch', [(i, i ^ bit) for i in range(size)])]
where the time goes in v5:
time: 179 us; the launch traced here: 178 us
  Pallas kernels  96.7 us (54%)
  waiting for transfers between devices  26.4 us (15%)
  starting transfers between devices  25.9 us (14%)
  other arithmetic  16 us (9%)
  local copies, waits for them, and re-layouts  12 us (7%)
    ppermute x17, waiting for transfers between devices, swap_head(): return lax.ppermute(values, 'head', [(i, i ^ bit) for i in range(size)])  20.7 us
    pallas_call x1, Pallas kernels, attend_back(): pl.pallas_call(kernel, grid_spec=pltpu.PrefetchScalarGridSpec(num_scalar_...  18.3 us
    ppermute x8, starting transfers between devices, swap_batch(): return lax.ppermute(values, 'batch', [(i, i ^ bit) for i in range(size)])  13.5 us
    pallas_call x1, Pallas kernels, ff_first(): pl.pallas_call(ff_first_kernel, grid_spec=pltpu.PrefetchScalarGridSpec(nu...  12 us
    pallas_call x1, Pallas kernels, attend(): pl.pallas_call(kernel, grid_spec=pltpu.PrefetchScalarGridSpec(num_scalar_...  10.9 us
    pallas_call x1, Pallas kernels, input_back(): pl.pallas_call(kernel, grid_spec=pltpu.PrefetchScalarGridSpec(num_scalar_...  9.55 us
    convert_element_type x11, other arithmetic, sent(): return self.wide().astype(BF16)  8.82 us
    ppermute x17, starting transfers between devices, swap_head(): return lax.ppermute(values, 'head', [(i, i ^ bit) for i in range(size)])  8.69 us
  transfers between devices with their start and end apart: 26, of which 10 were waited for; matrix products, arithmetic and copies ran while one was open for 10% of the time, Pallas kernels for 37%

profile of v5, /device:TPU:0, one launch (start us, length us, event | category | flops | bytes accessed | tf_op | source)
XLA Modules:
  0.0 178.4 jit_solution(8544489805819645926)
XLA Ops:
  1.3 7.1 %qkv_send.1 = (bf16[640,768]{1,0:T(8,128)(2,1)}, bf16[640,384]{1,0:T(8,128)(2,1)}, bf16[3,640,384]{2,1,0:T(8,128)(2,1)}) custom-call(s32[5]{0:T(128)} %stack.20.pos.refs_0_, bf16[640,768]{1,0:T(8,128)(2,1)} %refs_4_.1, s32[640]{0:T(1024)} %refs_5_.2, bf16[5,768]{1,0:T(8,128)(2,1)} %refs_6_.1, bf16[768]{0:T(1024)(128)(2,1)} %refs_7_.1, bf16[768]{0:T(1024)(128)(2,1)} %shift.2, ...), custom_call_target="tpu_custom_call" | custom-call | flops 1000 | bytes 1000 | tf_op jit(solution)/shard_map/qkv_send/pallas_call | solution.py:105
  9.4 1.3 copy-done.13
  10.8 2.8 %qkv_keep.1.refs_2_.refs_3_ = bf16[3,640,384]{2,1,0:T(8,128)(2,1)S(1)} custom-call(s32[5]{0:T(128)S(1)} %copy-done.23, bf16[640,768]{1,0:T(8,128)(2,1)S(1)} %copy-done.13, bf16[768,2304]{1,0:T(8,128)(2,1)S(1)} %copy-done, bf16[2,768]{1,0:T(2,128)(2,1)S(1)} %copy-done.31), custom_call_target="tpu_custom_call" | custom-call | flops 1000 | bytes 1000 | tf_op jit(solution)/shard_map/qkv_keep/pallas_call | solution.py:139
  14.1 10.9 %attend.1 = (bf16[640,384]{1,0:T(8,128)(2,1)S(1)}, bf16[640,384]{1,0:T(8,128)(2,1)S(1)}, f32[5,3,1,512]{3,2,1,0:T(1,128)S(1)}) custom-call(s32[5]{0:T(128)S(1)} %copy-done.23, s32[2,1280]{1,0:T(2,128)S(1)} %copy-done.24, bf16[3,640,384]{2,1,0:T(8,128)(2,1)S(1)} %qkv_keep.1.refs_2_.refs_3_, bf16[3,640,384]{2,1,0:T(8,128)(2,1)S(1)} %collective-permute-done.refs_3_.refs_4_, ...), custom_call_target="tpu_custom_call" | custom-call | flops 1000 | bytes 1000 | tf_op jit(solution)/shard_map/attend/pallas_call | solution.py:297
  25.5 1.5 collective-permute-done.3.far
  27.1 1.3 copy-done.10
  28.3 12.0 %ff_first.1 = (f32[640,768]{1,0:T(8,128)S(1)}, bf16[640,768]{1,0:T(8,128)(2,1)S(1)}, bf16[640,1536]{1,0:T(8,128)(2,1)S(1)}, bf16[640,1536]{1,0:T(8,128)(2,1)S(1)...) custom-call(s32[5]{0:T(128)S(1)} %copy-done.23, bf16[640,768]{1,0:T(8,128)(2,1)S(1)} %copy-done.2, ...), custom_call_target="tpu_custom_call" | custom-call | flops 1000 | bytes 1000 | tf_op jit(solution)/shard_map/ff_first/pallas_call | solution.py:509
  41.9 8.2 %ff_back.1 = (f32[640,768]{1,0:T(8,128)S(1)}, bf16[640,768]{1,0:T(8,128)(2,1)S(1)}, bf16[640,384]{1,0:T(8,128)(2,1)S(1)}, bf16[640,384]{1,0:T(8,128)(2,1)S(1)}, f32[4,768]{1,0:T(4,128)S(1)}) custom-call(s32[5]{0:T(128)S(1)} %copy-done.23, bf16[640,3072]{1,0:T(8,128)(2,1)S(1)} %get-tuple-element.62.grad_pre.grad, bf16[768,3072]{1,0:T(8,128)(2,1)S(1)} %bitcast.121, ...), custom_call_target="tpu_custom_call" | custom-call | flops 1000 | bytes 1000 | tf_op jit(solution)/shard_map/ff_back/pallas_call | solution.py:593
  50.7 1.3 collective-permute-done.8.normed_far
  52.0 7.2 %up_weight.1 = (bf16[2,4,240,384]{3,2,1,0:T(8,128)(2,1)S(1)}, bf16[2,4,240,384]{3,2,1,0:T(8,128)(2,1)S(1)}) custom-call(s32[5]{0:T(128)S(1)} %copy-done.23, bf16[640,3072]{1,0:T(8,128)(2,1)S(1)} %get-tuple-element.62.grad_pre.grad, bf16[640,3072]{1,0:T(8,128)(2,1)S(1)} %collective-permute-done.7.grad_far, bf16[640,768]{1,0:T(8,128)(2,1)S(1)} %get-tuple-element.66.normed, ...), custom_call_target="tpu_custom_call" | custom-call | flops 1000 | bytes 1000 | tf_op jit(solution)/shard_map/up_weight/pallas_call | solution.py:688
  59.3 2.0 %out_weight.1 = (bf16[2,4,240,384]{3,2,1,0:T(8,128)(2,1)S(1)}, bf16[2,4,240,384]{3,2,1,0:T(8,128)(2,1)S(1)}) custom-call(s32[5]{0:T(128)S(1)} %copy-done.23, bf16[640,768]{1,0:T(8,128)(2,1)S(1)} %get-tuple-element.65.branch, bf16[640,768]{1,0:T(8,128)(2,1)S(1)} %collective-permute-done.6.branch_far, ...), custom_call_target="tpu_custom_call", output_to_operand_aliasing={{0}: (5, {}), {1}: (6, {})} | custom-call | flops 1000 | bytes 1000 | tf_op jit(solution)/shard_map/out_weight/pallas_call | solution.py:716
  61.3 2.9 %collective-permute-start.12 = (bf16[2,4,240,384]{3,2,1,0:T(8,128)(2,1)S(1)}, bf16[2,4,240,384]{3,2,1,0:T(8,128)(2,1)S(1)}, u32[]{:S(2)}, u32[]{:S(2)}) collective-permute-start(bf16[2,4,240,384]{3,2,1,0:T(8,128)(2,1)S(1)} %get-tuple-element.69.refs_5_.refs_10_), channel_id=1, source_target_pairs={{0,4},{4,0},{8,12},{12,8},{16,20},{20,16},{24,28},{28,24},{1,5},{5... | collective-permute-start | bytes 4423688 | tf_op jit(solution)/shard_map/ppermute | solution.py:937
  64.2 5.4 %down_weight.1 = (bf16[2,4,192,384]{3,2,1,0:T(8,128)(2,1)S(1)}, bf16[2,4,192,384]{3,2,1,0:T(8,128)(2,1)S(1)}) custom-call(s32[5]{0:T(128)S(1)} %copy-done.23, bf16[640,1536]{1,0:T(8,128)(2,1)S(1)} %get-tuple-element.59.refs_1_.refs_2_, bf16[640,1536]{1,0:T(8,128)(2,1)S(1)} %collective-permute-done.5.refs_2_, bf16[640,768]{1,0:T(8,128)(2,1)S(1)} %copy-done.4, ...), custom_call_target="tpu_custom_call" | custom-call | flops 1000 | bytes 1000 | tf_op jit(solution)/shard_map/down_weight/pallas_call | solution.py:650
  69.6 0.7 collective-permute-start.10
  70.4 18.3 %attend_back.1 = (bf16[3,384,640]{2,1,0:T(8,128)(2,1)}, bf16[3,384,640]{2,1,0:T(8,128)(2,1)}) custom-call(s32[5]{0:T(128)S(1)} %copy-done.23, s32[2,1280]{1,0:T(2,128)S(1)} %copy-done.24, f32[5,3,1,512]{3,2,1,0:T(1,128)S(1)} %get-tuple-element.61.refs_2_, bf16[3,640,384]{2,1,0:T(8,128)(2,1)S(1)} %qkv_keep.1.refs_2_.refs_3_, ...), custom_call_target="tpu_custom_call" | custom-call | flops 1000 | bytes 1000 | tf_op jit(solution)/shard_map/attend_back/pallas_call | solution.py:419
  89.3 8.2 %collective-permute-done.10 = bf16[2,4,192,384]{3,2,1,0:T(8,128)(2,1)S(1)} collective-permute-done((bf16[2,4,192,384]{3,2,1,0:T(8,128)(2,1)S(1)}, bf16[2,4,192,384]{3,2,1,0:T(8,128)(2,1)S(1)}, u32[]{:S(2)}, u32[]{:S(2)}) %collective-permute-start.10) | collective-permute-done | bytes 1179680 | tf_op jit(solution)/shard_map/ppermute | solution.py:932
  97.5 1.1 fusion.2.refs_7_
  98.9 1.2 fusion.refs_8_
  100.3 1.7 collective-permute-start.13
  102.0 1.2 copy-done.14
  103.2 1.0 copy-done.20
  104.2 6.9 %qkv_weight.1 = (bf16[2,4,72,384]{3,2,1,0:T(8,128)(2,1)S(1)}, bf16[2,4,72,384]{3,2,1,0:T(8,128)(2,1)S(1)}, bf16[2,4,72,384]{3,2,1,0:T(8,128)(2,1)S(1)}, bf16[2,4,72,384]{3,2,1,0:T(8,128)(2,1)S(1)}, f32[3,768]{1,0:T(4,128)S(1)}) custom-call(s32[5]{0:T(128)S(1)} %copy-done.23, bf16[3,384,640]{2,1,0:T(8,128)(2,1)} %get-tuple-element.71.refs_1_, ...), custom_call_target="tpu_custom_call" | custom-call | flops 1000 | bytes 1000 | tf_op jit(solution)/shard_map/qkv_weight/pallas_call | solution.py:843
  111.6 1.7 collective-permute-start.18
  113.6 1.4 fusion.3
  115.0 4.9 %collective-permute-done.13 = bf16[4,240,384]{2,1,0:T(8,128)(2,1)} collective-permute-done((bf16[4,240,384]{2,1,0:T(8,128)(2,1)}, bf16[4,240,384]{2,1,0:T(8,128)(2,1)}, u32[]{:S(2)}, u32[]{:S(2)}) %collective-permute-start.13) | collective-permute-done | bytes 737312 | tf_op jit(solution)/shard_map/ppermute | solution.py:932
  120.0 1.3 fusion.1
  121.4 3.3 %collective-permute-start.15 = (bf16[2,432,384]{2,1,0:T(8,128)(2,1)S(1)}, bf16[2,432,384]{2,1,0:T(8,128)(2,1)S(1)}, u32[]{:S(2)}, u32[]{:S(2)}) collective-permute-start(bf16[2,432,384]{2,1,0:T(8,128)(2,1)S(1)} %pad_maximum_fusion.refs_9_), channel_id=1, source_target_pairs={{0,8},{4,12},{8,0},{12,4},{16,24},{20,28},{24,16},{28,20},{1,9},{5... | collective-permute-start | bytes 1990664 | tf_op jit(solution)/shard_map/ppermute | solution.py:937
  124.7 9.5 %input_back.1 = (f32[640,768]{1,0:T(8,128)}, f32[7,768]{1,0:T(8,128)S(1)}, bf16[2,4,72,384]{3,2,1,0:T(8,128)(2,1)S(1)}, bf16[2,4,72,384]{3,2,1,0:T(8,128)(2,1)S(1)}) custom-call(s32[5]{0:T(128)S(1)} %copy-done.23, bf16[3,384,640]{2,1,0:T(8,128)(2,1)} %get-tuple-element.71.refs_1_, ...), custom_call_target="tpu_custom_call", output_to_operand_aliasing={{2}: (10, {}), {3}: (11, {})} | custom-call | flops 1000 | bytes 1000 | tf_op jit(solution)/shard_map/input_back/pallas_call | solution.py:911
  134.4 1.7 collective-permute-start.19
  136.6 3.8 %collective-permute-done.19 = bf16[4,72,384]{2,1,0:T(8,128)(2,1)S(1)} collective-permute-done((bf16[4,72,384]{2,1,0:T(8,128)(2,1)S(1)}, bf16[4,72,384]{2,1,0:T(8,128)(2,1)S(1)}, u32[]{:S(2)}, u32[]{:S(2)}) %collective-permute-start.19) | collective-permute-done | bytes 221216 | tf_op jit(solution)/shard_map/ppermute | solution.py:932
  140.4 1.8 collective-permute-done.17
  142.9 1.4 fusion.7
  144.3 1.1 fusion.11
  145.5 1.5 collective-permute-start.23
  147.1 6.2 %mixed.1 = (bf16[640,768]{1,0:T(8,128)(2,1)}, f32[32,18,24]{2,1,0:T(8,128)S(1)}, bf16[2,4,72,384]{3,2,1,0:T(8,128)(2,1)S(1)}, bf16[2,4,72,384]{3,2,1,0:T(8,128)(2,1)S(1)}) custom-call(s32[5]{0:T(128)S(1)} %copy-done.23, bf16[640,1536]{1,0:T(8,128)(2,1)S(1)} %copy-done.16, ...), custom_call_target="tpu_custom_call", output_to_operand_aliasing={{2}: (12, {}), {3}: (13, {})} | custom-call | flops 1000 | bytes 1000 | tf_op jit(solution)/shard_map/mixed/pallas_call | solution.py:777
  153.3 0.8 copy-done.11
  154.1 0.8 copy-done.12
  154.8 1.0 reshape.387
  155.8 3.7 %all-to-all-start = ((f32[32,1,432]{2,1,0:T(1,128)}), f32[32,1,432]{2,1,0:T(1,128)S(1)}, u32[]{:S(2)}, u32[]{:S(2)}) async-start(f32[32,1,432]{2,1,0:T(1,128)} %reshape.387), calls=%async_computation | async-start | bytes 131072 | tf_op jit(solution)/shard_map/all_to_all | solution.py:1129
  159.6 1.0 fusion.21
  160.5 2.7 %collective-permute-start.21 = (bf16[1,144,384]{2,1,0:T(8,128)(2,1)S(1)}, bf16[1,144,384]{2,1,0:T(8,128)(2,1)S(1)}, u32[]{:S(2)}, u32[]{:S(2)}) collective-permute-start(bf16[1,144,384]{2,1,0:T(8,128)(2,1)S(1)} %pad_maximum_fusion.4), channel_id=1, source_target_pairs={{0,16},{4,20},{8,24},{12,28},{16,0},{20,4},{24,8},{28,12},{1,17},{... | collective-permute-start | bytes 331784 | tf_op jit(solution)/shard_map/ppermute | solution.py:937
  163.3 3.7 %all-to-all-done = f32[32,1,432]{2,1,0:T(1,128)S(1)} async-done(((f32[32,1,432]{2,1,0:T(1,128)}), f32[32,1,432]{2,1,0:T(1,128)S(1)}, u32[]{:S(2)}, u32[]{:S(2)}) %all-to-all-start) | async-done | bytes 55328 | tf_op jit(solution)/shard_map/all_to_all | solution.py:1129
  167.5 0.8 reduce
  170.8 1.0 select_bitcast_fusion.1
  172.0 1.2 fusion.5
  173.2 1.2 fusion.9
  176.3 0.7 copy.39
  177.0 0.7 maximum_bitcast_fusion
  (157 shorter events, 13.6 us)
Async XLA Ops:
  1.3 12.9 %copy-start.24 = (s32[2,1280]{1,0:T(2,128)S(1)}, s32[2,1280]{1,0:T(2,128)}, u32[]{:S(2)}) copy-start(s32[2,1280]{1,0:T(2,128)} %refs_1_.3) | copy-start | bytes 30724
  8.4 5.7 %collective-permute-start = (bf16[3,640,384]{2,1,0:T(8,128)(2,1)}, bf16[3,640,384]{2,1,0:T(8,128)(2,1)S(1)}, u32[]{:S(2)}, u32[]{:S(2)}) collective-permute-start(bf16[3,640,384]{2,1,0:T(8,128)(2,1)} %get-tuple-element.54), channel_id=1, source_target_pairs={{0,1},{1,0},{2,3},{3,2},{4,5},{5,4},{6,7},{7,6},{8,9},{9,8},{10,11... | collective-permute-start | bytes 4423688 | tf_op jit(solution)/shard_map/ppermute | solution.py:932
  8.9 5.2 %collective-permute-start.1 = (bf16[640,768]{1,0:T(8,128)(2,1)S(1)}, bf16[640,768]{1,0:T(8,128)(2,1)S(1)}, u32[]{:S(2)}, u32[]{:S(2)}) collective-permute-start(bf16[640,768]{1,0:T(8,128)(2,1)S(1)} %copy-done.4), channel_id=1, source_target_pairs={{0,1},{1,0},{2,3},{3,2},{4,5},{5,4},{6,7},{7,6},{8,9},{9,8},{10,11... | collective-permute-start | bytes 2949128 | tf_op jit(solution)/shard_map/ppermute | solution.py:932
  9.0 5.1 %collective-permute-start.2 = (bf16[640,384]{1,0:T(8,128)(2,1)}, bf16[640,384]{1,0:T(8,128)(2,1)S(1)}, u32[]{:S(2)}, u32[]{:S(2)}) collective-permute-start(bf16[640,384]{1,0:T(8,128)(2,1)} %get-tuple-element.55), channel_id=1, source_target_pairs={{0,1},{1,0},{2,3},{3,2},{4,5},{5,4},{6,7},{7,6},{8,9},{9,8},{10,11... | collective-permute-start | bytes 1474568 | tf_op jit(solution)/shard_map/ppermute | solution.py:932
  9.4 17.6 %slice-start = ((s8[4718592]{0:T(1024)(128)(4,1)}), s8[4194304]{0:T(1024)(128)(4,1)S(1)}, s32[]{:S(2)}) async-start(s8[4718592]{0:T(1024)(128)(4,1)} %bitcast.120), calls=%async_computation.1 | async-start | bytes 8388608
  10.8 14.7 %copy-start.43 = (bf16[3072]{0:T(1024)(128)(2,1)S(1)}, bf16[3072]{0:T(1024)(128)(2,1)}, u32[]{:S(2)}) copy-start(bf16[3072]{0:T(1024)(128)(2,1)} %param.30) | copy-start | bytes 18436
  10.8 16.2 %slice-start.1 = ((s8[4718592]{0:T(1024)(128)(4,1)}), s8[524288]{0:T(1024)(128)(4,1)S(1)}, s32[]{:S(2)}) async-start(s8[4718592]{0:T(1024)(128)(4,1)} %bitcast.120), calls=%async_computation.2 | async-start | bytes 1048576
  10.8 16.2 %copy-start.1 = (bf16[3072,768]{1,0:T(8,128)(2,1)S(1)}, bf16[3072,768]{1,0:T(8,128)(2,1)}, u32[]{:S(2)}) copy-start(bf16[3072,768]{1,0:T(8,128)(2,1)} %refs_3_.5) | copy-start | bytes 14155780
  13.6 13.4 %copy-start.2 = (bf16[640,768]{1,0:T(8,128)(2,1)S(1)}, bf16[640,768]{1,0:T(8,128)(2,1)}, u32[]{:S(2)}) copy-start(bf16[640,768]{1,0:T(8,128)(2,1)} %refs_4_.1) | copy-start | bytes 2949124
  13.6 13.4 %copy-start.22 = (bf16[5,768]{1,0:T(8,128)(2,1)S(1)}, bf16[5,768]{1,0:T(8,128)(2,1)}, u32[]{:S(2)}) copy-start(bf16[5,768]{1,0:T(8,128)(2,1)} %refs_6_.1) | copy-start | bytes 23044
  13.7 13.4 %copy-start.25 = (s32[640]{0:T(1024)S(1)}, s32[640]{0:T(1024)}, u32[]{:S(2)}) copy-start(s32[640]{0:T(1024)} %refs_5_.2) | copy-start | bytes 7684
  13.7 13.4 %copy-start.32 = (bf16[768]{0:T(1024)(128)(2,1)S(1)}, bf16[768]{0:T(1024)(128)(2,1)}, u32[]{:S(2)}) copy-start(bf16[768]{0:T(1024)(128)(2,1)} %gain.5) | copy-start | bytes 4612
  13.7 13.4 %copy-start.34 = (bf16[768]{0:T(1024)(128)(2,1)S(1)}, bf16[768]{0:T(1024)(128)(2,1)}, u32[]{:S(2)}) copy-start(bf16[768]{0:T(1024)(128)(2,1)} %bias.5) | copy-start | bytes 4612
  13.7 13.4 %copy-start.35 = (bf16[768]{0:T(1024)(128)(2,1)S(1)}, bf16[768]{0:T(1024)(128)(2,1)}, u32[]{:S(2)}) copy-start(bf16[768]{0:T(1024)(128)(2,1)} %shift.3) | copy-start | bytes 4612
  14.1 10.9 %copy-start.19 = (bf16[640,384]{1,0:T(8,128)(2,1)}, bf16[640,384]{1,0:T(8,128)(2,1)S(1)}, u32[]{:S(2)}) copy-start(bf16[640,384]{1,0:T(8,128)(2,1)S(1)} %collective-permute-done.2.refs_5_.refs_6_) | copy-start | bytes 1474564
  25.1 1.9 %collective-permute-start.3 = (bf16[640,384]{1,0:T(8,128)(2,1)S(1)}, bf16[640,384]{1,0:T(8,128)(2,1)S(1)}, u32[]{:S(2)}, u32[]{:S(2)}) collective-permute-start(bf16[640,384]{1,0:T(8,128)(2,1)S(1)} %get-tuple-element.57.far.refs_6_), channel_id=1, source_target_pairs={{0,1},{1,0},{2,3},{3,2},{4,5},{5,4},{6,7},{7,6},{8,9},{9,8},{10,11... | collective-permute-start | bytes 1474568 | tf_op jit(solution)/shard_map/ppermute | solution.py:932
  41.0 23.2 %copy-start.7 = (bf16[640,1536]{1,0:T(8,128)(2,1)}, bf16[640,1536]{1,0:T(8,128)(2,1)S(1)}, u32[]{:S(2)}) copy-start(bf16[640,1536]{1,0:T(8,128)(2,1)S(1)} %get-tuple-element.59.refs_1_.refs_2_) | copy-start | bytes 5898244
  41.0 11.0 %collective-permute-start.7 = (bf16[640,3072]{1,0:T(8,128)(2,1)S(1)}, bf16[640,3072]{1,0:T(8,128)(2,1)S(1)}, u32[]{:S(2)}, u32[]{:S(2)}) collective-permute-start(bf16[640,3072]{1,0:T(8,128)(2,1)S(1)} %get-tuple-element.62.grad_pre.grad), channel_id=1, source_target_pairs={{0,1},{1,0},{2,3},{3,2},{4,5},{5,4},{6,7},{7,6},{8,9},{9,8},{10,11... | collective-permute-start | bytes 11796488 | tf_op jit(solution)/shard_map/ppermute | solution.py:932
  41.3 22.9 %collective-permute-start.5 = (bf16[640,1536]{1,0:T(8,128)(2,1)S(1)}, bf16[640,1536]{1,0:T(8,128)(2,1)S(1)}, u32[]{:S(2)}, u32[]{:S(2)}) collective-permute-start(bf16[640,1536]{1,0:T(8,128)(2,1)S(1)} %get-tuple-element.58.refs_1_), channel_id=1, source_target_pairs={{0,1},{1,0},{2,3},{3,2},{4,5},{5,4},{6,7},{7,6},{8,9},{9,8},{10,11... | collective-permute-start | bytes 5898248 | tf_op jit(solution)/shard_map/ppermute | solution.py:932
  41.5 10.5 %collective-permute-start.8 = (bf16[640,768]{1,0:T(8,128)(2,1)S(1)}, bf16[640,768]{1,0:T(8,128)(2,1)S(1)}, u32[]{:S(2)}, u32[]{:S(2)}) collective-permute-start(bf16[640,768]{1,0:T(8,128)(2,1)S(1)} %get-tuple-element.66.normed), channel_id=1, source_target_pairs={{0,1},{1,0},{2,3},{3,2},{4,5},{5,4},{6,7},{7,6},{8,9},{9,8},{10,11... | collective-permute-start | bytes 2949128 | tf_op jit(solution)/shard_map/ppermute | solution.py:932
  50.1 9.1 %collective-permute-start.6 = (bf16[640,768]{1,0:T(8,128)(2,1)S(1)}, bf16[640,768]{1,0:T(8,128)(2,1)S(1)}, u32[]{:S(2)}, u32[]{:S(2)}) collective-permute-start(bf16[640,768]{1,0:T(8,128)(2,1)S(1)} %get-tuple-element.65.branch), channel_id=1, source_target_pairs={{0,1},{1,0},{2,3},{3,2},{4,5},{5,4},{6,7},{7,6},{8,9},{9,8},{10,11... | collective-permute-start | bytes 2949128 | tf_op jit(solution)/shard_map/ppermute | solution.py:932
  50.3 8.9 %collective-permute-start.4 = (bf16[640,384]{1,0:T(8,128)(2,1)S(1)}, bf16[640,384]{1,0:T(8,128)(2,1)S(1)}, u32[]{:S(2)}, u32[]{:S(2)}) collective-permute-start(bf16[640,384]{1,0:T(8,128)(2,1)S(1)} %get-tuple-element.64), channel_id=1, source_target_pairs={{0,1},{1,0},{2,3},{3,2},{4,5},{5,4},{6,7},{7,6},{8,9},{9,8},{10,11... | collective-permute-start | bytes 1474568 | tf_op jit(solution)/shard_map/ppermute | solution.py:932
  61.2 37.7 %copy-start.9 = (bf16[2,4,240,384]{3,2,1,0:T(8,128)(2,1)}, bf16[2,4,240,384]{3,2,1,0:T(8,128)(2,1)S(1)}, u32[]{:S(2)}) copy-start(bf16[2,4,240,384]{3,2,1,0:T(8,128)(2,1)S(1)} %get-tuple-element.75) | copy-start | bytes 4423684
  61.3 37.7 %collective-permute-start.12 = (bf16[2,4,240,384]{3,2,1,0:T(8,128)(2,1)S(1)}, bf16[2,4,240,384]{3,2,1,0:T(8,128)(2,1)S(1)}, u32[]{:S(2)}, u32[]{:S(2)}) collective-permute-start(bf16[2,4,240,384]{3,2,1,0:T(8,128)(2,1)S(1)} %get-tuple-element.69.refs_5_.refs_10_), channel_id=1, source_target_pairs={{0,4},{4,0},{8,12},{12,8},{16,20},{20,16},{24,28},{28,24},{1,5},{5... | collective-permute-start | bytes 4423688 | tf_op jit(solution)/shard_map/ppermute | solution.py:937
  69.6 27.8 %copy-start.21 = (bf16[2,4,192,384]{3,2,1,0:T(8,128)(2,1)}, bf16[2,4,192,384]{3,2,1,0:T(8,128)(2,1)S(1)}, u32[]{:S(2)}) copy-start(bf16[2,4,192,384]{3,2,1,0:T(8,128)(2,1)S(1)} %get-tuple-element.74) | copy-start | bytes 3538948
  69.6 27.8 %collective-permute-start.10 = (bf16[2,4,192,384]{3,2,1,0:T(8,128)(2,1)S(1)}, bf16[2,4,192,384]{3,2,1,0:T(8,128)(2,1)S(1)}, u32[]{:S(2)}, u32[]{:S(2)}) collective-permute-start(bf16[2,4,192,384]{3,2,1,0:T(8,128)(2,1)S(1)} %get-tuple-element.70.refs_9_), channel_id=1, source_target_pairs={{0,2},{1,3},{2,0},{3,1},{4,6},{5,7},{6,4},{7,5},{8,10},{9,11},{10,... | collective-permute-start | bytes 3538952 | tf_op jit(solution)/shard_map/ppermute | solution.py:932
  88.7 13.3 %collective-permute-start.9 = (bf16[3,384,640]{2,1,0:T(8,128)(2,1)}, bf16[3,384,640]{2,1,0:T(8,128)(2,1)}, u32[]{:S(2)}, u32[]{:S(2)}) collective-permute-start(bf16[3,384,640]{2,1,0:T(8,128)(2,1)} %get-tuple-element.72.refs_2_), channel_id=1, source_target_pairs={{0,1},{1,0},{2,3},{3,2},{4,5},{5,4},{6,7},{7,6},{8,9},{9,8},{10,11... | collective-permute-start | bytes 4423688 | tf_op jit(solution)/shard_map/ppermute | solution.py:932
  88.8 13.2 %collective-permute-start.14 = (bf16[3,384,640]{2,1,0:T(8,128)(2,1)}, bf16[3,384,640]{2,1,0:T(8,128)(2,1)}, u32[]{:S(2)}, u32[]{:S(2)}) collective-permute-start(bf16[3,384,640]{2,1,0:T(8,128)(2,1)} %get-tuple-element.71.refs_1_), channel_id=1, source_target_pairs={{0,1},{1,0},{2,3},{3,2},{4,5},{5,4},{6,7},{7,6},{8,9},{9,8},{10,11... | collective-permute-start | bytes 4423688 | tf_op jit(solution)/shard_map/ppermute | solution.py:932
  98.6 15.0 %collective-permute-start.11 = (bf16[4,192,384]{2,1,0:T(8,128)(2,1)}, bf16[4,192,384]{2,1,0:T(8,128)(2,1)}, u32[]{:S(2)}, u32[]{:S(2)}) collective-permute-start(bf16[4,192,384]{2,1,0:T(8,128)(2,1)} %fusion.2.refs_7_), channel_id=1, source_target_pairs={{0,4},{4,0},{8,12},{12,8},{16,20},{20,16},{24,28},{28,24},{1,5},{5... | collective-permute-start | bytes 1769480 | tf_op jit(solution)/shard_map/ppermute | solution.py:937
  100.3 19.7 %collective-permute-start.13 = (bf16[4,240,384]{2,1,0:T(8,128)(2,1)}, bf16[4,240,384]{2,1,0:T(8,128)(2,1)}, u32[]{:S(2)}, u32[]{:S(2)}) collective-permute-start(bf16[4,240,384]{2,1,0:T(8,128)(2,1)} %fusion.refs_8_), channel_id=1, source_target_pairs={{0,2},{1,3},{2,0},{3,1},{4,6},{5,7},{6,4},{7,5},{8,10},{9,11},{10,... | collective-permute-start | bytes 2211848 | tf_op jit(solution)/shard_map/ppermute | solution.py:932
  111.2 25.0 %collective-permute-start.16 = (bf16[2,4,72,384]{3,2,1,0:T(8,128)(2,1)S(1)}, bf16[2,4,72,384]{3,2,1,0:T(8,128)(2,1)S(1)}, u32[]{:S(2)}, u32[]{:S(2)}) collective-permute-start(bf16[2,4,72,384]{3,2,1,0:T(8,128)(2,1)S(1)} %get-tuple-element.83), channel_id=1, source_target_pairs={{0,2},{1,3},{2,0},{3,1},{4,6},{5,7},{6,4},{7,5},{8,10},{9,11},{10,... | collective-permute-start | bytes 1327112 | tf_op jit(solution)/shard_map/ppermute | solution.py:932
  111.6 22.7 %collective-permute-start.18 = (bf16[2,4,72,384]{3,2,1,0:T(8,128)(2,1)S(1)}, bf16[2,4,72,384]{3,2,1,0:T(8,128)(2,1)S(1)}, u32[]{:S(2)}, u32[]{:S(2)}) collective-permute-start(bf16[2,4,72,384]{3,2,1,0:T(8,128)(2,1)S(1)} %get-tuple-element.85), channel_id=1, source_target_pairs={{0,4},{4,0},{8,12},{12,8},{16,20},{20,16},{24,28},{28,24},{1,5},{5... | collective-permute-start | bytes 1327112 | tf_op jit(solution)/shard_map/ppermute | solution.py:937
  113.6 11.1 %copy-start.18 = (f32[640,768]{1,0:T(8,128)S(1)}, f32[640,768]{1,0:T(8,128)}, u32[]{:S(2)}) copy-start(f32[640,768]{1,0:T(8,128)} %copy-done.17) | copy-start | bytes 5898244
  121.3 25.7 %slice-start.2 = ((s8[4718592]{0:T(1024)(128)(4,1)}), s8[4194304]{0:T(1024)(128)(4,1)S(1)}, s32[]{:S(2)}) async-start(s8[4718592]{0:T(1024)(128)(4,1)} %bitcast.122), calls=%async_computation.3 | async-start | bytes 8388608
  121.4 21.5 %collective-permute-start.15 = (bf16[2,432,384]{2,1,0:T(8,128)(2,1)S(1)}, bf16[2,432,384]{2,1,0:T(8,128)(2,1)S(1)}, u32[]{:S(2)}, u32[]{:S(2)}) collective-permute-start(bf16[2,432,384]{2,1,0:T(8,128)(2,1)S(1)} %pad_maximum_fusion.refs_9_), channel_id=1, source_target_pairs={{0,8},{4,12},{8,0},{12,4},{16,24},{20,28},{24,16},{28,20},{1,9},{5... | collective-permute-start | bytes 1990664 | tf_op jit(solution)/shard_map/ppermute | solution.py:937
  124.7 22.3 %slice-start.3 = ((s8[4718592]{0:T(1024)(128)(4,1)}), s8[524288]{0:T(1024)(128)(4,1)S(1)}, s32[]{:S(2)}) async-start(s8[4718592]{0:T(1024)(128)(4,1)} %bitcast.122), calls=%async_computation.4 | async-start | bytes 1048576
  124.7 22.3 %copy-start.16 = (bf16[640,1536]{1,0:T(8,128)(2,1)S(1)}, bf16[640,1536]{1,0:T(8,128)(2,1)}, u32[]{:S(2)}) copy-start(bf16[640,1536]{1,0:T(8,128)(2,1)} %copy-done.15) | copy-start | bytes 5898244
  134.4 6.0 %collective-permute-start.19 = (bf16[4,72,384]{2,1,0:T(8,128)(2,1)S(1)}, bf16[4,72,384]{2,1,0:T(8,128)(2,1)S(1)}, u32[]{:S(2)}, u32[]{:S(2)}) collective-permute-start(bf16[4,72,384]{2,1,0:T(8,128)(2,1)S(1)} %fusion.13), channel_id=1, source_target_pairs={{0,2},{1,3},{2,0},{3,1},{4,6},{5,7},{6,4},{7,5},{8,10},{9,11},{10,... | collective-permute-start | bytes 663560 | tf_op jit(solution)/shard_map/ppermute | solution.py:932
  136.1 10.9 %copy-start.8 = (bf16[640,1536]{1,0:T(8,128)(2,1)S(1)}, bf16[640,1536]{1,0:T(8,128)(2,1)}, u32[]{:S(2)}) copy-start(bf16[640,1536]{1,0:T(8,128)(2,1)} %copy-done.7) | copy-start | bytes 5898244
  136.2 6.0 %collective-permute-start.17 = (bf16[4,72,384]{2,1,0:T(8,128)(2,1)S(1)}, bf16[4,72,384]{2,1,0:T(8,128)(2,1)S(1)}, u32[]{:S(2)}, u32[]{:S(2)}) collective-permute-start(bf16[4,72,384]{2,1,0:T(8,128)(2,1)S(1)} %fusion.12), channel_id=1, source_target_pairs={{0,4},{4,0},{8,12},{12,8},{16,20},{20,16},{24,28},{28,24},{1,5},{5... | collective-permute-start | bytes 663560 | tf_op jit(solution)/shard_map/ppermute | solution.py:937
  142.3 17.3 %collective-permute-start.20 = (bf16[2,144,384]{2,1,0:T(8,128)(2,1)S(1)}, bf16[2,144,384]{2,1,0:T(8,128)(2,1)S(1)}, u32[]{:S(2)}, u32[]{:S(2)}) collective-permute-start(bf16[2,144,384]{2,1,0:T(8,128)(2,1)S(1)} %pad_maximum_fusion.3.refs_11_), channel_id=1, source_target_pairs={{0,8},{4,12},{8,0},{12,4},{16,24},{20,28},{24,16},{28,20},{1,9},{5... | collective-permute-start | bytes 663560 | tf_op jit(solution)/shard_map/ppermute | solution.py:937
  142.9 10.4 %copy-start.39 = (bf16[2,432,384]{2,1,0:T(8,128)(2,1)}, bf16[2,432,384]{2,1,0:T(8,128)(2,1)S(1)}, u32[]{:S(2)}) copy-start(bf16[2,432,384]{2,1,0:T(8,128)(2,1)S(1)} %collective-permute-done.15) | copy-start | bytes 1990660
  145.5 26.4 %collective-permute-start.23 = (bf16[1,432,384]{2,1,0:T(8,128)(2,1)S(1)}, bf16[1,432,384]{2,1,0:T(8,128)(2,1)S(1)}, u32[]{:S(2)}, u32[]{:S(2)}) collective-permute-start(bf16[1,432,384]{2,1,0:T(8,128)(2,1)S(1)} %pad_maximum_fusion.1.refs_10_), channel_id=1, source_target_pairs={{0,16},{4,20},{8,24},{12,28},{16,0},{20,4},{24,8},{28,12},{1,17},{... | collective-permute-start | bytes 995336 | tf_op jit(solution)/shard_map/ppermute | solution.py:937
  155.8 16.1 %copy-start.40 = (bf16[2,432,384]{2,1,0:T(8,128)(2,1)S(1)}, bf16[2,432,384]{2,1,0:T(8,128)(2,1)}, u32[]{:S(2)}) copy-start(bf16[2,432,384]{2,1,0:T(8,128)(2,1)} %copy-done.39) | copy-start | bytes 1990660
  155.8 11.1 %all-to-all-start = ((f32[32,1,432]{2,1,0:T(1,128)}), f32[32,1,432]{2,1,0:T(1,128)S(1)}, u32[]{:S(2)}, u32[]{:S(2)}) async-start(f32[32,1,432]{2,1,0:T(1,128)} %reshape.387), calls=%async_computation | async-start | bytes 131072 | tf_op jit(solution)/shard_map/all_to_all | solution.py:1129
  160.5 10.2 %collective-permute-start.21 = (bf16[1,144,384]{2,1,0:T(8,128)(2,1)S(1)}, bf16[1,144,384]{2,1,0:T(8,128)(2,1)S(1)}, u32[]{:S(2)}, u32[]{:S(2)}) collective-permute-start(bf16[1,144,384]{2,1,0:T(8,128)(2,1)S(1)} %pad_maximum_fusion.4), channel_id=1, source_target_pairs={{0,16},{4,20},{8,24},{12,28},{16,0},{20,4},{24,8},{28,12},{1,17},{... | collective-permute-start | bytes 331784 | tf_op jit(solution)/shard_map/ppermute | solution.py:937
  171.8 3.1 %collective-permute-start.22 = (f32[72,384]{1,0:T(8,128)S(1)}, f32[72,384]{1,0:T(8,128)S(1)}, u32[]{:S(2)}, u32[]{:S(2)}) collective-permute-start(f32[72,384]{1,0:T(8,128)S(1)} %get-tuple-element.91), channel_id=1, source_target_pairs={{0,1},{1,0},{2,3},{3,2},{4,5},{5,4},{6,7},{7,6},{8,9},{9,8},{10,11... | collective-permute-start | bytes 331784 | tf_op jit(solution)/shard_map/ppermute | solution.py:932
  174.5 1.7 collective-permute-start.24
  (26 other events, 147.5 us)
